TPU v7x, 512 devices: a whole 4x8x8 slice. The times are simulated.
512 devices in a mesh: dp: 64 (over z, y_hi, core), cls: 8 (over x, y_lo).
Axes of the slice: x: 4, y: 8 (y_hi: 4, y_lo: 2; y = y_hi * 2 + y_lo), z: 8, core: 2. Of those that a mesh axis runs over, the one named last changes fastest.
Arguments:
- features: bfloat16 [32768, 12544], P('dp', 'cls'), may hold values from -6 to 6
- fc_weight: bfloat16 [12544, 512], P('cls'), may hold values from -0.0546875 to 0.0546875
- class_weight: bfloat16 [4096, 512], P('cls'), may hold values from -0.29882812 to 0.29882812
- labels: int32 [32768], P('dp'), may hold values from 0 to 4095
Outputs:
- fc_grad: bfloat16 [12544, 512], P('cls')
- class_grad: bfloat16 [4096, 512], P('cls')
All inputs are finite; a program needn't handle non-finite values.
Results may differ from a plain program's by a relative error of at most 0.024.
Values may be sent and summed in bfloat16 or wider, within the bound.
No kernel may reach another device: no remote copies, remote signals or barrier semaphores. Data moves between devices by JAX's collectives and lax.ppermute only.
A program may use at most 64 MiB of HBM per device.

v0:
```python
import math

import jax
import jax.numpy as jnp
from jax import lax
from jax.sharding import PartitionSpec as P

SCALE = 64.0
MARGIN = 0.5
SOFTEN = 0.01
EPSILON = 1e-06


def margin_terms(cosine, is_target):
    sine = jnp.sqrt(1.0 + SOFTEN - cosine * cosine)
    shifted = cosine * math.cos(MARGIN) - sine * math.sin(MARGIN)
    powers = jnp.exp(SCALE * jnp.where(is_target, shifted, cosine))
    slopes = SCALE * jnp.where(is_target, math.cos(MARGIN) + math.sin(MARGIN) * cosine / sine, 1.0)
    return (powers, slopes)


def softmax_grad(powers, totals, slopes, is_target, loss_weight):
    onehot = is_target.astype(jnp.float32)
    return ((powers / totals[:, None] - onehot) * loss_weight * slopes).astype(jnp.bfloat16)


def shards(features, fc_weight, class_weight, labels):
    rows_group = features.shape[0]
    class_count = class_weight.shape[0]
    loss_weight = 1.0 / math.sqrt(rows_group * lax.axis_size("dp"))
    position = lax.axis_index("cls")
    rows_block = features
    raw_embed = lax.psum_scatter(
        jnp.dot(rows_block, fc_weight, preferred_element_type=jnp.float32).astype(jnp.bfloat16),
        "cls",
        scatter_dimension=0,
        tiled=True,
    ).astype(jnp.float32)
    embed_norm = jnp.sqrt(jnp.sum(raw_embed * raw_embed, axis=1, keepdims=True) + EPSILON)
    unit_f = raw_embed / embed_norm
    unit_embed = unit_f.astype(jnp.bfloat16)
    class_f = class_weight.astype(jnp.float32)
    class_norm = jnp.sqrt(jnp.sum(class_f * class_f, axis=1, keepdims=True) + EPSILON)
    class_unit_f = class_f / class_norm
    class_unit = class_unit_f.astype(jnp.bfloat16)
    faces_all = lax.all_gather(unit_embed, "cls", axis=0, tiled=True)
    cosine = lax.dot_general(
        faces_all, class_unit, (((1,), (1,)), ((), ())), preferred_element_type=jnp.float32
    )
    columns = position * class_count + lax.broadcasted_iota(jnp.int32, cosine.shape, 1)
    is_target = columns == labels[:, None]
    powers, slopes = margin_terms(cosine, is_target)
    totals = lax.psum(jnp.sum(powers, axis=1), "cls")
    cos_grad = softmax_grad(powers, totals, slopes, is_target, loss_weight)
    rows_block = cos_grad
    unit_grad = lax.psum_scatter(
        jnp.dot(rows_block, class_unit, preferred_element_type=jnp.float32).astype(jnp.bfloat16),
        "cls",
        scatter_dimension=0,
        tiled=True,
    ).astype(jnp.float32)
    class_part = lax.dot_general(
        cos_grad, faces_all, (((0,), (0,)), ((), ())), preferred_element_type=jnp.float32
    )
    raw_grad = (
        (unit_grad - unit_f * jnp.sum(unit_f * unit_grad, axis=1, keepdims=True)) / embed_norm
    ).astype(jnp.bfloat16)
    rows_block = features
    fc_part = lax.dot_general(
        rows_block,
        lax.all_gather(raw_grad, "cls", axis=0, tiled=True),
        (((0,), (0,)), ((), ())),
        preferred_element_type=jnp.float32,
    )
    fc_total, class_total = lax.psum((fc_part, class_part), "dp")
    fc_out = fc_total.astype(jnp.bfloat16)
    class_grad = (
        class_total - class_unit_f * jnp.sum(class_unit_f * class_total, axis=1, keepdims=True)
    ) / class_norm
    return (fc_out, class_grad.astype(jnp.bfloat16))


def solution(mesh):
    placed = (P("dp", "cls"), P("cls", None), P("cls", None), P("dp"))
    return jax.shard_map(
        shards,
        mesh=mesh,
        in_specs=placed,
        out_specs=(P("cls", None), P("cls", None)),
        check_vma=False,
    )
```

profile of v0, /device:TPU:1, one launch (start us, length us, event | category | flops | bytes accessed | tf_op | source)
XLA Modules:
  0.0 728.4 jit_solution(15242433414679928124)
XLA Ops:
  7.2 0.0 copy-start
  7.2 0.0 copy-start.1
  7.2 0.0 reduce-scatter.3.cloned.1.call-start
  7.2 1.4 copy-done
  8.6 3.3 convolution_convert_fusion.1
  11.9 0.0 reduce-scatter.3.cloned.1.call-update
  12.0 0.0 reduce-scatter.5.cloned.1.call-start
  12.0 0.0 copy-done.1
  12.0 0.2 fusion
  12.2 43.8 %reduce-scatter.3.cloned.1.call-done = bf16[64,512]{1,0:T(8,128)(2,1)} async-done(((bf16[512,512]{1,0:T(8,128)(2,1)}), bf16[64,512]{1,0:T(8,128)(2,1)}) %reduce-scatter.3.cloned.1.call-update) | async-done | bytes 65552 | tf_op jit(solution)/shard_map/reduce_scatter | solution.py:33
  56.1 1.0 fusion.12
  57.0 0.9 fusion.16
  58.0 23.5 %all_gather.6 = bf16[512,512]{1,0:T(8,128)(2,1)S(1)} all-gather(bf16[64,512]{1,0:T(8,128)(2,1)S(1)} %fusion.16), channel_id=1, replica_groups=mesh['dp'=64,'cls'=8] {'cls'}, dimensions={0}, use_global_device_ids=true | all-gather | bytes 589824 | tf_op jit(solution)/shard_map/all_gather | solution.py:46
  81.5 0.0 copy-done.4
  81.5 1.9 fusion.8
  83.3 14.6 %psum.21 = f32[512]{0:T(512)S(1)} all-reduce(f32[512]{0:T(512)S(1)} %get-tuple-element.2), channel_id=1, replica_groups=mesh['dp'=64,'cls'=8] {'cls'}, use_global_device_ids=true, to_apply=%region_4.5 | all-reduce | flops 512 | bytes 4096 | tf_op jit(solution)/shard_map/psum | solution.py:53
  97.9 2.2 fusion.6
  100.1 1.3 convolution_convert_fusion
  101.4 0.0 reduce-scatter.5.cloned.1.call-update
  101.5 0.0 copy-start.3
  101.5 0.0 all-reduce.3.cloned.1.call-start
  101.5 1.4 fusion.17
  102.9 0.0 all-reduce.3.cloned.1.call-update
  103.0 50.0 %reduce-scatter.5.cloned.1.call-done = bf16[64,512]{1,0:T(8,128)(2,1)} async-done(((bf16[512,512]{1,0:T(8,128)(2,1)}), bf16[64,512]{1,0:T(8,128)(2,1)}) %reduce-scatter.5.cloned.1.call-update) | async-done | bytes 65552 | tf_op jit(solution)/shard_map/reduce_scatter | solution.py:56
  152.9 1.0 fusion.13
  154.0 0.9 fusion.15
  154.9 24.7 %all_gather.7 = bf16[512,512]{1,0:T(8,128)(2,1)S(1)} all-gather(bf16[64,512]{1,0:T(8,128)(2,1)S(1)} %fusion.15), channel_id=1, replica_groups=mesh['dp'=64,'cls'=8] {'cls'}, dimensions={0}, use_global_device_ids=true | all-gather | bytes 589824 | tf_op jit(solution)/shard_map/all_gather | solution.py:71
  179.6 2.7 convolution_bitcast_fusion
  182.2 327.0 %all-reduce.4 = bf16[1568,512]{1,0:T(8,128)(2,1)} all-reduce(f32[1568,512]{1,0:T(8,128)} %convolution_bitcast_fusion), channel_id=1, replica_groups=mesh['dp'=64,'cls'=8] {'dp'}, use_global_device_ids=true, to_apply=%region_7.8 | all-reduce | flops 802816 | bytes 4816896 | tf_op jit(solution)/shard_map/psum | solution.py:75
  509.2 210.0 %all-reduce.3.cloned.1.call-done = f32[512,512]{1,0:T(8,128)} async-done(((f32[512,512]{1,0:T(8,128)}), f32[512,512]{1,0:T(8,128)}) %all-reduce.3.cloned.1.call-update) | async-done | bytes 1048592 | tf_op jit(solution)/shard_map/psum | solution.py:75
  719.2 1.6 multiply_reduce_fusion
  720.8 1.1 divide_convert_fusion
  (7 shorter events, 0.0 us)
Async XLA Ops:
  7.2 1.4 copy-start
  7.2 4.9 copy-start.1
  7.2 48.9 %reduce-scatter.3.cloned.1.call-start = ((), (), s32[]{:S(2)}) async-start(), calls=%async_computation.2 | async-start | bytes 589824 | tf_op jit(solution)/shard_map/reduce_scatter | solution.py:33
  11.9 69.5 %copy-start.4 = (s32[512]{0:T(512)S(1)}, s32[512]{0:T(512)}, u32[]{:S(2)}) copy-start(s32[512]{0:T(512)} %param.7) | copy-start | bytes 6148
  12.0 140.9 %reduce-scatter.5.cloned.1.call-start = ((), (), s32[]{:S(2)}) async-start(), calls=%async_computation.3 | async-start | bytes 589824 | tf_op jit(solution)/shard_map/reduce_scatter | solution.py:56
  101.5 51.5 %copy-start.3 = (bf16[64,512]{1,0:T(8,128)(2,1)S(1)}, bf16[64,512]{1,0:T(8,128)(2,1)}, u32[]{:S(2)}) copy-start(bf16[64,512]{1,0:T(8,128)(2,1)} %reduce-scatter.3.cloned.1.call-done) | copy-start | bytes 196612
  101.5 617.7 %all-reduce.3.cloned.1.call-start = ((), (), s32[]{:S(2)}) async-start(), calls=%async_computation.4 | async-start | bytes 2097152 | tf_op jit(solution)/shard_map/psum | solution.py:75
  719.2 1.6 copy-start.2
Sparse Core Ops, SparseCore 0:
  12.1 43.9 reduce-scatter.2
  101.6 51.2 reduce-scatter.4
  155.8 563.3 all-reduce.2
where the time goes:
time: 729 us; the launch traced here: 728 us
  blocking collectives  390 us (53%)
  waiting for transfers between devices  304 us (42%)
  between operations  13.8 us (2%)
  matrix products  10.6 us (1%)
  other arithmetic  8.94 us (1%)
    psum x1, blocking collectives, shards(): fc_total, class_total = lax.psum((fc_part, class_part), 'dp')  327 us
    psum x1, waiting for transfers between devices, shards(): fc_total, class_total = lax.psum((fc_part, class_part), 'dp')  210 us
    reduce_scatter x1, waiting for transfers between devices, shards(): lax.psum_scatter(jnp.dot(rows_block, class_unit, preferred_element_type=j...  50 us
    reduce_scatter x1, waiting for transfers between devices, shards(): lax.psum_scatter(jnp.dot(rows_block, fc_weight, preferred_element_type=jn...  43.8 us
    all_gather x1, blocking collectives, shards(): lax.all_gather(raw_grad, 'cls', axis=0, tiled=True)  24.7 us
    all_gather x1, blocking collectives, shards(): faces_all = lax.all_gather(unit_embed, 'cls', axis=0, tiled=True)  23.5 us
  transfers between devices with their start and end apart: 3, of which 3 were waited for; matrix products, arithmetic and copies ran while one was open for 1% of the time, Pallas kernels for 0%

commit v1 on v0

v1 whole, which is shorter than its diff:
```python
import math

import jax
import jax.numpy as jnp
from jax import lax
from jax.sharding import Mesh
from jax.sharding import PartitionSpec as P

SCALE = 64.0
MARGIN = 0.5
SOFTEN = 0.01
EPSILON = 1e-06

CLS = ("x", "yl")
CHIPS = ("z", "yh")
LANES = 128


def exchange(blocks, axes):
    return lax.all_to_all(blocks, axes, 0, 0, tiled=True)


def repeat_rows(block, count):
    return jnp.broadcast_to(block[None], (count,) + block.shape).reshape(
        (count * block.shape[0],) + block.shape[1:]
    )


def split_f32(value):
    high = lax.reduce_precision(value, 8, 7)
    rest = value - high
    mid = lax.reduce_precision(rest, 8, 7)
    low = rest - mid
    return [part.astype(jnp.bfloat16) for part in (high, mid, low)]


def packed(matrix, *columns):
    parts = [matrix]
    for column in columns:
        parts.extend(split_f32(column))
    parts.append(jnp.zeros((matrix.shape[0], LANES - 3 * len(columns)), jnp.bfloat16))
    return jnp.concatenate(parts, axis=1)


def unpacked(extra, which):
    low = 3 * which
    return jnp.sum(extra[:, low : low + 3].astype(jnp.float32), axis=1, keepdims=True)


def shards(features, fc_weight, class_weight, labels):
    faces = features.shape[0]
    classes, width = class_weight.shape
    n_cls = lax.axis_size(CLS)
    n_chips = lax.axis_size(CHIPS)
    loss_weight = 1.0 / math.sqrt(faces * n_chips * lax.axis_size("core"))
    position = lax.axis_index(CLS)

    class_f = class_weight.astype(jnp.float32)
    class_norm = jnp.sqrt(jnp.sum(class_f * class_f, axis=1, keepdims=True) + EPSILON)
    class_unit_f = class_f / class_norm
    class_unit = class_unit_f.astype(jnp.bfloat16)
    columns = position * classes + lax.broadcasted_iota(jnp.int32, (faces, classes), 1)
    is_target = columns == labels[:, None]

    raw_part = jnp.dot(features, fc_weight, preferred_element_type=jnp.float32)
    target_part = jnp.dot(
        is_target.astype(jnp.bfloat16), class_unit, preferred_element_type=jnp.float32
    )
    sent = jnp.concatenate([raw_part, target_part], axis=1).astype(jnp.bfloat16)
    got = exchange(sent, CLS).reshape(n_cls, faces // n_cls, 2 * width)
    got = jnp.sum(got.astype(jnp.float32), axis=0)
    raw_embed, target_unit = got[:, :width], got[:, width:]
    embed_norm = jnp.sqrt(jnp.sum(raw_embed * raw_embed, axis=1, keepdims=True) + EPSILON)
    unit_f = raw_embed / embed_norm
    unit = unit_f.astype(jnp.bfloat16)

    units = exchange(repeat_rows(unit, n_cls), CLS)
    cosine = lax.dot_general(
        units, class_unit, (((1,), (1,)), ((), ())), preferred_element_type=jnp.float32
    )
    others = jnp.where(is_target, 0.0, jnp.exp(SCALE * cosine))
    rest_part = jnp.sum(others, axis=1, keepdims=True)
    pull_part = jnp.dot(
        others.astype(jnp.bfloat16), class_unit, preferred_element_type=jnp.float32
    ).astype(jnp.bfloat16)
    got = exchange(packed(pull_part, rest_part), CLS).reshape(
        n_cls, faces // n_cls, width + LANES
    )
    got = jnp.sum(got.astype(jnp.float32), axis=0)
    pull, rest = got[:, :width], unpacked(got[:, width:], 0)

    cos_t = jnp.sum(
        unit.astype(jnp.float32) * target_unit, axis=1, keepdims=True
    )
    sine_t = jnp.sqrt(1.0 + SOFTEN - cos_t * cos_t)
    power_t = jnp.exp(SCALE * (cos_t * math.cos(MARGIN) - sine_t * math.sin(MARGIN)))
    slope_t = SCALE * (math.cos(MARGIN) + math.sin(MARGIN) * cos_t / sine_t)
    inverse = loss_weight / (rest + power_t)
    pull_scale = SCALE * inverse
    target_scale = rest * inverse * slope_t
    unit_grad = pull * pull_scale - target_unit * target_scale
    raw_grad = (
        (unit_grad - unit_f * jnp.sum(unit_f * unit_grad, axis=1, keepdims=True)) / embed_norm
    ).astype(jnp.bfloat16)

    got = exchange(repeat_rows(packed(raw_grad, pull_scale, target_scale), n_cls), CLS)
    raw_grads = got[:, :width]
    pull_scales, target_scales = unpacked(got[:, width:], 0), unpacked(got[:, width:], 1)
    cos_grad = jnp.where(is_target, -target_scales, others * pull_scales).astype(jnp.bfloat16)
    class_part = lax.dot_general(
        cos_grad, units, (((0,), (0,)), ((), ())), preferred_element_type=jnp.float32
    )
    class_part = (
        class_part - class_unit_f * jnp.sum(class_unit_f * class_part, axis=1, keepdims=True)
    ) / class_norm
    fc_part = lax.dot_general(
        features, raw_grads, (((0,), (0,)), ((), ())), preferred_element_type=jnp.float32
    )

    fc_rows = fc_part.shape[0]
    rows = fc_rows + classes
    groups = width // LANES
    piece = -(-rows * groups // (2 * n_chips * 8)) * 8
    half = piece * n_chips
    parts = jnp.concatenate([fc_part, class_part], axis=0)
    parts = parts.reshape(rows, groups, LANES).transpose(1, 0, 2).reshape(rows * groups, LANES)
    parts = jnp.pad(parts, ((0, 2 * half - rows * groups), (0, 0)))
    core = lax.axis_index("core")
    swap = [(0, 1), (1, 0)]
    mine = lax.dynamic_slice_in_dim(parts, core * half, half)
    theirs = lax.dynamic_slice_in_dim(parts, (1 - core) * half, half).astype(jnp.bfloat16)
    theirs = lax.ppermute(theirs, "core", swap)
    mine = (mine + theirs.astype(jnp.float32)).astype(jnp.bfloat16)
    got = exchange(mine, CHIPS).reshape(n_chips, piece, LANES)
    done = jnp.sum(got.astype(jnp.float32), axis=0).astype(jnp.bfloat16)
    mine = exchange(repeat_rows(done, n_chips), CHIPS)
    theirs = lax.ppermute(mine, "core", swap)
    first = jnp.where(core == 0, mine, theirs)
    second = jnp.where(core == 0, theirs, mine)
    whole = jnp.concatenate([first, second], axis=0)[: rows * groups]
    whole = whole.reshape(groups, rows, LANES).transpose(1, 0, 2).reshape(rows, width)
    return whole[:fc_rows], whole[fc_rows:]


def solution(mesh):
    fine = Mesh(mesh.devices.reshape(8, 4, 2, 4, 2), ("z", "yh", "core", "x", "yl"))
    dp = ("z", "yh", "core")
    placed = (P(dp, CLS), P(CLS, None), P(CLS, None), P(dp))
    return jax.shard_map(
        shards,
        mesh=fine,
        in_specs=placed,
        out_specs=(P(CLS, None), P(CLS, None)),
        check_vma=False,
    )
```

time: 729 us -> 205 us (0.28)
  the two profiles are of different devices: /device:TPU:1 before, /device:TPU:21 now
where the time goes in v1:
time: 205 us; the launch traced here: 204 us
  blocking collectives  134 us (65%)
  local copies, waits for them, and re-layouts  18.3 us (9%)
  starting transfers between devices  15.8 us (8%)
  other arithmetic  14.3 us (7%)
  waiting for transfers between devices  10.7 us (5%)
  matrix products  9.84 us (5%)
    all_to_all x5, blocking collectives, exchange(): return lax.all_to_all(blocks, axes, 0, 0, tiled=True)  134 us
    concatenate x1, other arithmetic, shards(): whole = jnp.concatenate([first, second], axis=0)[:rows * groups]  7.84 us
    ppermute x1, starting transfers between devices, shards(): theirs = lax.ppermute(theirs, 'core', swap)  6.93 us
    slice x4, local copies, waits for them, and re-layouts, shards(): return (whole[:fc_rows], whole[fc_rows:])  6.04 us
    all_to_all x1, waiting for transfers between devices, exchange(): return lax.all_to_all(blocks, axes, 0, 0, tiled=True)  5.85 us
    unnamed x20, local copies, waits for them, and re-layouts  5.79 us
    all_to_all x1, starting transfers between devices, exchange(): return lax.all_to_all(blocks, axes, 0, 0, tiled=True)  5.56 us
  transfers between devices with their start and end apart: 3, of which 3 were waited for; matrix products, arithmetic and copies ran while one was open for 0% of the time, Pallas kernels for 0%

profile of v1, /device:TPU:21, one launch (start us, length us, event | category | flops | bytes accessed | tf_op | source)
XLA Modules:
  0.0 204.3 jit_solution(11925049054749996689)
XLA Ops:
  0.7 1.3 fusion.9
  2.2 2.6 %convolution_convert_fusion.1 = bf16[512,512]{1,0:T(8,128)(2,1)S(1)} fusion(bf16[512,1568]{0,1:T(8,128)(2,1)S(1)} %copy-done, bf16[1568,512]{1,0:T(8,128)(2,1)} %param.5), kind=kOutput, calls=%fused_computation.21 | convolution fusion | flops 822345728 | bytes 3735552 | tf_op jit(solution)/shard_map/dot_general | solution.py:65
  4.9 0.7 fusion.6
  5.7 17.6 %all_to_all.48 = bf16[8,64,1024]{2,1,0:T(8,128)(2,1)S(1)} all-to-all(bf16[8,64,1024]{2,1,0:T(8,128)(2,1)S(1)} %pad_maximum_fusion.1), channel_id=1, replica_groups=mesh['z'=8,'yh'=4,'core'=2,'x'=4,'yl'=2] {'x','yl'}, dimensions={0} | all-to-all | bytes 2097152 | tf_op jit(solution)/shard_map/all_to_all | solution.py:20
  23.8 10.5 %all_to_all.49 = bf16[8,64,512]{2,1,0:T(8,128)(2,1)S(1)} all-to-all(bf16[8,64,512]{2,1,0:T(8,128)(2,1)S(1)} %broadcast_in_dim.20), channel_id=1, replica_groups=mesh['z'=8,'yh'=4,'core'=2,'x'=4,'yl'=2] {'x','yl'}, dimensions={0} | all-to-all | bytes 1048576 | tf_op jit(solution)/shard_map/all_to_all | solution.py:20
  35.1 1.3 convolution_convert_fusion
  37.8 1.3 concatenate.28
  39.0 11.6 %all_to_all.50 = bf16[8,64,640]{2,1,0:T(8,128)(2,1)S(1)} all-to-all(bf16[8,64,640]{2,1,0:T(8,128)(2,1)S(1)} %concatenate.28), channel_id=1, replica_groups=mesh['z'=8,'yh'=4,'core'=2,'x'=4,'yl'=2] {'x','yl'}, dimensions={0} | all-to-all | bytes 1310720 | tf_op jit(solution)/shard_map/all_to_all | solution.py:20
  52.0 0.9 broadcast_in_dim.23
  52.9 5.6 %all-to-all-start.3 = ((bf16[8,64,640]{2,1,0:T(8,128)(2,1)}), bf16[8,64,640]{2,1,0:T(8,128)(2,1)S(1)}, u32[]{:S(2)}, u32[]{:S(2)}) async-start(bf16[8,64,640]{2,1,0:T(8,128)(2,1)} %broadcast_in_dim.23), calls=%async_computation.3 | async-start | bytes 1310720 | tf_op jit(solution)/shard_map/all_to_all | solution.py:20
  58.5 5.8 %all-to-all-done.3 = bf16[8,64,640]{2,1,0:T(8,128)(2,1)S(1)} async-done(((bf16[8,64,640]{2,1,0:T(8,128)(2,1)}), bf16[8,64,640]{2,1,0:T(8,128)(2,1)S(1)}, u32[]{:S(2)}, u32[]{:S(2)}) %all-to-all-start.3) | async-done | bytes 655392 | tf_op jit(solution)/shard_map/all_to_all | solution.py:20
  64.3 2.7 %convolution_bitcast_fusion = f32[1568,512]{1,0:T(8,128)} fusion(bf16[512,1568]{0,1:T(8,128)(2,1)S(1)} %copy-done, bf16[512,640]{1,0:T(8,128)(2,1)S(1)} %bitcast.51), kind=kOutput, calls=%fused_computation.4 | convolution fusion | flops 822083584 | bytes 5341184 | tf_op jit(solution)/shard_map/dot_general | solution.py:116
  67.0 0.8 fusion.32
  67.7 1.0 copy.87
  68.9 1.9 multiply_reduce_fusion
  71.5 1.3 fusion.2
  72.7 1.0 copy-done.1
  73.7 6.9 %collective-permute-start = (bf16[4352,128]{1,0:T(8,128)(2,1)}, bf16[4352,128]{1,0:T(8,128)(2,1)S(1)}, u32[]{:S(2)}, u32[]{:S(2)}) collective-permute-start(bf16[4352,128]{1,0:T(8,128)(2,1)} %fusion.2), channel_id=1, source_target_pairs={{0,8},{8,0},{1,9},{9,1},{2,10},{10,2},{3,11},{11,3},{4,12},{12,4},... | collective-permute-start | bytes 3342344 | tf_op jit(solution)/shard_map/ppermute | solution.py:132
  80.7 2.6 %collective-permute-done = bf16[4352,128]{1,0:T(8,128)(2,1)S(1)} collective-permute-done((bf16[4352,128]{1,0:T(8,128)(2,1)}, bf16[4352,128]{1,0:T(8,128)(2,1)S(1)}, u32[]{:S(2)}, u32[]{:S(2)}) %collective-permute-start) | collective-permute-done | bytes 1114144 | tf_op jit(solution)/shard_map/ppermute | solution.py:132
  83.3 1.8 fusion.1
  85.0 48.4 %all_to_all.51 = bf16[32,136,128]{2,1,0:T(8,128)(2,1)S(1)} all-to-all(bf16[32,136,128]{2,1,0:T(8,128)(2,1)S(1)} %bitcast.49), channel_id=1, replica_groups=mesh['z'=8,'yh'=4,'core'=2,'x'=4,'yl'=2] {'z','yh'}, dimensions={0} | all-to-all | bytes 2228224 | tf_op jit(solution)/shard_map/all_to_all | solution.py:20
  133.8 46.4 %all_to_all.52 = bf16[32,136,128]{2,1,0:T(8,128)(2,1)S(1)} all-to-all(bf16[32,136,128]{2,1,0:T(8,128)(2,1)S(1)} %broadcast_in_dim.28), channel_id=1, replica_groups=mesh['z'=8,'yh'=4,'core'=2,'x'=4,'yl'=2] {'z','yh'}, dimensions={0} | all-to-all | bytes 2228224 | tf_op jit(solution)/shard_map/all_to_all | solution.py:20
  180.2 3.3 %collective-permute-start.1 = (bf16[4352,128]{1,0:T(8,128)(2,1)S(1)}, bf16[4352,128]{1,0:T(8,128)(2,1)}, u32[]{:S(2)}, u32[]{:S(2)}) collective-permute-start(bf16[4352,128]{1,0:T(8,128)(2,1)S(1)} %bitcast.50), channel_id=1, source_target_pairs={{0,8},{8,0},{1,9},{9,1},{2,10},{10,2},{3,11},{11,3},{4,12},{12,4},... | collective-permute-start | bytes 3342344 | tf_op jit(solution)/shard_map/ppermute | solution.py:137
  183.5 2.3 %collective-permute-done.1 = bf16[4352,128]{1,0:T(8,128)(2,1)} collective-permute-done((bf16[4352,128]{1,0:T(8,128)(2,1)S(1)}, bf16[4352,128]{1,0:T(8,128)(2,1)}, u32[]{:S(2)}, u32[]{:S(2)}) %collective-permute-start.1) | collective-permute-done | bytes 1114144 | tf_op jit(solution)/shard_map/ppermute | solution.py:137
  185.8 1.4 broadcast_select_fusion.1
  187.2 7.8 %pad_maximum_fusion = bf16[8320,128]{1,0:T(8,128)(2,1)S(1)} fusion(bf16[4352,128]{1,0:T(8,128)(2,1)S(1)} %get-tuple-element.20, bf16[4352,128]{1,0:T(8,128)(2,1)S(1)} %get-tuple-element.19), kind=kLoop, calls=%fused_computation.8 | loop fusion | flops 4259840 | bytes 4358144 | tf_op jit(solution)/shard_map/concatenate | solution.py:140
  195.0 1.3 slice.61
  196.3 0.8 slice.62
  197.1 2.7 %copy.82 = bf16[1568,4,128]{0,2,1:T(8,128)(2,1)S(1)} copy(bf16[1568,4,128]{2,0,1:T(8,128)(2,1)} %slice.61) | data formatting | bytes 3211264 | tf_op jit(solution)/shard_map/slice | solution.py:142
  199.8 2.2 %copy.84 = bf16[1568,512]{1,0:T(8,128)(2,1)} copy(bf16[1568,512]{0,1:T(8,128)(2,1)S(1)} %bitcast.48) | data formatting | bytes 3211264
  202.1 1.2 copy.83
  203.3 1.0 copy.85
  (54 shorter events, 5.3 us)
Async XLA Ops:
  0.6 1.6 copy-start
  2.2 2.6 %copy-start.3 = (bf16[512,512]{1,0:T(8,128)(2,1)S(1)}, bf16[512,512]{1,0:T(8,128)(2,1)}, u32[]{:S(2)}) copy-start(bf16[512,512]{1,0:T(8,128)(2,1)} %param.6) | copy-start | bytes 1572868
  2.2 2.6 %copy-start.6 = (s32[512]{0:T(512)S(1)}, s32[512]{0:T(512)}, u32[]{:S(2)}) copy-start(s32[512]{0:T(512)} %param.7) | copy-start | bytes 6148
  34.4 0.8 copy-start.4
  35.1 1.3 copy-start.7
  52.9 11.4 %all-to-all-start.3 = ((bf16[8,64,640]{2,1,0:T(8,128)(2,1)}), bf16[8,64,640]{2,1,0:T(8,128)(2,1)S(1)}, u32[]{:S(2)}, u32[]{:S(2)}) async-start(bf16[8,64,640]{2,1,0:T(8,128)(2,1)} %broadcast_in_dim.23), calls=%async_computation.3 | async-start | bytes 1310720 | tf_op jit(solution)/shard_map/all_to_all | solution.py:20
  64.3 4.6 %copy-start.5 = (bf16[8,64,512]{2,1,0:T(8,128)(2,1)S(1)}, bf16[8,64,512]{2,1,0:T(8,128)(2,1)}, u32[]{:S(2)}) copy-start(bf16[8,64,512]{2,1,0:T(8,128)(2,1)} %copy-done.4) | copy-start | bytes 1572868
  68.9 2.2 %copy-start.2 = (f32[1568,512]{1,0:T(8,128)S(1)}, f32[1568,512]{1,0:T(8,128)}, u32[]{:S(2)}) copy-start(f32[1568,512]{1,0:T(8,128)} %convolution_bitcast_fusion) | copy-start | bytes 9633796
  71.4 2.3 %copy-start.1 = (f32[2080,4,128]{2,0,1:T(8,128)}, f32[2080,4,128]{2,0,1:T(8,128)S(1)}, u32[]{:S(2)}) copy-start(f32[2080,4,128]{2,0,1:T(8,128)S(1)} %copy_bitcast_fusion) | copy-start | bytes 12779524
  73.7 9.5 %collective-permute-start = (bf16[4352,128]{1,0:T(8,128)(2,1)}, bf16[4352,128]{1,0:T(8,128)(2,1)S(1)}, u32[]{:S(2)}, u32[]{:S(2)}) collective-permute-start(bf16[4352,128]{1,0:T(8,128)(2,1)} %fusion.2), channel_id=1, source_target_pairs={{0,8},{8,0},{1,9},{9,1},{2,10},{10,2},{3,11},{11,3},{4,12},{12,4},... | collective-permute-start | bytes 3342344 | tf_op jit(solution)/shard_map/ppermute | solution.py:132
  180.2 5.6 %collective-permute-start.1 = (bf16[4352,128]{1,0:T(8,128)(2,1)S(1)}, bf16[4352,128]{1,0:T(8,128)(2,1)}, u32[]{:S(2)}, u32[]{:S(2)}) collective-permute-start(bf16[4352,128]{1,0:T(8,128)(2,1)S(1)} %bitcast.50), channel_id=1, source_target_pairs={{0,8},{8,0},{1,9},{9,1},{2,10},{10,2},{3,11},{11,3},{4,12},{12,4},... | collective-permute-start | bytes 3342344 | tf_op jit(solution)/shard_map/ppermute | solution.py:137

commit v2 on v0

v2 whole, which is shorter than its diff:
```python
import functools
import math

import jax
import jax.numpy as jnp
from jax import lax
from jax.experimental import pallas as pl
from jax.experimental.pallas import tpu as pltpu
from jax.sharding import Mesh
from jax.sharding import PartitionSpec as P

SCALE = 64.0
MARGIN = 0.5
SOFTEN = 0.01
EPSILON = 1e-06

CLS = ("x", "yl")
CHIPS = ("z", "yh")
LANES = 128
VMEM = pl.BlockSpec(memory_space=pltpu.VMEM)
SMEM = pl.BlockSpec(memory_space=pltpu.SMEM)


def exchange(blocks, axes):
    return lax.all_to_all(blocks, axes, 0, 0, tiled=True)


def across(left, right):
    return lax.dot_general(
        left, right, (((0,), (0,)), ((), ())), preferred_element_type=jnp.float32
    )


def row_norm(values):
    return jnp.sqrt(jnp.sum(values * values, axis=1, keepdims=True) + EPSILON)


def packed_columns(*columns):
    rows = columns[0].shape[0]
    lane = lax.broadcasted_iota(jnp.int32, (rows, LANES), 1)
    block = jnp.zeros((rows, LANES), jnp.float32)
    for at, column in enumerate(columns):
        rest = column
        for part in range(3):
            term = rest.astype(jnp.bfloat16).astype(jnp.float32)
            block = jnp.where(lane == 3 * at + part, term, block)
            rest = rest - term
    return block.astype(jnp.bfloat16)


def unpacked_column(block, at):
    lane = lax.broadcasted_iota(jnp.int32, block.shape, 1)
    inside = (lane >= 3 * at) & (lane < 3 * at + 3)
    return jnp.sum(jnp.where(inside, block, 0.0), axis=1, keepdims=True)


def embed_kernel(first_ref, features_ref, fc_ref, class_ref, labels_ref, sent_ref, unit_ref):
    width = fc_ref.shape[1]

    @pl.when(pl.program_id(0) == 0)
    def _():
        class_f = class_ref[...].astype(jnp.float32)
        unit_ref[...] = (class_f / row_norm(class_f)).astype(jnp.bfloat16)

    raw_part = jnp.dot(features_ref[...], fc_ref[...], preferred_element_type=jnp.float32)
    sent_ref[:, :width] = raw_part.astype(jnp.bfloat16)
    classes = unit_ref.shape[0]
    columns = first_ref[0] + lax.broadcasted_iota(
        jnp.int32, (features_ref.shape[0], classes), 1
    )
    chosen = jnp.where(columns == labels_ref[...], 1.0, 0.0).astype(jnp.bfloat16)
    target_part = jnp.dot(chosen, unit_ref[...], preferred_element_type=jnp.float32)
    sent_ref[:, width:] = target_part.astype(jnp.bfloat16)


def embed(first, features, fc_weight, class_weight, labels):
    faces, inputs = features.shape
    classes, width = class_weight.shape
    step = 128
    return pl.pallas_call(
        embed_kernel,
        grid=(faces // step,),
        in_specs=[
            SMEM,
            pl.BlockSpec((step, inputs), lambda i: (i, 0)),
            pl.BlockSpec((inputs, width), lambda i: (0, 0)),
            pl.BlockSpec((classes, width), lambda i: (0, 0)),
            pl.BlockSpec((step, 1), lambda i: (i, 0)),
        ],
        out_specs=[
            pl.BlockSpec((step, 2 * width), lambda i: (i, 0)),
            pl.BlockSpec((classes, width), lambda i: (0, 0)),
        ],
        out_shape=[
            jax.ShapeDtypeStruct((faces, 2 * width), jnp.bfloat16),
            jax.ShapeDtypeStruct((classes, width), jnp.bfloat16),
        ],
        name="embed",
    )(first, features, fc_weight, class_weight, labels)


def cosine_kernel(first_ref, units_ref, class_ref, labels_ref, pull_ref, others_ref):
    faces, width = units_ref.shape
    classes = class_ref.shape[0]
    step = 128
    for at in range(0, faces, step):
        here = slice(at, at + step)
        cosine = lax.dot_general(
            units_ref[here, :],
            class_ref[...],
            (((1,), (1,)), ((), ())),
            preferred_element_type=jnp.float32,
        )
        columns = first_ref[0] + lax.broadcasted_iota(jnp.int32, (step, classes), 1)
        is_target = columns == labels_ref[here, :]
        powers = jnp.exp(SCALE * cosine)
        others = jnp.where(is_target, 0.0, powers)
        others_ref[here, :] = jnp.where(is_target, -1.0, powers)
        pull = jnp.dot(
            others.astype(jnp.bfloat16), class_ref[...], preferred_element_type=jnp.float32
        )
        pull_ref[here, :width] = pull.astype(jnp.bfloat16)
        pull_ref[here, width:] = packed_columns(jnp.sum(others, axis=1, keepdims=True))


def cosines(first, units, class_unit, labels):
    faces, width = units.shape
    classes = class_unit.shape[0]
    return pl.pallas_call(
        cosine_kernel,
        in_specs=[SMEM, VMEM, VMEM, VMEM],
        out_specs=[VMEM, VMEM],
        out_shape=[
            jax.ShapeDtypeStruct((faces, width + LANES), jnp.bfloat16),
            jax.ShapeDtypeStruct((faces, classes), jnp.float32),
        ],
        name="cosines",
    )(first, units, class_unit, labels)


def raw_grad_kernel(loss_weight, pulls_ref, raw_ref, target_ref, sent_ref):
    width = raw_ref.shape[1]
    pulls = jnp.sum(pulls_ref[...].astype(jnp.float32), axis=0)
    pull, rest = pulls[:, :width], unpacked_column(pulls[:, width:], 0)
    raw_embed, target = raw_ref[...], target_ref[...]
    embed_norm = row_norm(raw_embed)
    unit_f = raw_embed / embed_norm
    unit = unit_f.astype(jnp.bfloat16).astype(jnp.float32)
    cos_t = jnp.sum(unit * target, axis=1, keepdims=True)
    sine_t = jnp.sqrt(1.0 + SOFTEN - cos_t * cos_t)
    power_t = jnp.exp(SCALE * (cos_t * math.cos(MARGIN) - sine_t * math.sin(MARGIN)))
    slope_t = SCALE * (math.cos(MARGIN) + math.sin(MARGIN) * cos_t / sine_t)
    inverse = loss_weight / (rest + power_t)
    pull_scale = SCALE * inverse
    target_scale = rest * inverse * slope_t
    unit_grad = pull * pull_scale - target * target_scale
    raw_grad = (
        unit_grad - unit_f * jnp.sum(unit_f * unit_grad, axis=1, keepdims=True)
    ) / embed_norm
    raw_grad = raw_grad.astype(jnp.bfloat16)
    scales = packed_columns(pull_scale, target_scale)
    for copy in range(sent_ref.shape[0]):
        sent_ref[copy, :, :width] = raw_grad
        sent_ref[copy, :, width:] = scales


def raw_grads(loss_weight, pulls, raw_embed, target_unit):
    return pl.pallas_call(
        functools.partial(raw_grad_kernel, loss_weight),
        in_specs=[VMEM, VMEM, VMEM],
        out_specs=VMEM,
        out_shape=jax.ShapeDtypeStruct(pulls.shape, jnp.bfloat16),
        name="raw_grads",
    )(pulls, raw_embed, target_unit)


def parts_kernel(
    half_ref, features_ref, grads_ref, units_ref, others_ref, class_ref, out_ref
):
    chips = out_ref.shape[0]
    classes, width = class_ref.shape
    groups = width // LANES
    inputs = features_ref.shape[1]
    rows = inputs // (2 * chips * 8) * 8
    main = 2 * chips * rows
    half = half_ref[0]
    grads = grads_ref[:, :width]
    some = chips // 2
    for at in range(0, chips, some):
        first = pl.multiple_of(half * (chips * rows) + at * rows, LANES)
        part = across(features_ref[:, pl.ds(first, some * rows)], grads)
        part = part.astype(out_ref.dtype).reshape(some, rows, width)
        for group in range(groups):
            out_ref[at : at + some, group * rows : (group + 1) * rows, :] = part[
                :, :, group * LANES : (group + 1) * LANES
            ]

    over = across(features_ref[:, main:], grads)
    each = over.shape[0] // 2
    over = jnp.where(half == 0, over[:each], over[each:]).astype(out_ref.dtype)
    base = groups * rows
    used = each // 8 * groups
    for tile in range(used):
        row, group = tile // groups * 8, tile % groups * LANES
        out_ref[tile, base + groups * 8 :, :] = over[row : row + 8, group : group + LANES]
    out_ref[used:, base + groups * 8 :, :] = jnp.zeros(
        (chips - used, 8, LANES), out_ref.dtype
    )

    scales = grads_ref[:, width:].astype(jnp.float32)
    pull_scale, target_scale = unpacked_column(scales, 0), unpacked_column(scales, 1)
    count = classes // 2
    first = pl.multiple_of(half * count, LANES)
    others = others_ref[:, pl.ds(first, count)]
    cos_grad = jnp.where(others < 0.0, -target_scale, others * pull_scale)
    part = across(cos_grad.astype(jnp.bfloat16), units_ref[...])
    class_f = class_ref[pl.ds(first, count), :].astype(jnp.float32)
    class_norm = row_norm(class_f)
    class_unit = class_f / class_norm
    part = (part - class_unit * jnp.sum(class_unit * part, axis=1, keepdims=True)) / class_norm
    part = part.astype(out_ref.dtype).reshape(chips, 8, width)
    for group in range(groups):
        out_ref[:, base + group * 8 : base + (group + 1) * 8, :] = part[
            :, :, group * LANES : (group + 1) * LANES
        ]


def parts(half, dtype, chips, features, grads, units, others, class_weight):
    groups = class_weight.shape[1] // LANES
    rows = features.shape[1] // (2 * chips * 8) * 8
    height = groups * rows + groups * 8 + 8
    return pl.pallas_call(
        parts_kernel,
        in_specs=[SMEM, VMEM, VMEM, VMEM, VMEM, VMEM],
        out_specs=VMEM,
        out_shape=jax.ShapeDtypeStruct((chips, height, LANES), dtype),
        name="parts",
    )(half, features, grads, units, others, class_weight)


def assemble_kernel(core_ref, mine_ref, theirs_ref, fc_ref, class_ref):
    chips = mine_ref.shape[0]
    inputs, width = fc_ref.shape
    groups = width // LANES
    rows = inputs // (2 * chips * 8) * 8
    main = 2 * chips * rows
    each = (inputs - main) // 2
    base = groups * rows
    count = class_ref.shape[0] // 2
    for source, half in ((mine_ref, core_ref[0]), (theirs_ref, 1 - core_ref[0])):
        for group in range(groups):
            lanes = slice(group * LANES, (group + 1) * LANES)
            block = source[:, group * rows : (group + 1) * rows, :].astype(jnp.float32)
            fc_ref[pl.ds(pl.multiple_of(half * (chips * rows), LANES), chips * rows), lanes] = (
                block.reshape(chips * rows, LANES).astype(jnp.bfloat16)
            )
            block = source[:, base + group * 8 : base + (group + 1) * 8, :].astype(jnp.float32)
            class_ref[pl.ds(pl.multiple_of(half * count, LANES), count), lanes] = (
                block.reshape(count, LANES).astype(jnp.bfloat16)
            )
            strips = each // 8
            block = jnp.concatenate(
                [source[strip * groups + group, base + groups * 8 :, :] for strip in range(strips)],
                axis=0,
            )
            fc_ref[pl.ds(pl.multiple_of(main + half * each, each), each), lanes] = block


def assemble(core, mine, theirs, inputs, classes, width):
    return pl.pallas_call(
        assemble_kernel,
        in_specs=[SMEM, VMEM, VMEM],
        out_specs=[VMEM, VMEM],
        out_shape=[
            jax.ShapeDtypeStruct((inputs, width), jnp.bfloat16),
            jax.ShapeDtypeStruct((classes, width), jnp.bfloat16),
        ],
        name="assemble",
    )(core, mine, theirs)


def shards(features, fc_weight, class_weight, labels):
    faces, inputs = features.shape
    classes, width = class_weight.shape
    n_cls = lax.axis_size(CLS)
    chips = lax.axis_size(CHIPS)
    loss_weight = 1.0 / math.sqrt(faces * chips * lax.axis_size("core"))
    first = (lax.axis_index(CLS) * classes).reshape(1)
    core = lax.axis_index("core").reshape(1)
    labels = labels.reshape(faces, 1)

    sent, class_unit = embed(first, features, fc_weight, class_weight, labels)
    got = exchange(sent, CLS).reshape(n_cls, faces // n_cls, 2 * width)
    got = jnp.sum(got.astype(jnp.float32), axis=0)
    raw_embed, target_unit = got[:, :width], got[:, width:]
    unit = (raw_embed / row_norm(raw_embed)).astype(jnp.bfloat16)
    units = exchange(jnp.broadcast_to(unit, (n_cls,) + unit.shape), CLS)
    units = units.reshape(faces, width)

    pull, others = cosines(first, units, class_unit, labels)
    got = exchange(pull, CLS).reshape(n_cls, faces // n_cls, width + LANES)
    sent = raw_grads(loss_weight, got, raw_embed, target_unit)
    grads = exchange(sent, CLS).reshape(faces, width + LANES)

    swap = [(0, 1), (1, 0)]
    operands = (features, grads, units, others, class_weight)
    theirs = lax.ppermute(parts(1 - core, jnp.bfloat16, chips, *operands), "core", swap)
    mine = parts(core, jnp.float32, chips, *operands)
    mine = (mine + theirs.astype(jnp.float32)).astype(jnp.bfloat16)
    done = jnp.sum(exchange(mine, CHIPS).astype(jnp.float32), axis=0).astype(jnp.bfloat16)
    mine = exchange(jnp.broadcast_to(done, (chips,) + done.shape), CHIPS)
    theirs = lax.ppermute(mine, "core", swap)
    return tuple(assemble(core, mine, theirs, inputs, classes, width))


def solution(mesh):
    fine = Mesh(mesh.devices.reshape(8, 4, 2, 4, 2), ("z", "yh", "core", "x", "yl"))
    dp = ("z", "yh", "core")
    placed = (P(dp, CLS), P(CLS, None), P(CLS, None), P(dp))
    return jax.shard_map(
        shards,
        mesh=fine,
        in_specs=placed,
        out_specs=(P(CLS, None), P(CLS, None)),
        check_vma=False,
    )
```

time: 729 us -> 195 us (0.27)
  waiting for transfers between devices: 304 us -> 10.5 us
  blocking collectives: 390 us -> 132 us
  Pallas kernels: 0 us -> 23.7 us
  starting transfers between devices: 0.12 us -> 17 us
  between operations: 13.8 us -> 0.72 us
  matrix products: 10.6 us -> 0 us
    psum x2 -> x0, blocking collectives: 342 us -> none  [the longest x1 327 us: shards(): fc_total, class_total = lax.psum((fc_part, class_part), 'dp')]
    psum x1 -> x0, waiting for transfers between devices: 210 us -> none  [shards(): fc_total, class_total = lax.psum((fc_part, class_part), 'dp')]
    all_to_all x0 -> x5, blocking collectives: none -> 132 us  [exchange(): return lax.all_to_all(blocks, axes, 0, 0, tiled=True)]
    reduce_scatter x2 -> x0, waiting for transfers between devices: 93.8 us -> none  [the longest x1 50 us: shards(): lax.psum_scatter(jnp.dot(rows_block, class_unit, preferred_element_type=j...]
    all_gather x2 -> x0, blocking collectives: 48.1 us -> none  [the longest x1 24.7 us: shards(): lax.all_gather(raw_grad, 'cls', axis=0, tiled=True)]
    pallas_call x0 -> x6, Pallas kernels: none -> 23.7 us  [the longest x2 8.83 us: parts(): pl.pallas_call(parts_kernel, in_specs=[SMEM, VMEM, VMEM, VMEM, VMEM, VMEM...]
    ppermute x0 -> x2, starting transfers between devices: none -> 13.4 us  [the longest x1 10.8 us: shards(): lax.ppermute(parts(1 - core, jnp.bfloat16, chips, *operands), 'core', swap)]
    dot_general x5 -> x0, matrix products: 10.6 us -> none  [the longest x1 3.35 us: shards(): jnp.dot(rows_block, fc_weight, preferred_element_type=jnp.float32)]
  transfers between devices with their start and end apart: 3 -> 3, of which waited for: 3 -> 2; matrix products, arithmetic and copies ran while one was open for 1% -> 0% of each run, Pallas kernels for 0% -> 2%
where the time goes in v2:
time: 195 us; the launch traced here: 194 us
  blocking collectives  132 us (68%)
  Pallas kernels  23.7 us (12%)
  starting transfers between devices  17 us (9%)
  waiting for transfers between devices  10.5 us (5%)
  local copies, waits for them, and re-layouts  7.14 us (4%)
  other arithmetic  3.11 us (2%)
    all_to_all x5, blocking collectives, exchange(): return lax.all_to_all(blocks, axes, 0, 0, tiled=True)  132 us
    ppermute x1, starting transfers between devices, shards(): lax.ppermute(parts(1 - core, jnp.bfloat16, chips, *operands), 'core', swap)  10.8 us
    pallas_call x2, Pallas kernels, parts(): pl.pallas_call(parts_kernel, in_specs=[SMEM, VMEM, VMEM, VMEM, VMEM, VMEM...  8.83 us
    all_to_all x1, waiting for transfers between devices, exchange(): return lax.all_to_all(blocks, axes, 0, 0, tiled=True)  8.17 us
    unnamed x7, local copies, waits for them, and re-layouts  5.43 us
    pallas_call x1, Pallas kernels, embed(): pl.pallas_call(embed_kernel, grid=(faces // step,), in_specs=[SMEM, pl.Bl...  5.34 us
  transfers between devices with their start and end apart: 3, of which 2 were waited for; matrix products, arithmetic and copies ran while one was open for 0% of the time, Pallas kernels for 2%

profile of v2, /device:TPU:1, one launch (start us, length us, event | category | flops | bytes accessed | tf_op | source)
XLA Modules:
  0.0 194.1 jit_solution(5186182340721349106)
XLA Ops:
  0.6 1.5 copy.10.labels_ref
  2.2 3.5 %copy.12.features_ref = bf16[512,1568]{1,0:T(8,128)(2,1)} copy(bf16[512,1568]{0,1:T(8,128)(2,1)} %param.4) | data formatting | bytes 3211264 | tf_op args[0]
  5.7 5.3 %embed.1 = (bf16[512,1024]{1,0:T(8,128)(2,1)}, bf16[512,512]{1,0:T(8,128)(2,1)}) custom-call(s32[1]{0:T(128)} %bitcast.1.first_ref, bf16[512,1568]{1,0:T(8,128)(2,1)} %copy.12.features_ref, bf16[1568,512]{1,0:T(8,128)(2,1)} %fc_ref.1, bf16[512,512]{1,0:T(8,128)(2,1)} %class_ref.5, s32[512,1]{1,0:T(8,128)} %copy.10.labels_ref), custom_call_target="tpu_custom_call" | custom-call | tf_op jit(solution)/shard_map/embed/pallas_call | solution.py:80
  11.0 17.1 %all_to_all.38 = bf16[8,64,1024]{2,1,0:T(8,128)(2,1)S(1)} all-to-all(bf16[8,64,1024]{2,1,0:T(8,128)(2,1)} %bitcast.12), channel_id=1, replica_groups=mesh['z'=8,'yh'=4,'core'=2,'x'=4,'yl'=2] {'x','yl'}, dimensions={0} | all-to-all | bytes 2097152 | tf_op jit(solution)/shard_map/all_to_all | solution.py:25
  28.1 0.2 convert_reduce_fusion
  28.3 0.8 fusion
  29.1 0.1 divide_convert_fusion
  29.3 10.6 %all_to_all.39 = bf16[8,64,512]{2,1,0:T(8,128)(2,1)} all-to-all(bf16[8,64,512]{2,1,0:T(8,128)(2,1)S(1)} %broadcast_in_dim.7), channel_id=1, replica_groups=mesh['z'=8,'yh'=4,'core'=2,'x'=4,'yl'=2] {'x','yl'}, dimensions={0} | all-to-all | bytes 1048576 | tf_op jit(solution)/shard_map/all_to_all | solution.py:25
  39.9 3.9 %cosines.1 = (bf16[512,640]{1,0:T(8,128)(2,1)}, f32[512,512]{1,0:T(8,128)}) custom-call(s32[1]{0:T(128)} %bitcast.1.first_ref, bf16[512,512]{1,0:T(8,128)(2,1)} %bitcast.7, bf16[512,512]{1,0:T(8,128)(2,1)} %get-tuple-element.7.class_ref, s32[512,1]{1,0:T(8,128)} %copy.10.labels_ref), custom_call_target="tpu_custom_call" | custom-call | tf_op jit(solution)/shard_map/cosines/pallas_call | solution.py:129
  43.8 12.5 %all_to_all.40.pulls_ref = bf16[8,64,640]{2,1,0:T(8,128)(2,1)} all-to-all(bf16[8,64,640]{2,1,0:T(8,128)(2,1)} %bitcast.13), channel_id=1, replica_groups=mesh['z'=8,'yh'=4,'core'=2,'x'=4,'yl'=2] {'x','yl'}, dimensions={0} | all-to-all | bytes 1310720 | tf_op jit(solution)/shard_map/all_to_all | solution.py:25
  56.3 2.4 %raw_grads.1 = bf16[8,64,640]{2,1,0:T(8,128)(2,1)} custom-call(bf16[8,64,640]{2,1,0:T(8,128)(2,1)} %all_to_all.40.pulls_ref, f32[64,512]{1,0:T(8,128)} %get-tuple-element.12.raw_ref, f32[64,512]{1,0:T(8,128)} %get-tuple-element.10.target_ref), custom_call_target="tpu_custom_call" | custom-call | tf_op jit(solution)/shard_map/raw_grads/pallas_call | solution.py:168
  58.7 3.5 %all-to-all-start.3 = ((bf16[8,64,640]{2,1,0:T(8,128)(2,1)}), bf16[8,64,640]{2,1,0:T(8,128)(2,1)S(1)}, u32[]{:S(2)}, u32[]{:S(2)}) async-start(bf16[8,64,640]{2,1,0:T(8,128)(2,1)} %raw_grads.1), calls=%async_computation.3 | async-start | bytes 1310720 | tf_op jit(solution)/shard_map/all_to_all | solution.py:25
  62.3 8.2 %all-to-all-done.3 = bf16[8,64,640]{2,1,0:T(8,128)(2,1)S(1)} async-done(((bf16[8,64,640]{2,1,0:T(8,128)(2,1)}), bf16[8,64,640]{2,1,0:T(8,128)(2,1)S(1)}, u32[]{:S(2)}, u32[]{:S(2)}) %all-to-all-start.3) | async-done | bytes 655392 | tf_op jit(solution)/shard_map/all_to_all | solution.py:25
  70.4 0.0 copy-start
  70.4 0.9 copy-done
  71.3 4.2 %parts.3 = bf16[32,136,128]{2,1,0:T(8,128)(2,1)} custom-call(s32[1]{0:T(128)S(6)} %sub.3.half_ref, bf16[512,1568]{1,0:T(8,128)(2,1)} %copy.12.features_ref, bf16[512,640]{1,0:T(8,128)(2,1)} %bitcast.10, bf16[512,512]{1,0:T(8,128)(2,1)} %bitcast.8, f32[512,512]{1,0:T(8,128)} %get-tuple-element.9.others_ref, bf16[512,512]{1,0:T(8,128)(2,1)} %class_ref.5), custom_call_target="tpu_custom_call" | custom-call | tf_op jit(solution)/shard_map/parts/pallas_call | solution.py:232
  75.5 10.8 %collective-permute-start = (bf16[32,136,128]{2,1,0:T(8,128)(2,1)}, bf16[32,136,128]{2,1,0:T(8,128)(2,1)S(1)}, u32[]{:S(2)}, u32[]{:S(2)}) collective-permute-start(bf16[32,136,128]{2,1,0:T(8,128)(2,1)} %parts.3), channel_id=1, source_target_pairs={{0,8},{8,0},{1,9},{9,1},{2,10},{10,2},{3,11},{11,3},{4,12},{12,4},... | collective-permute-start | bytes 3342344 | tf_op jit(solution)/shard_map/ppermute | solution.py:307
  86.3 4.6 %parts.2 = f32[32,136,128]{2,1,0:T(8,128)} custom-call(s32[1]{0:T(128)} %bitcast.half_ref.core_ref, bf16[512,1568]{1,0:T(8,128)(2,1)} %copy.12.features_ref, bf16[512,640]{1,0:T(8,128)(2,1)} %bitcast.11, bf16[512,512]{1,0:T(8,128)(2,1)} %bitcast.9, f32[512,512]{1,0:T(8,128)} %get-tuple-element.9.others_ref, bf16[512,512]{1,0:T(8,128)(2,1)} %class_ref.5), custom_call_target="tpu_custom_call" | custom-call | tf_op jit(solution)/shard_map/parts/pallas_call | solution.py:232
  90.9 0.0 collective-permute-done
  90.9 1.8 add_convert_fusion
  92.8 50.1 %all_to_all.41 = bf16[32,136,128]{2,1,0:T(8,128)(2,1)S(1)} all-to-all(bf16[32,136,128]{2,1,0:T(8,128)(2,1)S(1)} %add_convert_fusion), channel_id=1, replica_groups=mesh['z'=8,'yh'=4,'core'=2,'x'=4,'yl'=2] {'z','yh'}, dimensions={0} | all-to-all | bytes 2228224 | tf_op jit(solution)/shard_map/all_to_all | solution.py:25
  142.9 0.2 reduce_sum.32
  143.1 0.1 broadcast_in_dim.8
  143.2 41.5 %all_to_all.42.mine_ref = bf16[32,136,128]{2,1,0:T(8,128)(2,1)S(1)} all-to-all(bf16[32,136,128]{2,1,0:T(8,128)(2,1)S(1)} %broadcast_in_dim.8), channel_id=1, replica_groups=mesh['z'=8,'yh'=4,'core'=2,'x'=4,'yl'=2] {'z','yh'}, dimensions={0} | all-to-all | bytes 2228224 | tf_op jit(solution)/shard_map/all_to_all | solution.py:25
  184.7 0.0 copy-start.1
  184.7 2.7 %collective-permute-start.1 = (bf16[32,136,128]{2,1,0:T(8,128)(2,1)S(1)}, bf16[32,136,128]{2,1,0:T(8,128)(2,1)S(1)}, u32[]{:S(2)}, u32[]{:S(2)}) collective-permute-start(bf16[32,136,128]{2,1,0:T(8,128)(2,1)S(1)} %all_to_all.42.mine_ref), channel_id=1, source_target_pairs={{0,8},{8,0},{1,9},{9,1},{2,10},{10,2},{3,11},{11,3},{4,12},{12,4},... | collective-permute-start | bytes 3342344 | tf_op jit(solution)/shard_map/ppermute | solution.py:312
  187.4 2.4 %collective-permute-done.1.theirs_ref = bf16[32,136,128]{2,1,0:T(8,128)(2,1)S(1)} collective-permute-done((bf16[32,136,128]{2,1,0:T(8,128)(2,1)S(1)}, bf16[32,136,128]{2,1,0:T(8,128)(2,1)S(1)}, u32[]{:S(2)}, u32[]{:S(2)}) %collective-permute-start.1) | collective-permute-done | bytes 1114144 | tf_op jit(solution)/shard_map/ppermute | solution.py:312
  189.8 0.0 copy-done.1
  189.8 0.0 copy-start.2
  189.8 1.0 copy-done.2
  190.8 3.3 %assemble.1 = (bf16[1568,512]{1,0:T(8,128)(2,1)}, bf16[512,512]{1,0:T(8,128)(2,1)}) custom-call(s32[1]{0:T(128)} %bitcast.half_ref.core_ref, bf16[32,136,128]{2,1,0:T(8,128)(2,1)} %copy-done.1, bf16[32,136,128]{2,1,0:T(8,128)(2,1)} %copy-done.2), custom_call_target="tpu_custom_call" | custom-call | tf_op jit(solution)/shard_map/assemble/pallas_call | solution.py:270
  (2 shorter events, 0.0 us)
Async XLA Ops:
  58.7 11.7 %all-to-all-start.3 = ((bf16[8,64,640]{2,1,0:T(8,128)(2,1)}), bf16[8,64,640]{2,1,0:T(8,128)(2,1)S(1)}, u32[]{:S(2)}, u32[]{:S(2)}) async-start(bf16[8,64,640]{2,1,0:T(8,128)(2,1)} %raw_grads.1), calls=%async_computation.3 | async-start | bytes 1310720 | tf_op jit(solution)/shard_map/all_to_all | solution.py:25
  70.4 0.9 copy-start
  75.5 15.4 %collective-permute-start = (bf16[32,136,128]{2,1,0:T(8,128)(2,1)}, bf16[32,136,128]{2,1,0:T(8,128)(2,1)S(1)}, u32[]{:S(2)}, u32[]{:S(2)}) collective-permute-start(bf16[32,136,128]{2,1,0:T(8,128)(2,1)} %parts.3), channel_id=1, source_target_pairs={{0,8},{8,0},{1,9},{9,1},{2,10},{10,2},{3,11},{11,3},{4,12},{12,4},... | collective-permute-start | bytes 3342344 | tf_op jit(solution)/shard_map/ppermute | solution.py:307
  184.7 5.0 %copy-start.1 = (bf16[32,136,128]{2,1,0:T(8,128)(2,1)}, bf16[32,136,128]{2,1,0:T(8,128)(2,1)S(1)}, u32[]{:S(2)}) copy-start(bf16[32,136,128]{2,1,0:T(8,128)(2,1)S(1)} %all_to_all.42.mine_ref) | copy-start | bytes 3342340
  184.7 5.0 %collective-permute-start.1 = (bf16[32,136,128]{2,1,0:T(8,128)(2,1)S(1)}, bf16[32,136,128]{2,1,0:T(8,128)(2,1)S(1)}, u32[]{:S(2)}, u32[]{:S(2)}) collective-permute-start(bf16[32,136,128]{2,1,0:T(8,128)(2,1)S(1)} %all_to_all.42.mine_ref), channel_id=1, source_target_pairs={{0,8},{8,0},{1,9},{9,1},{2,10},{10,2},{3,11},{11,3},{4,12},{12,4},... | collective-permute-start | bytes 3342344 | tf_op jit(solution)/shard_map/ppermute | solution.py:312
  189.8 1.0 copy-start.2

commit v3 on v2

v3 whole, which is shorter than its diff:
```python
import functools
import math

import jax
import jax.numpy as jnp
from jax import lax
from jax.experimental import pallas as pl
from jax.experimental.pallas import tpu as pltpu
from jax.sharding import Mesh
from jax.sharding import PartitionSpec as P

SCALE = 64.0
MARGIN = 0.5
SOFTEN = 0.01
EPSILON = 1e-06

CLS = ("x", "yl")
CHIPS = ("z", "yh")
LANES = 128
CHUNKS = 3
LIMIT = 24 << 20
VMEM = pl.BlockSpec(memory_space=pltpu.VMEM)
SMEM = pl.BlockSpec(memory_space=pltpu.SMEM)


def exchange(blocks, axes):
    return lax.all_to_all(blocks, axes, 0, 0, tiled=True)


def across(left, right):
    return lax.dot_general(
        left, right, (((0,), (0,)), ((), ())), preferred_element_type=jnp.float32
    )


def row_norm(values):
    return jnp.sqrt(jnp.sum(values * values, axis=1, keepdims=True) + EPSILON)


def packed_columns(*columns):
    rows = columns[0].shape[0]
    lane = lax.broadcasted_iota(jnp.int32, (rows, LANES), 1)
    block = jnp.zeros((rows, LANES), jnp.float32)
    for at, column in enumerate(columns):
        rest = column
        for part in range(3):
            term = rest.astype(jnp.bfloat16).astype(jnp.float32)
            block = jnp.where(lane == 3 * at + part, term, block)
            rest = rest - term
    return block.astype(jnp.bfloat16)


def unpacked_column(block, at):
    lane = lax.broadcasted_iota(jnp.int32, block.shape, 1)
    inside = (lane >= 3 * at) & (lane < 3 * at + 3)
    return jnp.sum(jnp.where(inside, block, 0.0), axis=1, keepdims=True)


def placed(array, space=pltpu.VMEM):
    return pltpu.with_memory_space_constraint(array, space)


def half_of(place_ref, other):
    core = lax.rem(place_ref[0], 2)
    return 1 - core if other else core


def first_of(place_ref, classes):
    return lax.div(place_ref[0], 2) * classes


def call(kernel, name, operands, results, **options):
    specs = [SMEM if operand.ndim == 1 else VMEM for operand in operands]
    operands = [operand if operand.ndim == 1 else placed(operand) for operand in operands]
    return pl.pallas_call(
        kernel,
        in_specs=specs,
        out_specs=[VMEM] * len(results),
        out_shape=[pltpu.VMEM(shape, dtype) for shape, dtype in results],
        compiler_params=pltpu.CompilerParams(vmem_limit_bytes=LIMIT),
        name=name,
        **options,
    )(*operands)


def target_mask(first, labels, rows, classes):
    lane = lax.broadcasted_iota(jnp.int32, (rows, LANES), 1)
    return jnp.concatenate(
        [labels == lane + (first + at) for at in range(0, classes, LANES)], axis=1
    )


def spread_labels(labels_row):
    faces = labels_row.shape[1]
    return jnp.transpose(jnp.broadcast_to(labels_row, (LANES, faces)))


def embed_kernel(
    place_ref, features_ref, fc_ref, class_ref, labels_ref, sent_ref, unit_ref,
    left_ref, right_ref, total_ref, left_sem, right_sem
):
    width = fc_ref.shape[1]
    inputs, faces = features_ref.shape
    classes = class_ref.shape[0]
    ends = [inputs * at // CHUNKS // LANES * LANES for at in range(CHUNKS)] + [inputs]
    copies = []
    for at in range(CHUNKS):
        rows = pl.ds(ends[at], ends[at + 1] - ends[at])
        pair = (
            pltpu.make_async_copy(features_ref.at[rows, :], left_ref.at[rows, :], left_sem.at[at]),
            pltpu.make_async_copy(fc_ref.at[rows, :], right_ref.at[rows, :], right_sem.at[at]),
        )
        for copy in pair:
            copy.start()
        copies.append(pair)

    class_f = class_ref[...].astype(jnp.float32)
    unit_ref[...] = (class_f / row_norm(class_f)).astype(jnp.bfloat16)
    labels = spread_labels(labels_ref[...])
    chosen = target_mask(first_of(place_ref, classes), labels, faces, classes)
    chosen = jnp.where(chosen, 1.0, 0.0).astype(jnp.bfloat16)
    target_part = jnp.dot(chosen, unit_ref[...], preferred_element_type=jnp.float32)
    sent_ref[:, width:] = target_part.astype(jnp.bfloat16)

    for at in range(CHUNKS):
        for copy in copies[at]:
            copy.wait()
        here = slice(ends[at], ends[at + 1])
        part = across(left_ref[here, :], right_ref[here, :])
        if at > 0:
            part = part + total_ref[...]
        if at < CHUNKS - 1:
            total_ref[...] = part
        else:
            sent_ref[:, :width] = part.astype(jnp.bfloat16)


def embed(place, features, fc_weight, class_weight, labels):
    inputs, faces = features.shape
    classes, width = class_weight.shape
    anywhere = pl.BlockSpec(memory_space=pltpu.HBM)
    return pl.pallas_call(
        embed_kernel,
        in_specs=[SMEM, anywhere, anywhere, VMEM, VMEM],
        out_specs=[VMEM, VMEM],
        out_shape=[
            pltpu.VMEM((faces, 2 * width), jnp.bfloat16),
            pltpu.VMEM((classes, width), jnp.bfloat16),
        ],
        scratch_shapes=[
            pltpu.VMEM((inputs, faces), jnp.bfloat16),
            pltpu.VMEM((inputs, width), jnp.bfloat16),
            pltpu.VMEM((faces, width), jnp.float32),
            pltpu.SemaphoreType.DMA((CHUNKS,)),
            pltpu.SemaphoreType.DMA((CHUNKS,)),
        ],
        compiler_params=pltpu.CompilerParams(vmem_limit_bytes=LIMIT),
        name="embed",
    )(
        place,
        placed(features, pltpu.HBM),
        placed(fc_weight, pltpu.HBM),
        placed(class_weight),
        placed(labels),
    )


def cosine_kernel(place_ref, units_ref, class_ref, labels_ref, pull_ref, others_ref):
    faces, width = units_ref.shape
    classes = class_ref.shape[0]
    step = 128
    labels = spread_labels(labels_ref[...])
    for at in range(0, faces, step):
        here = slice(at, at + step)
        cosine = lax.dot_general(
            units_ref[here, :],
            class_ref[...],
            (((1,), (1,)), ((), ())),
            preferred_element_type=jnp.float32,
        )
        is_target = target_mask(first_of(place_ref, classes), labels[here, :], step, classes)
        powers = jnp.exp(SCALE * cosine)
        others = jnp.where(is_target, 0.0, powers)
        others_ref[here, :] = jnp.where(is_target, -1.0, powers)
        pull = jnp.dot(
            others.astype(jnp.bfloat16), class_ref[...], preferred_element_type=jnp.float32
        )
        pull_ref[here, :width] = pull.astype(jnp.bfloat16)
        pull_ref[here, width:] = packed_columns(jnp.sum(others, axis=1, keepdims=True))


def cosines(place, units, class_unit, labels):
    faces, width = units.shape
    classes = class_unit.shape[0]
    return call(
        cosine_kernel,
        "cosines",
        (place, units, class_unit, labels),
        [((faces, width + LANES), jnp.bfloat16), ((faces, classes), jnp.float32)],
    )


def raw_grad_kernel(loss_weight, pulls_ref, raw_ref, target_ref, sent_ref):
    width = raw_ref.shape[1]
    pulls = jnp.sum(pulls_ref[...].astype(jnp.float32), axis=0)
    pull, rest = pulls[:, :width], unpacked_column(pulls[:, width:], 0)
    raw_embed, target = raw_ref[...], target_ref[...]
    embed_norm = row_norm(raw_embed)
    unit_f = raw_embed / embed_norm
    unit = unit_f.astype(jnp.bfloat16).astype(jnp.float32)
    cos_t = jnp.sum(unit * target, axis=1, keepdims=True)
    sine_t = jnp.sqrt(1.0 + SOFTEN - cos_t * cos_t)
    power_t = jnp.exp(SCALE * (cos_t * math.cos(MARGIN) - sine_t * math.sin(MARGIN)))
    slope_t = SCALE * (math.cos(MARGIN) + math.sin(MARGIN) * cos_t / sine_t)
    inverse = loss_weight / (rest + power_t)
    pull_scale = SCALE * inverse
    target_scale = rest * inverse * slope_t
    unit_grad = pull * pull_scale - target * target_scale
    raw_grad = (
        unit_grad - unit_f * jnp.sum(unit_f * unit_grad, axis=1, keepdims=True)
    ) / embed_norm
    raw_grad = raw_grad.astype(jnp.bfloat16)
    scales = packed_columns(pull_scale, target_scale)
    for copy in range(sent_ref.shape[0]):
        sent_ref[copy, :, :width] = raw_grad
        sent_ref[copy, :, width:] = scales


def raw_grads(loss_weight, pulls, raw_embed, target_unit):
    return call(
        functools.partial(raw_grad_kernel, loss_weight),
        "raw_grads",
        (pulls, raw_embed, target_unit),
        [(pulls.shape, jnp.bfloat16)],
    )[0]


def parts_kernel(
    other, place_ref, features_ref, grads_ref, units_ref, others_ref, class_ref, out_ref
):
    chips = out_ref.shape[0]
    classes, width = class_ref.shape
    groups = width // LANES
    inputs = features_ref.shape[0]
    rows = inputs // (2 * chips * 8) * 8
    main = 2 * chips * rows
    half = half_of(place_ref, other)
    grads = grads_ref[:, :width]
    some = chips // 2
    for at in range(0, chips, some):
        first = pl.multiple_of(half * (chips * rows) + at * rows, LANES)
        part = jnp.dot(
            features_ref[pl.ds(first, some * rows), :], grads, preferred_element_type=jnp.float32
        )
        part = part.astype(out_ref.dtype).reshape(some, rows, width)
        for group in range(groups):
            out_ref[at : at + some, group * rows : (group + 1) * rows, :] = part[
                :, :, group * LANES : (group + 1) * LANES
            ]

    each = (inputs - main) // 2
    over = jnp.dot(
        features_ref[pl.ds(pl.multiple_of(main + half * each, each), each), :],
        grads,
        preferred_element_type=jnp.float32,
    ).astype(out_ref.dtype)
    base = groups * rows
    used = each // 8 * groups
    for tile in range(used):
        row, group = tile // groups * 8, tile % groups * LANES
        out_ref[tile, base + groups * 8 :, :] = over[row : row + 8, group : group + LANES]
    out_ref[used:, base + groups * 8 :, :] = jnp.zeros(
        (chips - used, 8, LANES), out_ref.dtype
    )

    scales = grads_ref[:, width:].astype(jnp.float32)
    pull_scale, target_scale = unpacked_column(scales, 0), unpacked_column(scales, 1)
    count = classes // 2
    first = pl.multiple_of(half * count, LANES)
    others = others_ref[:, pl.ds(first, count)]
    cos_grad = jnp.where(others < 0.0, -target_scale, others * pull_scale)
    part = across(cos_grad.astype(jnp.bfloat16), units_ref[...])
    class_f = class_ref[pl.ds(first, count), :].astype(jnp.float32)
    class_norm = row_norm(class_f)
    class_unit = class_f / class_norm
    part = (part - class_unit * jnp.sum(class_unit * part, axis=1, keepdims=True)) / class_norm
    part = part.astype(out_ref.dtype).reshape(chips, 8, width)
    for group in range(groups):
        out_ref[:, base + group * 8 : base + (group + 1) * 8, :] = part[
            :, :, group * LANES : (group + 1) * LANES
        ]


def parts(other, place, dtype, chips, features, grads, units, others, class_weight):
    groups = class_weight.shape[1] // LANES
    rows = features.shape[0] // (2 * chips * 8) * 8
    height = groups * rows + groups * 8 + 8
    return call(
        functools.partial(parts_kernel, other),
        "parts",
        (place, features, grads, units, others, class_weight),
        [((chips, height, LANES), dtype)],
    )[0]


def assemble_kernel(other, place_ref, source_ref, *refs):
    fc_ref, class_ref, fc_half, fc_over, class_half, sems = refs[-6:]
    chips = source_ref.shape[0]
    inputs, width = fc_ref.shape
    groups = width // LANES
    rows = inputs // (2 * chips * 8) * 8
    main = 2 * chips * rows
    each = (inputs - main) // 2
    base = groups * rows
    count = class_ref.shape[0] // 2
    half = half_of(place_ref, other)

    for group in range(groups):
        lanes = slice(group * LANES, (group + 1) * LANES)
        block = source_ref[:, base + group * 8 : base + (group + 1) * 8, :].astype(jnp.float32)
        class_half[:, lanes] = block.reshape(count, LANES).astype(jnp.bfloat16)
        for strip in range(each // 8):
            fc_over[strip * 8 : strip * 8 + 8, lanes] = source_ref[
                strip * groups + group, base + groups * 8 :, :
            ]
    copies = [
        pltpu.make_async_copy(
            class_half, class_ref.at[pl.ds(pl.multiple_of(half * count, count), count), :], sems.at[0]
        ),
        pltpu.make_async_copy(
            fc_over, fc_ref.at[pl.ds(pl.multiple_of(main + half * each, each), each), :], sems.at[1]
        ),
    ]
    for copy in copies:
        copy.start()
    some = chips // 4
    for at in range(0, chips, some):
        for group in range(groups):
            lanes = slice(group * LANES, (group + 1) * LANES)
            block = source_ref[at : at + some, group * rows : (group + 1) * rows, :]
            block = block.astype(jnp.float32).reshape(some * rows, LANES)
            fc_half[at * rows : (at + some) * rows, lanes] = block.astype(jnp.bfloat16)
        first = pl.multiple_of(half * (chips * rows) + at * rows, some * rows)
        copies.append(
            pltpu.make_async_copy(
                fc_half.at[at * rows : (at + some) * rows, :],
                fc_ref.at[pl.ds(first, some * rows), :],
                sems.at[2 + at // some],
            )
        )
        copies[-1].start()
    for copy in copies:
        copy.wait()


def assemble(other, place, source, inputs, classes, width, *into):
    chips = source.shape[0]
    groups = width // LANES
    rows = inputs // (2 * chips * 8) * 8
    each = (inputs - 2 * chips * rows) // 2
    anywhere = pl.BlockSpec(memory_space=pltpu.HBM)
    return pl.pallas_call(
        functools.partial(assemble_kernel, other),
        in_specs=[SMEM, VMEM] + [anywhere] * len(into),
        out_specs=[anywhere, anywhere],
        out_shape=[
            jax.ShapeDtypeStruct((inputs, width), jnp.bfloat16),
            jax.ShapeDtypeStruct((classes, width), jnp.bfloat16),
        ],
        scratch_shapes=[
            pltpu.VMEM((chips * rows, width), jnp.bfloat16),
            pltpu.VMEM((each, width), jnp.bfloat16),
            pltpu.VMEM((classes // 2, width), jnp.bfloat16),
            pltpu.SemaphoreType.DMA((6,)),
        ],
        input_output_aliases={2 + at: at for at in range(len(into))},
        compiler_params=pltpu.CompilerParams(vmem_limit_bytes=LIMIT),
        name="assemble",
    )(place, placed(source), *into)


def shards(features, fc_weight, class_weight, labels):
    faces, inputs = features.shape
    features = features.T
    classes, width = class_weight.shape
    n_cls = lax.axis_size(CLS)
    chips = lax.axis_size(CHIPS)
    loss_weight = 1.0 / math.sqrt(faces * chips * lax.axis_size("core"))
    place = (lax.axis_index(CLS) * 2 + lax.axis_index("core")).reshape(1)
    labels = labels.reshape(1, faces)

    sent, class_unit = embed(place, features, fc_weight, class_weight, labels)
    got = exchange(sent, CLS).reshape(n_cls, faces // n_cls, 2 * width)
    got = jnp.sum(got.astype(jnp.float32), axis=0)
    raw_embed, target_unit = got[:, :width], got[:, width:]
    unit = (raw_embed / row_norm(raw_embed)).astype(jnp.bfloat16)
    units = exchange(jnp.broadcast_to(unit, (n_cls,) + unit.shape), CLS)
    units = units.reshape(faces, width)

    pull, others = cosines(place, units, class_unit, labels)
    got = exchange(pull, CLS).reshape(n_cls, faces // n_cls, width + LANES)
    sent = raw_grads(loss_weight, got, raw_embed, target_unit)
    grads = exchange(sent, CLS).reshape(faces, width + LANES)

    swap = [(0, 1), (1, 0)]
    operands = (features, grads, units, others, class_weight)
    theirs = lax.ppermute(parts(True, place, jnp.bfloat16, chips, *operands), "core", swap)
    mine = parts(False, place, jnp.float32, chips, *operands)
    mine = (mine + theirs.astype(jnp.float32)).astype(jnp.bfloat16)
    done = jnp.sum(exchange(mine, CHIPS).astype(jnp.float32), axis=0).astype(jnp.bfloat16)
    mine = exchange(jnp.broadcast_to(done, (chips,) + done.shape), CHIPS)
    theirs = lax.ppermute(mine, "core", swap)
    sizes = (inputs, classes, width)
    written = assemble(False, place, mine, *sizes)
    return tuple(assemble(True, place, theirs, *sizes, *written))


def solution(mesh):
    fine = Mesh(mesh.devices.reshape(8, 4, 2, 4, 2), ("z", "yh", "core", "x", "yl"))
    dp = ("z", "yh", "core")
    specs = (P(dp, CLS), P(CLS, None), P(CLS, None), P(dp))
    return jax.shard_map(
        shards,
        mesh=fine,
        in_specs=specs,
        out_specs=(P(CLS, None), P(CLS, None)),
        check_vma=False,
    )
```

time: 195 us -> 170 us (0.87)
  the two profiles are of different devices: /device:TPU:1 before, /device:TPU:5 now
where the time goes in v3:
time: 170 us
  blocking collectives  142 us (84%)
  starting transfers between devices  12.7 us (7%)
  Pallas kernels  8.73 us (5%)
  waiting for transfers between devices  2.71 us (2%)
  local copies, waits for them, and re-layouts  1.91 us (1%)
    all_to_all x6, blocking collectives, exchange(): return lax.all_to_all(blocks, axes, 0, 0, tiled=True)  142 us
    ppermute x1, starting transfers between devices, shards(): lax.ppermute(parts(True, place, jnp.bfloat16, chips, *operands), 'core',...  10 us
    pallas_call x4, Pallas kernels, call(): pl.pallas_call(kernel, in_specs=specs, out_specs=[VMEM] * len(results), o...  3.84 us
  transfers between devices with their start and end apart: 2, of which 2 were waited for; matrix products, arithmetic and copies ran while one was open for 0% of the time, Pallas kernels for 1%

profile of v3, /device:TPU:5, one launch (start us, length us, event | category | flops | bytes accessed | tf_op | source)
XLA Modules:
  0.0 169.8 jit_solution(7499399390796181081)
XLA Ops:
  0.6 0.0 copy-start.1
  0.7 1.0 copy-done.1
  1.7 0.0 copy-start.3
  1.7 0.7 copy-done.3
  2.4 2.8 %embed.1 = (bf16[512,1024]{1,0:T(8,128)(2,1)S(1)}, bf16[512,512]{1,0:T(8,128)(2,1)S(1)}) custom-call(s32[1]{0:T(128)} %bitcast.place_ref, bf16[1568,512]{1,0:T(8,128)(2,1)} %bitcast.7, bf16[1568,512]{1,0:T(8,128)(2,1)} %fc_ref.1, bf16[512,512]{1,0:T(8,128)(2,1)S(1)} %copy-done.1, s32[1,512]{1,0:T(1,128)S(1)} %bitcast.17), custom_call_target="tpu_custom_call" | custom-call | tf_op jit(solution)/shard_map/embed/pallas_call | solution.py:142
  5.1 14.8 %all_to_all.38 = bf16[8,64,1024]{2,1,0:T(8,128)(2,1)S(1)} all-to-all(bf16[8,64,1024]{2,1,0:T(8,128)(2,1)S(1)} %bitcast.15), channel_id=1, replica_groups=mesh['z'=8,'yh'=4,'core'=2,'x'=4,'yl'=2] {'x','yl'}, dimensions={0} | all-to-all | bytes 2097152 | tf_op jit(solution)/shard_map/all_to_all | solution.py:27
  19.9 0.2 convert_reduce_fusion
  20.1 0.1 fusion
  20.2 0.1 divide_convert_fusion
  20.4 10.4 %all_to_all.39 = bf16[8,64,512]{2,1,0:T(8,128)(2,1)S(1)} all-to-all(bf16[8,64,512]{2,1,0:T(8,128)(2,1)S(1)} %broadcast_in_dim.7), channel_id=1, replica_groups=mesh['z'=8,'yh'=4,'core'=2,'x'=4,'yl'=2] {'x','yl'}, dimensions={0} | all-to-all | bytes 1048576 | tf_op jit(solution)/shard_map/all_to_all | solution.py:27
  30.8 1.6 cosines.1
  32.4 10.8 %all_to_all.40.pulls_ref = bf16[8,64,640]{2,1,0:T(8,128)(2,1)S(1)} all-to-all(bf16[8,64,640]{2,1,0:T(8,128)(2,1)S(1)} %bitcast.16), channel_id=1, replica_groups=mesh['z'=8,'yh'=4,'core'=2,'x'=4,'yl'=2] {'x','yl'}, dimensions={0} | all-to-all | bytes 1310720 | tf_op jit(solution)/shard_map/all_to_all | solution.py:27
  43.3 0.0 copy-start
  43.3 0.0 copy-start.2
  43.3 0.4 raw_grads.1
  43.6 10.9 %all_to_all.41 = bf16[8,64,640]{2,1,0:T(8,128)(2,1)S(1)} all-to-all(bf16[8,64,640]{2,1,0:T(8,128)(2,1)S(1)} %raw_grads.1), channel_id=1, replica_groups=mesh['z'=8,'yh'=4,'core'=2,'x'=4,'yl'=2] {'x','yl'}, dimensions={0} | all-to-all | bytes 1310720 | tf_op jit(solution)/shard_map/all_to_all | solution.py:27
  54.5 0.0 copy-done
  54.5 0.0 copy-done.2
  54.5 0.9 parts.3
  55.5 10.0 %collective-permute-start = (bf16[32,136,128]{2,1,0:T(8,128)(2,1)S(1)}, bf16[32,136,128]{2,1,0:T(8,128)(2,1)S(1)}, u32[]{:S(2)}, u32[]{:S(2)}) collective-permute-start(bf16[32,136,128]{2,1,0:T(8,128)(2,1)S(1)} %parts.3), channel_id=1, source_target_pairs={{0,8},{8,0},{1,9},{9,1},{2,10},{10,2},{3,11},{11,3},{4,12},{12,4},... | collective-permute-start | bytes 3342344 | tf_op jit(solution)/shard_map/ppermute | solution.py:407
  65.5 0.9 parts.2
  66.4 1.4 collective-permute-done
  67.8 0.2 add_convert_fusion
  68.0 50.2 %all_to_all.42 = bf16[32,136,128]{2,1,0:T(8,128)(2,1)S(1)} all-to-all(bf16[32,136,128]{2,1,0:T(8,128)(2,1)S(1)} %add_convert_fusion), channel_id=1, replica_groups=mesh['z'=8,'yh'=4,'core'=2,'x'=4,'yl'=2] {'z','yh'}, dimensions={0} | all-to-all | bytes 2228224 | tf_op jit(solution)/shard_map/all_to_all | solution.py:27
  118.3 0.2 reduce_sum.32
  118.5 0.1 broadcast_in_dim.8
  118.6 45.0 %all_to_all.43.source_ref = bf16[32,136,128]{2,1,0:T(8,128)(2,1)S(1)} all-to-all(bf16[32,136,128]{2,1,0:T(8,128)(2,1)S(1)} %broadcast_in_dim.8), channel_id=1, replica_groups=mesh['z'=8,'yh'=4,'core'=2,'x'=4,'yl'=2] {'z','yh'}, dimensions={0} | all-to-all | bytes 2228224 | tf_op jit(solution)/shard_map/all_to_all | solution.py:27
  163.6 2.7 %collective-permute-start.1 = (bf16[32,136,128]{2,1,0:T(8,128)(2,1)S(1)}, bf16[32,136,128]{2,1,0:T(8,128)(2,1)S(1)}, u32[]{:S(2)}, u32[]{:S(2)}) collective-permute-start(bf16[32,136,128]{2,1,0:T(8,128)(2,1)S(1)} %all_to_all.43.source_ref), channel_id=1, source_target_pairs={{0,8},{8,0},{1,9},{9,1},{2,10},{10,2},{3,11},{11,3},{4,12},{12,4},... | collective-permute-start | bytes 3342344 | tf_op jit(solution)/shard_map/ppermute | solution.py:412
  166.4 1.1 assemble.2
  167.5 1.3 collective-permute-done.1.source_ref
  168.7 1.1 assemble.3
  (2 shorter events, 0.0 us)
Async XLA Ops:
  0.6 1.0 copy-start.1
  1.7 0.7 copy-start.3
  43.3 11.3 %copy-start = (bf16[512,1568]{0,1:T(8,128)(2,1)S(1)}, bf16[512,1568]{0,1:T(8,128)(2,1)}, u32[]{:S(2)}) copy-start(bf16[512,1568]{0,1:T(8,128)(2,1)} %param.4) | copy-start | bytes 4816900
  43.3 11.3 %copy-start.2 = (bf16[512,512]{1,0:T(8,128)(2,1)S(1)}, bf16[512,512]{1,0:T(8,128)(2,1)}, u32[]{:S(2)}) copy-start(bf16[512,512]{1,0:T(8,128)(2,1)} %class_ref.5) | copy-start | bytes 1572868
  55.5 12.4 %collective-permute-start = (bf16[32,136,128]{2,1,0:T(8,128)(2,1)S(1)}, bf16[32,136,128]{2,1,0:T(8,128)(2,1)S(1)}, u32[]{:S(2)}, u32[]{:S(2)}) collective-permute-start(bf16[32,136,128]{2,1,0:T(8,128)(2,1)S(1)} %parts.3), channel_id=1, source_target_pairs={{0,8},{8,0},{1,9},{9,1},{2,10},{10,2},{3,11},{11,3},{4,12},{12,4},... | collective-permute-start | bytes 3342344 | tf_op jit(solution)/shard_map/ppermute | solution.py:407
  163.6 5.1 %collective-permute-start.1 = (bf16[32,136,128]{2,1,0:T(8,128)(2,1)S(1)}, bf16[32,136,128]{2,1,0:T(8,128)(2,1)S(1)}, u32[]{:S(2)}, u32[]{:S(2)}) collective-permute-start(bf16[32,136,128]{2,1,0:T(8,128)(2,1)S(1)} %all_to_all.43.source_ref), channel_id=1, source_target_pairs={{0,8},{8,0},{1,9},{9,1},{2,10},{10,2},{3,11},{11,3},{4,12},{12,4},... | collective-permute-start | bytes 3342344 | tf_op jit(solution)/shard_map/ppermute | solution.py:412

commit v4 on v3

--- a/solution.py
+++ b/solution.py
@@ -15,7 +15,7 @@
 EPSILON = 1e-06
 
 CLS = ("x", "yl")
-CHIPS = ("z", "yh")
+CHIPS = ("zh", "yh")
 LANES = 128
 CHUNKS = 3
 LIMIT = 24 << 20
@@ -65,8 +65,13 @@
     return 1 - core if other else core
 
 
+def parity_of(place_ref, other):
+    odd = lax.rem(lax.div(place_ref[0], 2), 2)
+    return 1 - odd if other else odd
+
+
 def first_of(place_ref, classes):
-    return lax.div(place_ref[0], 2) * classes
+    return lax.div(place_ref[0], 4) * classes
 
 
 def call(kernel, name, operands, results, **options):
@@ -235,148 +240,147 @@
     )[0]
 
 
+def block_sizes(inputs, width, blocks):
+    rows = inputs // (2 * blocks * 8) * 8
+    return rows, width // LANES, 2 * blocks * rows
+
+
 def parts_kernel(
     other, place_ref, features_ref, grads_ref, units_ref, others_ref, class_ref, out_ref
 ):
-    chips = out_ref.shape[0]
+    blocks = out_ref.shape[0]
+    some = blocks // 2
     classes, width = class_ref.shape
-    groups = width // LANES
     inputs = features_ref.shape[0]
-    rows = inputs // (2 * chips * 8) * 8
-    main = 2 * chips * rows
+    rows, groups, main = block_sizes(inputs, width, blocks)
+    base = groups * rows
     half = half_of(place_ref, other)
     grads = grads_ref[:, :width]
-    some = chips // 2
-    for at in range(0, chips, some):
-        first = pl.multiple_of(half * (chips * rows) + at * rows, LANES)
-        part = jnp.dot(
-            features_ref[pl.ds(first, some * rows), :], grads, preferred_element_type=jnp.float32
-        )
-        part = part.astype(out_ref.dtype).reshape(some, rows, width)
-        for group in range(groups):
-            out_ref[at : at + some, group * rows : (group + 1) * rows, :] = part[
-                :, :, group * LANES : (group + 1) * LANES
-            ]
-
+    scales = grads_ref[:, width:].astype(jnp.float32)
+    pull_scale, target_scale = unpacked_column(scales, 0), unpacked_column(scales, 1)
     each = (inputs - main) // 2
     over = jnp.dot(
         features_ref[pl.ds(pl.multiple_of(main + half * each, each), each), :],
         grads,
         preferred_element_type=jnp.float32,
     ).astype(out_ref.dtype)
-    base = groups * rows
-    used = each // 8 * groups
-    for tile in range(used):
-        row, group = tile // groups * 8, tile % groups * LANES
-        out_ref[tile, base + groups * 8 :, :] = over[row : row + 8, group : group + LANES]
-    out_ref[used:, base + groups * 8 :, :] = jnp.zeros(
-        (chips - used, 8, LANES), out_ref.dtype
-    )
-
-    scales = grads_ref[:, width:].astype(jnp.float32)
-    pull_scale, target_scale = unpacked_column(scales, 0), unpacked_column(scales, 1)
-    count = classes // 2
-    first = pl.multiple_of(half * count, LANES)
-    others = others_ref[:, pl.ds(first, count)]
-    cos_grad = jnp.where(others < 0.0, -target_scale, others * pull_scale)
-    part = across(cos_grad.astype(jnp.bfloat16), units_ref[...])
-    class_f = class_ref[pl.ds(first, count), :].astype(jnp.float32)
-    class_norm = row_norm(class_f)
-    class_unit = class_f / class_norm
-    part = (part - class_unit * jnp.sum(class_unit * part, axis=1, keepdims=True)) / class_norm
-    part = part.astype(out_ref.dtype).reshape(chips, 8, width)
-    for group in range(groups):
-        out_ref[:, base + group * 8 : base + (group + 1) * 8, :] = part[
-            :, :, group * LANES : (group + 1) * LANES
-        ]
-
-
-def parts(other, place, dtype, chips, features, grads, units, others, class_weight):
-    groups = class_weight.shape[1] // LANES
-    rows = features.shape[0] // (2 * chips * 8) * 8
-    height = groups * rows + groups * 8 + 8
+    count = classes // 4
+
+    for at, parity in ((0, parity_of(place_ref, True)), (some, parity_of(place_ref, False))):
+        here = slice(at, at + some)
+        first = pl.multiple_of((2 * half + parity) * (some * rows), LANES)
+        part = jnp.dot(
+            features_ref[pl.ds(first, some * rows), :], grads, preferred_element_type=jnp.float32
+        )
+        part = part.astype(out_ref.dtype).reshape(some, rows, width)
+        for group in range(groups):
+            out_ref[here, group * rows : (group + 1) * rows, :] = part[
+                :, :, group * LANES : (group + 1) * LANES
+            ]
+
+        first = pl.multiple_of((2 * half + parity) * count, LANES)
+        others = others_ref[:, pl.ds(first, count)]
+        cos_grad = jnp.where(others < 0.0, -target_scale, others * pull_scale)
+        part = across(cos_grad.astype(jnp.bfloat16), units_ref[...])
+        class_f = class_ref[pl.ds(first, count), :].astype(jnp.float32)
+        class_norm = row_norm(class_f)
+        class_unit = class_f / class_norm
+        part = part - class_unit * jnp.sum(class_unit * part, axis=1, keepdims=True)
+        part = (part / class_norm).astype(out_ref.dtype).reshape(some, 8, width)
+        for group in range(groups):
+            out_ref[here, base + group * 8 : base + (group + 1) * 8, :] = part[
+                :, :, group * LANES : (group + 1) * LANES
+            ]
+
+        strip = jnp.where(parity == 0, over[:8], over[8:])
+        for group in range(groups):
+            out_ref[at + group, base + groups * 8 :, :] = strip[
+                :, group * LANES : (group + 1) * LANES
+            ]
+        out_ref[at + groups : at + some, base + groups * 8 :, :] = jnp.zeros(
+            (some - groups, 8, LANES), out_ref.dtype
+        )
+
+
+def parts(other, place, dtype, blocks, features, grads, units, others, class_weight):
+    rows, groups, _ = block_sizes(features.shape[0], class_weight.shape[1], blocks)
     return call(
         functools.partial(parts_kernel, other),
         "parts",
         (place, features, grads, units, others, class_weight),
-        [((chips, height, LANES), dtype)],
+        [((blocks, groups * (rows + 8) + 8, LANES), dtype)],
     )[0]
 
 
-def assemble_kernel(other, place_ref, source_ref, *refs):
-    fc_ref, class_ref, fc_half, fc_over, class_half, sems = refs[-6:]
-    chips = source_ref.shape[0]
+def assemble_kernel(pieces, blocks, place_ref, *refs):
+    sources = refs[: len(pieces)]
+    fc_ref, class_ref, fc_rows, class_rows, over_rows, sems = refs[-6:]
     inputs, width = fc_ref.shape
-    groups = width // LANES
-    rows = inputs // (2 * chips * 8) * 8
-    main = 2 * chips * rows
+    rows, groups, main = block_sizes(inputs, width, blocks)
     each = (inputs - main) // 2
     base = groups * rows
-    count = class_ref.shape[0] // 2
-    half = half_of(place_ref, other)
-
-    for group in range(groups):
-        lanes = slice(group * LANES, (group + 1) * LANES)
-        block = source_ref[:, base + group * 8 : base + (group + 1) * 8, :].astype(jnp.float32)
-        class_half[:, lanes] = block.reshape(count, LANES).astype(jnp.bfloat16)
-        for strip in range(each // 8):
-            fc_over[strip * 8 : strip * 8 + 8, lanes] = source_ref[
-                strip * groups + group, base + groups * 8 :, :
-            ]
-    copies = [
-        pltpu.make_async_copy(
-            class_half, class_ref.at[pl.ds(pl.multiple_of(half * count, count), count), :], sems.at[0]
-        ),
-        pltpu.make_async_copy(
-            fc_over, fc_ref.at[pl.ds(pl.multiple_of(main + half * each, each), each), :], sems.at[1]
-        ),
-    ]
-    for copy in copies:
-        copy.start()
-    some = chips // 4
-    for at in range(0, chips, some):
+    some = blocks // 2
+    copies = []
+    done = 0
+
+    def send(source, target, at, size):
+        copies.append(
+            pltpu.make_async_copy(
+                source, target.at[pl.ds(pl.multiple_of(at, 8), size), :], sems.at[len(copies)]
+            )
+        )
+        copies[-1].start()
+
+    for number, (piece, source) in enumerate(zip(pieces, sources)):
+        other_half, other_parity, start = piece
+        half, parity = half_of(place_ref, other_half), parity_of(place_ref, other_parity)
+        count = source.shape[0]
+        block = (2 * half + parity) * some + start
+        fc_here = slice(done * rows, (done + count) * rows)
+        class_here = slice(done * 8, (done + count) * 8)
         for group in range(groups):
             lanes = slice(group * LANES, (group + 1) * LANES)
-            block = source_ref[at : at + some, group * rows : (group + 1) * rows, :]
-            block = block.astype(jnp.float32).reshape(some * rows, LANES)
-            fc_half[at * rows : (at + some) * rows, lanes] = block.astype(jnp.bfloat16)
-        first = pl.multiple_of(half * (chips * rows) + at * rows, some * rows)
-        copies.append(
-            pltpu.make_async_copy(
-                fc_half.at[at * rows : (at + some) * rows, :],
-                fc_ref.at[pl.ds(first, some * rows), :],
-                sems.at[2 + at // some],
-            )
-        )
-        copies[-1].start()
+            values = source[:, group * rows : (group + 1) * rows, :].astype(jnp.float32)
+            fc_rows[fc_here, lanes] = values.reshape(count * rows, LANES).astype(jnp.bfloat16)
+            values = source[:, base + group * 8 : base + (group + 1) * 8, :].astype(jnp.float32)
+            class_rows[class_here, lanes] = values.reshape(count * 8, LANES).astype(jnp.bfloat16)
+            if start == 0:
+                over_rows[number, :, lanes] = source[group, base + groups * 8 :, :]
+        send(fc_rows.at[fc_here, :], fc_ref, block * rows, count * rows)
+        send(class_rows.at[class_here, :], class_ref, block * 8, count * 8)
+        if start == 0:
+            send(over_rows.at[number], fc_ref, main + half * each + parity * 8, 8)
+        done += count
     for copy in copies:
         copy.wait()
 
 
-def assemble(other, place, source, inputs, classes, width, *into):
-    chips = source.shape[0]
-    groups = width // LANES
-    rows = inputs // (2 * chips * 8) * 8
-    each = (inputs - 2 * chips * rows) // 2
+def assemble(place, blocks, sizes, pieces, into):
+    inputs, classes, width = sizes
+    rows, _, _ = block_sizes(inputs, width, blocks)
+    total = sum(source.shape[0] for source in pieces.values())
     anywhere = pl.BlockSpec(memory_space=pltpu.HBM)
     return pl.pallas_call(
-        functools.partial(assemble_kernel, other),
-        in_specs=[SMEM, VMEM] + [anywhere] * len(into),
+        functools.partial(assemble_kernel, tuple(pieces), blocks),
+        in_specs=[SMEM] + [VMEM] * len(pieces) + [anywhere] * len(into),
         out_specs=[anywhere, anywhere],
         out_shape=[
             jax.ShapeDtypeStruct((inputs, width), jnp.bfloat16),
             jax.ShapeDtypeStruct((classes, width), jnp.bfloat16),
         ],
         scratch_shapes=[
-            pltpu.VMEM((chips * rows, width), jnp.bfloat16),
-            pltpu.VMEM((each, width), jnp.bfloat16),
-            pltpu.VMEM((classes // 2, width), jnp.bfloat16),
-            pltpu.SemaphoreType.DMA((6,)),
+            pltpu.VMEM((total * rows, width), jnp.bfloat16),
+            pltpu.VMEM((total * 8, width), jnp.bfloat16),
+            pltpu.VMEM((len(pieces), 8, width), jnp.bfloat16),
+            pltpu.SemaphoreType.DMA((3 * len(pieces),)),
         ],
-        input_output_aliases={2 + at: at for at in range(len(into))},
+        input_output_aliases={1 + len(pieces) + at: at for at in range(len(into))},
+        cost_estimate=pl.CostEstimate(
+            flops=0, transcendentals=0, bytes_accessed=total * (rows + 8) * width * 8
+        ),
         compiler_params=pltpu.CompilerParams(vmem_limit_bytes=LIMIT),
         name="assemble",
-    )(place, placed(source), *into)
+    )(place, *[placed(source) for source in pieces.values()], *into)
 
 
 def shards(features, fc_weight, class_weight, labels):
@@ -385,8 +389,10 @@
     classes, width = class_weight.shape
     n_cls = lax.axis_size(CLS)
     chips = lax.axis_size(CHIPS)
-    loss_weight = 1.0 / math.sqrt(faces * chips * lax.axis_size("core"))
-    place = (lax.axis_index(CLS) * 2 + lax.axis_index("core")).reshape(1)
+    blocks = 2 * chips
+    loss_weight = 1.0 / math.sqrt(faces * blocks * lax.axis_size("core"))
+    place = (lax.axis_index(CLS) * 2 + lax.axis_index("zl")) * 2 + lax.axis_index("core")
+    place = place.reshape(1)
     labels = labels.reshape(1, faces)
 
     sent, class_unit = embed(place, features, fc_weight, class_weight, labels)
@@ -403,21 +409,44 @@
     grads = exchange(sent, CLS).reshape(faces, width + LANES)
 
     swap = [(0, 1), (1, 0)]
-    operands = (features, grads, units, others, class_weight)
-    theirs = lax.ppermute(parts(True, place, jnp.bfloat16, chips, *operands), "core", swap)
-    mine = parts(False, place, jnp.float32, chips, *operands)
-    mine = (mine + theirs.astype(jnp.float32)).astype(jnp.bfloat16)
+    length = 2 * lax.axis_size("zh")
+    pairs = [[(z, z ^ 1) for z in range(length)]]
+    pairs.append([(z, (z + 2 * (z % 2) - 1) % length) for z in range(length)])
+
+    def neighbours(values):
+        parts_of = (values[: chips // 2], values[chips // 2 :])
+        return [lax.ppermute(part, ("zh", "zl"), pair) for part, pair in zip(parts_of, pairs)]
+
+    operands = (blocks, features, grads, units, others, class_weight)
+    theirs = lax.ppermute(parts(True, place, jnp.bfloat16, *operands), "core", swap)
+    total = parts(False, place, jnp.float32, *operands) + theirs.astype(jnp.float32)
+    got = jnp.concatenate(neighbours(total[:chips].astype(jnp.bfloat16)), axis=0)
+    mine = (total[chips:] + got.astype(jnp.float32)).astype(jnp.bfloat16)
     done = jnp.sum(exchange(mine, CHIPS).astype(jnp.float32), axis=0).astype(jnp.bfloat16)
+
+    sizes = (inputs, classes, width)
     mine = exchange(jnp.broadcast_to(done, (chips,) + done.shape), CHIPS)
-    theirs = lax.ppermute(mine, "core", swap)
-    sizes = (inputs, classes, width)
-    written = assemble(False, place, mine, *sizes)
-    return tuple(assemble(True, place, theirs, *sizes, *written))
+    left, right = neighbours(mine)
+    across_own = lax.ppermute(mine, "core", swap)
+    across_next = lax.ppermute(jnp.concatenate([left, right], axis=0), "core", swap)
+    written = assemble(place, blocks, sizes, {(False, False, 0): mine}, ())
+    written = assemble(
+        place,
+        blocks,
+        sizes,
+        {
+            (False, True, 0): left,
+            (False, True, chips // 2): right,
+            (True, False, 0): across_own,
+        },
+        written,
+    )
+    return tuple(assemble(place, blocks, sizes, {(True, True, 0): across_next}, written))
 
 
 def solution(mesh):
-    fine = Mesh(mesh.devices.reshape(8, 4, 2, 4, 2), ("z", "yh", "core", "x", "yl"))
-    dp = ("z", "yh", "core")
+    fine = Mesh(mesh.devices.reshape(4, 2, 4, 2, 4, 2), ("zh", "zl", "yh", "core", "x", "yl"))
+    dp = ("zh", "zl", "yh", "core")
     specs = (P(dp, CLS), P(CLS, None), P(CLS, None), P(dp))
     return jax.shard_map(
         shards,

time: 170 us -> 168 us (0.988)
  the two profiles are of different devices: /device:TPU:5 before, /device:TPU:1 now
where the time goes in v4:
time: 168 us; the launch traced here: 167 us
  blocking collectives  106 us (63%)
  starting transfers between devices  35.4 us (21%)
  waiting for transfers between devices  12.6 us (8%)
  Pallas kernels  9.53 us (6%)
  local copies, waits for them, and re-layouts  1.92 us (1%)
    all_to_all x6, blocking collectives, exchange(): return lax.all_to_all(blocks, axes, 0, 0, tiled=True)  106 us
    ppermute x4, starting transfers between devices, neighbours(): lax.ppermute(part, ('zh', 'zl'), pair)  18.3 us
    ppermute x4, waiting for transfers between devices, neighbours(): lax.ppermute(part, ('zh', 'zl'), pair)  11.2 us
    ppermute x1, starting transfers between devices, shards(): lax.ppermute(parts(True, place, jnp.bfloat16, *operands), 'core', swap)  10 us
    pallas_call x4, Pallas kernels, call(): pl.pallas_call(kernel, in_specs=specs, out_specs=[VMEM] * len(results), o...  3.85 us
    ppermute x1, starting transfers between devices, shards(): lax.ppermute(jnp.concatenate([left, right], axis=0), 'core', swap)  3.84 us
  transfers between devices with their start and end apart: 7, of which 4 were waited for; matrix products, arithmetic and copies ran while one was open for 0% of the time, Pallas kernels for 2%

profile of v4, /device:TPU:1, one launch (start us, length us, event | category | flops | bytes accessed | tf_op | source)
XLA Modules:
  0.0 167.2 jit_solution(6926241308918053471)
XLA Ops:
  0.7 1.0 copy-done.1
  1.7 0.7 copy-done.3
  2.4 2.8 %embed.1 = (bf16[512,1024]{1,0:T(8,128)(2,1)S(1)}, bf16[512,512]{1,0:T(8,128)(2,1)S(1)}) custom-call(s32[1]{0:T(128)} %bitcast.place_ref, bf16[1568,512]{1,0:T(8,128)(2,1)} %bitcast.7, bf16[1568,512]{1,0:T(8,128)(2,1)} %fc_ref.1, bf16[512,512]{1,0:T(8,128)(2,1)S(1)} %copy-done.1, s32[1,512]{1,0:T(1,128)S(1)} %bitcast.17), custom_call_target="tpu_custom_call" | custom-call | tf_op jit(solution)/shard_map/embed/pallas_call | solution.py:147
  5.1 17.7 %all_to_all.38 = bf16[8,64,1024]{2,1,0:T(8,128)(2,1)S(1)} all-to-all(bf16[8,64,1024]{2,1,0:T(8,128)(2,1)S(1)} %bitcast.15), channel_id=1, replica_groups=mesh['zh'=4,'zl'=2,'yh'=4,'core'=2,'x'=4,'yl'=2] {'x','yl'}, dimensions={0} | all-to-all | bytes 2097152 | tf_op jit(solution)/shard_map/all_to_all | solution.py:27
  22.8 0.2 convert_reduce_fusion
  23.0 0.1 fusion.4
  23.1 0.1 divide_convert_fusion
  23.3 10.3 %all_to_all.39 = bf16[8,64,512]{2,1,0:T(8,128)(2,1)S(1)} all-to-all(bf16[8,64,512]{2,1,0:T(8,128)(2,1)S(1)} %broadcast_in_dim.7), channel_id=1, replica_groups=mesh['zh'=4,'zl'=2,'yh'=4,'core'=2,'x'=4,'yl'=2] {'x','yl'}, dimensions={0} | all-to-all | bytes 1048576 | tf_op jit(solution)/shard_map/all_to_all | solution.py:27
  33.6 1.6 cosines.1
  35.2 10.8 %all_to_all.40.pulls_ref = bf16[8,64,640]{2,1,0:T(8,128)(2,1)S(1)} all-to-all(bf16[8,64,640]{2,1,0:T(8,128)(2,1)S(1)} %bitcast.16), channel_id=1, replica_groups=mesh['zh'=4,'zl'=2,'yh'=4,'core'=2,'x'=4,'yl'=2] {'x','yl'}, dimensions={0} | all-to-all | bytes 1310720 | tf_op jit(solution)/shard_map/all_to_all | solution.py:27
  45.9 0.4 raw_grads.1
  46.3 10.9 %all_to_all.41 = bf16[8,64,640]{2,1,0:T(8,128)(2,1)S(1)} all-to-all(bf16[8,64,640]{2,1,0:T(8,128)(2,1)S(1)} %raw_grads.1), channel_id=1, replica_groups=mesh['zh'=4,'zl'=2,'yh'=4,'core'=2,'x'=4,'yl'=2] {'x','yl'}, dimensions={0} | all-to-all | bytes 1310720 | tf_op jit(solution)/shard_map/all_to_all | solution.py:27
  57.2 0.9 parts.3
  58.1 10.0 %collective-permute-start = (bf16[32,136,128]{2,1,0:T(8,128)(2,1)S(1)}, bf16[32,136,128]{2,1,0:T(8,128)(2,1)S(1)}, u32[]{:S(2)}, u32[]{:S(2)}) collective-permute-start(bf16[32,136,128]{2,1,0:T(8,128)(2,1)S(1)} %parts.3), channel_id=1, source_target_pairs={{0,8},{8,0},{1,9},{9,1},{2,10},{10,2},{3,11},{11,3},{4,12},{12,4},... | collective-permute-start | bytes 3342344 | tf_op jit(solution)/shard_map/ppermute | solution.py:421
  68.1 0.9 parts.2
  69.1 1.4 collective-permute-done
  70.5 0.3 fusion.1
  70.8 4.6 %collective-permute-start.1 = (bf16[8,136,128]{2,1,0:T(8,128)(2,1)S(1)}, bf16[8,136,128]{2,1,0:T(8,128)(2,1)S(1)}, u32[]{:S(2)}, u32[]{:S(2)}) collective-permute-start(bf16[8,136,128]{2,1,0:T(8,128)(2,1)S(1)} %get-tuple-element.20), channel_id=1, source_target_pairs={{0,64},{64,0},{128,192},{192,128},{256,320},{320,256},{384,448},{4... | collective-permute-start | bytes 835592 | tf_op jit(solution)/shard_map/ppermute | solution.py:418
  75.5 8.8 %collective-permute-start.2 = (bf16[8,136,128]{2,1,0:T(8,128)(2,1)S(1)}, bf16[8,136,128]{2,1,0:T(8,128)(2,1)S(1)}, u32[]{:S(2)}, u32[]{:S(2)}) collective-permute-start(bf16[8,136,128]{2,1,0:T(8,128)(2,1)S(1)} %get-tuple-element.21), channel_id=1, source_target_pairs={{0,448},{64,128},{128,64},{192,256},{256,192},{320,384},{384,320},... | collective-permute-start | bytes 835592 | tf_op jit(solution)/shard_map/ppermute | solution.py:418
  84.3 6.4 %collective-permute-done.2 = bf16[8,136,128]{2,1,0:T(8,128)(2,1)S(1)} collective-permute-done((bf16[8,136,128]{2,1,0:T(8,128)(2,1)S(1)}, bf16[8,136,128]{2,1,0:T(8,128)(2,1)S(1)}, u32[]{:S(2)}, u32[]{:S(2)}) %collective-permute-start.2) | collective-permute-done | bytes 278560 | tf_op jit(solution)/shard_map/ppermute | solution.py:418
  90.7 0.1 fusion
  90.9 29.2 %all_to_all.42 = bf16[16,136,128]{2,1,0:T(8,128)(2,1)S(1)} all-to-all(bf16[16,136,128]{2,1,0:T(8,128)(2,1)S(1)} %fusion), channel_id=1, replica_groups=mesh['zh'=4,'zl'=2,'yh'=4,'core'=2,'x'=4,'yl'=2] {'zh','yh'}, dimensions={0} | all-to-all | bytes 1114112 | tf_op jit(solution)/shard_map/all_to_all | solution.py:27
  120.2 27.2 %all_to_all.43.refs_0_ = bf16[16,136,128]{2,1,0:T(8,128)(2,1)S(1)} all-to-all(bf16[16,136,128]{2,1,0:T(8,128)(2,1)S(1)} %broadcast_in_dim.8), channel_id=1, replica_groups=mesh['zh'=4,'zl'=2,'yh'=4,'core'=2,'x'=4,'yl'=2] {'zh','yh'}, dimensions={0} | all-to-all | bytes 1114112 | tf_op jit(solution)/shard_map/all_to_all | solution.py:27
  147.4 2.7 %collective-permute-start.3 = (bf16[8,136,128]{2,1,0:T(8,128)(2,1)S(1)}, bf16[8,136,128]{2,1,0:T(8,128)(2,1)S(1)}, u32[]{:S(2)}, u32[]{:S(2)}) collective-permute-start(bf16[8,136,128]{2,1,0:T(8,128)(2,1)S(1)} %get-tuple-element.22), channel_id=1, source_target_pairs={{0,64},{64,0},{128,192},{192,128},{256,320},{320,256},{384,448},{4... | collective-permute-start | bytes 835592 | tf_op jit(solution)/shard_map/ppermute | solution.py:418
  150.1 2.2 %collective-permute-start.4 = (bf16[8,136,128]{2,1,0:T(8,128)(2,1)S(1)}, bf16[8,136,128]{2,1,0:T(8,128)(2,1)S(1)}, u32[]{:S(2)}, u32[]{:S(2)}) collective-permute-start(bf16[8,136,128]{2,1,0:T(8,128)(2,1)S(1)} %get-tuple-element.23), channel_id=1, source_target_pairs={{0,448},{64,128},{128,64},{192,256},{256,192},{320,384},{384,320},... | collective-permute-start | bytes 835592 | tf_op jit(solution)/shard_map/ppermute | solution.py:418
  152.3 3.3 %collective-permute-start.6 = (bf16[16,136,128]{2,1,0:T(8,128)(2,1)S(1)}, bf16[16,136,128]{2,1,0:T(8,128)(2,1)S(1)}, u32[]{:S(2)}, u32[]{:S(2)}) collective-permute-start(bf16[16,136,128]{2,1,0:T(8,128)(2,1)S(1)} %all_to_all.43.refs_0_), channel_id=1, source_target_pairs={{0,8},{8,0},{1,9},{9,1},{2,10},{10,2},{3,11},{11,3},{4,12},{12,4},... | collective-permute-start | bytes 1671176 | tf_op jit(solution)/shard_map/ppermute | solution.py:430
  155.6 0.7 collective-permute-done.3.refs_0_
  156.3 4.1 %collective-permute-done.4.refs_1_ = bf16[8,136,128]{2,1,0:T(8,128)(2,1)S(1)} collective-permute-done((bf16[8,136,128]{2,1,0:T(8,128)(2,1)S(1)}, bf16[8,136,128]{2,1,0:T(8,128)(2,1)S(1)}, u32[]{:S(2)}, u32[]{:S(2)}) %collective-permute-start.4) | collective-permute-done | bytes 278560 | tf_op jit(solution)/shard_map/ppermute | solution.py:418
  160.4 3.8 %collective-permute-start.5 = (bf16[16,136,128]{2,1,0:T(8,128)(2,1)S(1)}, bf16[16,136,128]{2,1,0:T(8,128)(2,1)S(1)}, u32[]{:S(2)}, u32[]{:S(2)}) collective-permute-start(bf16[16,136,128]{2,1,0:T(8,128)(2,1)S(1)} %pad_maximum_fusion), channel_id=1, source_target_pairs={{0,8},{8,0},{1,9},{9,1},{2,10},{10,2},{3,11},{11,3},{4,12},{12,4},... | collective-permute-start | bytes 1671176 | tf_op jit(solution)/shard_map/ppermute | solution.py:431
  164.3 0.9 assemble.3
  165.2 1.1 assemble.4
  166.3 0.9 assemble.5
  (16 shorter events, 0.4 us)
Async XLA Ops:
  0.6 1.0 copy-start.1
  1.7 0.7 copy-start.3
  45.9 11.3 %copy-start = (bf16[512,1568]{0,1:T(8,128)(2,1)S(1)}, bf16[512,1568]{0,1:T(8,128)(2,1)}, u32[]{:S(2)}) copy-start(bf16[512,1568]{0,1:T(8,128)(2,1)} %param.4) | copy-start | bytes 4816900
  45.9 11.3 %copy-start.2 = (bf16[512,512]{1,0:T(8,128)(2,1)S(1)}, bf16[512,512]{1,0:T(8,128)(2,1)}, u32[]{:S(2)}) copy-start(bf16[512,512]{1,0:T(8,128)(2,1)} %class_ref.5) | copy-start | bytes 1572868
  58.1 12.4 %collective-permute-start = (bf16[32,136,128]{2,1,0:T(8,128)(2,1)S(1)}, bf16[32,136,128]{2,1,0:T(8,128)(2,1)S(1)}, u32[]{:S(2)}, u32[]{:S(2)}) collective-permute-start(bf16[32,136,128]{2,1,0:T(8,128)(2,1)S(1)} %parts.3), channel_id=1, source_target_pairs={{0,8},{8,0},{1,9},{9,1},{2,10},{10,2},{3,11},{11,3},{4,12},{12,4},... | collective-permute-start | bytes 3342344 | tf_op jit(solution)/shard_map/ppermute | solution.py:421
  70.8 13.5 %collective-permute-start.1 = (bf16[8,136,128]{2,1,0:T(8,128)(2,1)S(1)}, bf16[8,136,128]{2,1,0:T(8,128)(2,1)S(1)}, u32[]{:S(2)}, u32[]{:S(2)}) collective-permute-start(bf16[8,136,128]{2,1,0:T(8,128)(2,1)S(1)} %get-tuple-element.20), channel_id=1, source_target_pairs={{0,64},{64,0},{128,192},{192,128},{256,320},{320,256},{384,448},{4... | collective-permute-start | bytes 835592 | tf_op jit(solution)/shard_map/ppermute | solution.py:418
  75.5 15.2 %collective-permute-start.2 = (bf16[8,136,128]{2,1,0:T(8,128)(2,1)S(1)}, bf16[8,136,128]{2,1,0:T(8,128)(2,1)S(1)}, u32[]{:S(2)}, u32[]{:S(2)}) collective-permute-start(bf16[8,136,128]{2,1,0:T(8,128)(2,1)S(1)} %get-tuple-element.21), channel_id=1, source_target_pairs={{0,448},{64,128},{128,64},{192,256},{256,192},{320,384},{384,320},... | collective-permute-start | bytes 835592 | tf_op jit(solution)/shard_map/ppermute | solution.py:418
  147.4 8.8 %collective-permute-start.3 = (bf16[8,136,128]{2,1,0:T(8,128)(2,1)S(1)}, bf16[8,136,128]{2,1,0:T(8,128)(2,1)S(1)}, u32[]{:S(2)}, u32[]{:S(2)}) collective-permute-start(bf16[8,136,128]{2,1,0:T(8,128)(2,1)S(1)} %get-tuple-element.22), channel_id=1, source_target_pairs={{0,64},{64,0},{128,192},{192,128},{256,320},{320,256},{384,448},{4... | collective-permute-start | bytes 835592 | tf_op jit(solution)/shard_map/ppermute | solution.py:418
  150.1 10.2 %collective-permute-start.4 = (bf16[8,136,128]{2,1,0:T(8,128)(2,1)S(1)}, bf16[8,136,128]{2,1,0:T(8,128)(2,1)S(1)}, u32[]{:S(2)}, u32[]{:S(2)}) collective-permute-start(bf16[8,136,128]{2,1,0:T(8,128)(2,1)S(1)} %get-tuple-element.23), channel_id=1, source_target_pairs={{0,448},{64,128},{128,64},{192,256},{256,192},{320,384},{384,320},... | collective-permute-start | bytes 835592 | tf_op jit(solution)/shard_map/ppermute | solution.py:418
  152.3 12.9 %collective-permute-start.6 = (bf16[16,136,128]{2,1,0:T(8,128)(2,1)S(1)}, bf16[16,136,128]{2,1,0:T(8,128)(2,1)S(1)}, u32[]{:S(2)}, u32[]{:S(2)}) collective-permute-start(bf16[16,136,128]{2,1,0:T(8,128)(2,1)S(1)} %all_to_all.43.refs_0_), channel_id=1, source_target_pairs={{0,8},{8,0},{1,9},{9,1},{2,10},{10,2},{3,11},{11,3},{4,12},{12,4},... | collective-permute-start | bytes 1671176 | tf_op jit(solution)/shard_map/ppermute | solution.py:430
  160.4 5.9 %collective-permute-start.5 = (bf16[16,136,128]{2,1,0:T(8,128)(2,1)S(1)}, bf16[16,136,128]{2,1,0:T(8,128)(2,1)S(1)}, u32[]{:S(2)}, u32[]{:S(2)}) collective-permute-start(bf16[16,136,128]{2,1,0:T(8,128)(2,1)S(1)} %pad_maximum_fusion), channel_id=1, source_target_pairs={{0,8},{8,0},{1,9},{9,1},{2,10},{10,2},{3,11},{11,3},{4,12},{12,4},... | collective-permute-start | bytes 1671176 | tf_op jit(solution)/shard_map/ppermute | solution.py:431

commit v5 on v4

--- a/solution.py
+++ b/solution.py
@@ -102,34 +102,40 @@
 
 def embed_kernel(
     place_ref, features_ref, fc_ref, class_ref, labels_ref, sent_ref, unit_ref,
-    left_ref, right_ref, total_ref, left_sem, right_sem
+    left_ref, right_ref, total_ref, weight_ref, row_ref, sems
 ):
     width = fc_ref.shape[1]
     inputs, faces = features_ref.shape
     classes = class_ref.shape[0]
     ends = [inputs * at // CHUNKS // LANES * LANES for at in range(CHUNKS)] + [inputs]
-    copies = []
+    copies = [
+        pltpu.make_async_copy(labels_ref, row_ref, sems.at[0]),
+        pltpu.make_async_copy(class_ref, weight_ref, sems.at[1]),
+    ]
     for at in range(CHUNKS):
         rows = pl.ds(ends[at], ends[at + 1] - ends[at])
-        pair = (
-            pltpu.make_async_copy(features_ref.at[rows, :], left_ref.at[rows, :], left_sem.at[at]),
-            pltpu.make_async_copy(fc_ref.at[rows, :], right_ref.at[rows, :], right_sem.at[at]),
-        )
-        for copy in pair:
-            copy.start()
-        copies.append(pair)
-
-    class_f = class_ref[...].astype(jnp.float32)
-    unit_ref[...] = (class_f / row_norm(class_f)).astype(jnp.bfloat16)
-    labels = spread_labels(labels_ref[...])
+        for source, target in ((features_ref, left_ref), (fc_ref, right_ref)):
+            copies.append(
+                pltpu.make_async_copy(
+                    source.at[rows, :], target.at[rows, :], sems.at[len(copies)]
+                )
+            )
+    for copy in copies:
+        copy.start()
+
+    copies[0].wait()
+    labels = spread_labels(row_ref[...])
     chosen = target_mask(first_of(place_ref, classes), labels, faces, classes)
     chosen = jnp.where(chosen, 1.0, 0.0).astype(jnp.bfloat16)
+    copies[1].wait()
+    class_f = weight_ref[...].astype(jnp.float32)
+    unit_ref[...] = (class_f / row_norm(class_f)).astype(jnp.bfloat16)
     target_part = jnp.dot(chosen, unit_ref[...], preferred_element_type=jnp.float32)
     sent_ref[:, width:] = target_part.astype(jnp.bfloat16)
 
     for at in range(CHUNKS):
-        for copy in copies[at]:
-            copy.wait()
+        copies[2 + 2 * at].wait()
+        copies[3 + 2 * at].wait()
         here = slice(ends[at], ends[at + 1])
         part = across(left_ref[here, :], right_ref[here, :])
         if at > 0:
@@ -143,10 +149,10 @@
 def embed(place, features, fc_weight, class_weight, labels):
     inputs, faces = features.shape
     classes, width = class_weight.shape
-    anywhere = pl.BlockSpec(memory_space=pltpu.HBM)
+    arrays = [placed(array, pltpu.HBM) for array in (features, fc_weight, class_weight, labels)]
     return pl.pallas_call(
         embed_kernel,
-        in_specs=[SMEM, anywhere, anywhere, VMEM, VMEM],
+        in_specs=[SMEM] + [pl.BlockSpec(memory_space=pltpu.HBM)] * len(arrays),
         out_specs=[VMEM, VMEM],
         out_shape=[
             pltpu.VMEM((faces, 2 * width), jnp.bfloat16),
@@ -156,18 +162,13 @@
             pltpu.VMEM((inputs, faces), jnp.bfloat16),
             pltpu.VMEM((inputs, width), jnp.bfloat16),
             pltpu.VMEM((faces, width), jnp.float32),
-            pltpu.SemaphoreType.DMA((CHUNKS,)),
-            pltpu.SemaphoreType.DMA((CHUNKS,)),
+            pltpu.VMEM((classes, width), jnp.bfloat16),
+            pltpu.VMEM((1, faces), jnp.int32),
+            pltpu.SemaphoreType.DMA((2 + 2 * CHUNKS,)),
         ],
         compiler_params=pltpu.CompilerParams(vmem_limit_bytes=LIMIT),
         name="embed",
-    )(
-        place,
-        placed(features, pltpu.HBM),
-        placed(fc_weight, pltpu.HBM),
-        placed(class_weight),
-        placed(labels),
-    )
+    )(place, *arrays)
 
 
 def cosine_kernel(place_ref, units_ref, class_ref, labels_ref, pull_ref, others_ref):
@@ -332,10 +333,9 @@
         copies[-1].start()
 
     for number, (piece, source) in enumerate(zip(pieces, sources)):
-        other_half, other_parity, start = piece
-        half, parity = half_of(place_ref, other_half), parity_of(place_ref, other_parity)
+        half, parity = half_of(place_ref, piece[0]), parity_of(place_ref, piece[1])
         count = source.shape[0]
-        block = (2 * half + parity) * some + start
+        block = (2 * half + parity) * some
         fc_here = slice(done * rows, (done + count) * rows)
         class_here = slice(done * 8, (done + count) * 8)
         for group in range(groups):
@@ -344,12 +344,10 @@
             fc_rows[fc_here, lanes] = values.reshape(count * rows, LANES).astype(jnp.bfloat16)
             values = source[:, base + group * 8 : base + (group + 1) * 8, :].astype(jnp.float32)
             class_rows[class_here, lanes] = values.reshape(count * 8, LANES).astype(jnp.bfloat16)
-            if start == 0:
-                over_rows[number, :, lanes] = source[group, base + groups * 8 :, :]
+            over_rows[number, :, lanes] = source[group, base + groups * 8 :, :]
         send(fc_rows.at[fc_here, :], fc_ref, block * rows, count * rows)
         send(class_rows.at[class_here, :], class_ref, block * 8, count * 8)
-        if start == 0:
-            send(over_rows.at[number], fc_ref, main + half * each + parity * 8, 8)
+        send(over_rows.at[number], fc_ref, main + half * each + parity * 8, 8)
         done += count
     for copy in copies:
         copy.wait()
@@ -410,38 +408,29 @@
 
     swap = [(0, 1), (1, 0)]
     length = 2 * lax.axis_size("zh")
-    pairs = [[(z, z ^ 1) for z in range(length)]]
-    pairs.append([(z, (z + 2 * (z % 2) - 1) % length) for z in range(length)])
-
-    def neighbours(values):
-        parts_of = (values[: chips // 2], values[chips // 2 :])
-        return [lax.ppermute(part, ("zh", "zl"), pair) for part, pair in zip(parts_of, pairs)]
+    pairs = []
+    for z in range(length):
+        pairs.append((2 * z, 2 * (z ^ 1)))
+        pairs.append((2 * z + 1, 2 * ((z + 2 * (z % 2) - 1) % length) + 1))
+    neighbour = ("zh", "zl", "core")
 
     operands = (blocks, features, grads, units, others, class_weight)
     theirs = lax.ppermute(parts(True, place, jnp.bfloat16, *operands), "core", swap)
     total = parts(False, place, jnp.float32, *operands) + theirs.astype(jnp.float32)
-    got = jnp.concatenate(neighbours(total[:chips].astype(jnp.bfloat16)), axis=0)
+    got = lax.ppermute(total[:chips].astype(jnp.bfloat16), neighbour, pairs)
     mine = (total[chips:] + got.astype(jnp.float32)).astype(jnp.bfloat16)
     done = jnp.sum(exchange(mine, CHIPS).astype(jnp.float32), axis=0).astype(jnp.bfloat16)
 
     sizes = (inputs, classes, width)
     mine = exchange(jnp.broadcast_to(done, (chips,) + done.shape), CHIPS)
-    left, right = neighbours(mine)
-    across_own = lax.ppermute(mine, "core", swap)
-    across_next = lax.ppermute(jnp.concatenate([left, right], axis=0), "core", swap)
-    written = assemble(place, blocks, sizes, {(False, False, 0): mine}, ())
-    written = assemble(
-        place,
-        blocks,
-        sizes,
-        {
-            (False, True, 0): left,
-            (False, True, chips // 2): right,
-            (True, False, 0): across_own,
-        },
-        written,
-    )
-    return tuple(assemble(place, blocks, sizes, {(True, True, 0): across_next}, written))
+    next_mine = lax.ppermute(mine, neighbour, pairs)
+    across_mine = lax.ppermute(mine, "core", swap)
+    written = assemble(place, blocks, sizes, {(False, False): mine}, ())
+    next_mine, written = lax.optimization_barrier((next_mine, written))
+    across_next = lax.ppermute(next_mine, "core", swap)
+    pieces = {(False, True): next_mine, (True, False): across_mine}
+    written = assemble(place, blocks, sizes, pieces, written)
+    return tuple(assemble(place, blocks, sizes, {(True, True): across_next}, written))
 
 
 def solution(mesh):

time: 168 us -> 162 us (0.964)
  starting transfers between devices: 35.4 us -> 30.6 us
  local copies, waits for them, and re-layouts: 1.92 us -> 0.2 us
    ppermute x6 -> x4, starting transfers between devices: 25.4 us -> 20.6 us  [the longest x1 11.3 us: shards(): got = lax.ppermute(total[:chips].astype(jnp.bfloat16), neighbour, pairs)]
    unnamed x8 -> x6, local copies, waits for them, and re-layouts: 1.73 us -> 0.01 us
    ppermute x6 -> x4, waiting for transfers between devices: 11.2 us -> 11.8 us  [the longest x1 6.91 us: shards(): got = lax.ppermute(total[:chips].astype(jnp.bfloat16), neighbour, pairs)]
  transfers between devices with their start and end apart: 7 -> 5, of which waited for: 4 -> 4; matrix products, arithmetic and copies ran while one was open for 0% -> 0% of each run, Pallas kernels for 2% -> 2%
where the time goes in v5:
time: 162 us
  blocking collectives  107 us (66%)
  starting transfers between devices  30.6 us (19%)
  waiting for transfers between devices  13.3 us (8%)
  Pallas kernels  9.82 us (6%)
    all_to_all x6, blocking collectives, exchange(): return lax.all_to_all(blocks, axes, 0, 0, tiled=True)  107 us
    ppermute x1, starting transfers between devices, shards(): got = lax.ppermute(total[:chips].astype(jnp.bfloat16), neighbour, pairs)  11.3 us
    ppermute x1, starting transfers between devices, shards(): lax.ppermute(parts(True, place, jnp.bfloat16, *operands), 'core', swap)  10 us
    ppermute x1, waiting for transfers between devices, shards(): got = lax.ppermute(total[:chips].astype(jnp.bfloat16), neighbour, pairs)  6.91 us
    ppermute x1, waiting for transfers between devices, shards(): next_mine = lax.ppermute(mine, neighbour, pairs)  4.51 us
    ppermute x1, starting transfers between devices, shards(): next_mine = lax.ppermute(mine, neighbour, pairs)  3.89 us
    pallas_call x4, Pallas kernels, call(): pl.pallas_call(kernel, in_specs=specs, out_specs=[VMEM] * len(results), o...  3.85 us
    ppermute x1, starting transfers between devices, shards(): across_next = lax.ppermute(next_mine, 'core', swap)  3.26 us
  transfers between devices with their start and end apart: 5, of which 4 were waited for; matrix products, arithmetic and copies ran while one was open for 0% of the time, Pallas kernels for 2%

profile of v5, /device:TPU:1, one launch (start us, length us, event | category | flops | bytes accessed | tf_op | source)
XLA Modules:
  0.0 162.0 jit_solution(15000488520541318858)
XLA Ops:
  0.6 3.0 %embed.1 = (bf16[512,1024]{1,0:T(8,128)(2,1)S(1)}, bf16[512,512]{1,0:T(8,128)(2,1)S(1)}) custom-call(s32[1]{0:T(128)} %bitcast.place_ref, bf16[1568,512]{1,0:T(8,128)(2,1)} %bitcast.7, bf16[1568,512]{1,0:T(8,128)(2,1)} %fc_ref.1, bf16[512,512]{1,0:T(8,128)(2,1)} %class_ref.5, s32[1,512]{1,0:T(1,128)} %bitcast.17), custom_call_target="tpu_custom_call" | custom-call | tf_op jit(solution)/shard_map/embed/pallas_call | solution.py:153
  3.7 17.7 %all_to_all.38 = bf16[8,64,1024]{2,1,0:T(8,128)(2,1)S(1)} all-to-all(bf16[8,64,1024]{2,1,0:T(8,128)(2,1)S(1)} %bitcast.15), channel_id=1, replica_groups=mesh['zh'=4,'zl'=2,'yh'=4,'core'=2,'x'=4,'yl'=2] {'x','yl'}, dimensions={0} | all-to-all | bytes 2097152 | tf_op jit(solution)/shard_map/all_to_all | solution.py:27
  21.4 0.2 convert_reduce_fusion
  21.6 0.1 fusion.1
  21.7 0.1 divide_convert_fusion
  21.8 10.3 %all_to_all.39 = bf16[8,64,512]{2,1,0:T(8,128)(2,1)S(1)} all-to-all(bf16[8,64,512]{2,1,0:T(8,128)(2,1)S(1)} %broadcast_in_dim.7), channel_id=1, replica_groups=mesh['zh'=4,'zl'=2,'yh'=4,'core'=2,'x'=4,'yl'=2] {'x','yl'}, dimensions={0} | all-to-all | bytes 1048576 | tf_op jit(solution)/shard_map/all_to_all | solution.py:27
  32.1 1.6 %cosines.1 = (bf16[512,640]{1,0:T(8,128)(2,1)S(1)}, f32[512,512]{1,0:T(8,128)S(1)}) custom-call(s32[1]{0:T(128)} %bitcast.place_ref, bf16[512,512]{1,0:T(8,128)(2,1)S(1)} %bitcast.10, bf16[512,512]{1,0:T(8,128)(2,1)S(1)} %get-tuple-element.14.class_ref, s32[1,512]{1,0:T(1,128)S(1)} %bitcast.18), custom_call_target="tpu_custom_call" | custom-call | tf_op jit(solution)/shard_map/cosines/pallas_call | solution.py:80
  33.7 10.8 %all_to_all.40.pulls_ref = bf16[8,64,640]{2,1,0:T(8,128)(2,1)S(1)} all-to-all(bf16[8,64,640]{2,1,0:T(8,128)(2,1)S(1)} %bitcast.16), channel_id=1, replica_groups=mesh['zh'=4,'zl'=2,'yh'=4,'core'=2,'x'=4,'yl'=2] {'x','yl'}, dimensions={0} | all-to-all | bytes 1310720 | tf_op jit(solution)/shard_map/all_to_all | solution.py:27
  44.5 0.4 raw_grads.1
  44.9 10.9 %all_to_all.41 = bf16[8,64,640]{2,1,0:T(8,128)(2,1)S(1)} all-to-all(bf16[8,64,640]{2,1,0:T(8,128)(2,1)S(1)} %raw_grads.1), channel_id=1, replica_groups=mesh['zh'=4,'zl'=2,'yh'=4,'core'=2,'x'=4,'yl'=2] {'x','yl'}, dimensions={0} | all-to-all | bytes 1310720 | tf_op jit(solution)/shard_map/all_to_all | solution.py:27
  55.8 0.9 parts.3
  56.7 10.0 %collective-permute-start = (bf16[32,136,128]{2,1,0:T(8,128)(2,1)S(1)}, bf16[32,136,128]{2,1,0:T(8,128)(2,1)S(1)}, u32[]{:S(2)}, u32[]{:S(2)}) collective-permute-start(bf16[32,136,128]{2,1,0:T(8,128)(2,1)S(1)} %parts.3), channel_id=1, source_target_pairs={{0,8},{8,0},{1,9},{9,1},{2,10},{10,2},{3,11},{11,3},{4,12},{12,4},... | collective-permute-start | bytes 3342344 | tf_op jit(solution)/shard_map/ppermute | solution.py:418
  66.7 0.9 parts.2
  67.6 1.4 collective-permute-done
  69.1 0.2 convert_add_fusion
  69.2 0.1 slice.27
  69.3 11.3 %collective-permute-start.1 = (bf16[16,136,128]{2,1,0:T(8,128)(2,1)S(1)}, bf16[16,136,128]{2,1,0:T(8,128)(2,1)S(1)}, u32[]{:S(2)}, u32[]{:S(2)}) collective-permute-start(bf16[16,136,128]{2,1,0:T(8,128)(2,1)S(1)} %slice.27), channel_id=1, source_target_pairs={{0,64},{8,456},{64,0},{72,136},{128,192},{136,72},{192,128},{200,2... | collective-permute-start | bytes 1671176 | tf_op jit(solution)/shard_map/ppermute | solution.py:420
  80.6 6.9 %collective-permute-done.1 = bf16[16,136,128]{2,1,0:T(8,128)(2,1)S(1)} collective-permute-done((bf16[16,136,128]{2,1,0:T(8,128)(2,1)S(1)}, bf16[16,136,128]{2,1,0:T(8,128)(2,1)S(1)}, u32[]{:S(2)}, u32[]{:S(2)}) %collective-permute-start.1) | collective-permute-done | bytes 557088 | tf_op jit(solution)/shard_map/ppermute | solution.py:420
  87.5 0.1 fusion
  87.7 29.0 %all_to_all.42 = bf16[16,136,128]{2,1,0:T(8,128)(2,1)S(1)} all-to-all(bf16[16,136,128]{2,1,0:T(8,128)(2,1)S(1)} %fusion), channel_id=1, replica_groups=mesh['zh'=4,'zl'=2,'yh'=4,'core'=2,'x'=4,'yl'=2] {'zh','yh'}, dimensions={0} | all-to-all | bytes 1114112 | tf_op jit(solution)/shard_map/all_to_all | solution.py:27
  116.6 0.1 reduce_sum.32
  116.7 0.1 broadcast_in_dim.8
  116.8 28.0 %all_to_all.43.refs_0_ = bf16[16,136,128]{2,1,0:T(8,128)(2,1)S(1)} all-to-all(bf16[16,136,128]{2,1,0:T(8,128)(2,1)S(1)} %broadcast_in_dim.8), channel_id=1, replica_groups=mesh['zh'=4,'zl'=2,'yh'=4,'core'=2,'x'=4,'yl'=2] {'zh','yh'}, dimensions={0} | all-to-all | bytes 1114112 | tf_op jit(solution)/shard_map/all_to_all | solution.py:27
  144.8 3.9 %collective-permute-start.2 = (bf16[16,136,128]{2,1,0:T(8,128)(2,1)S(1)}, bf16[16,136,128]{2,1,0:T(8,128)(2,1)S(1)}, u32[]{:S(2)}, u32[]{:S(2)}) collective-permute-start(bf16[16,136,128]{2,1,0:T(8,128)(2,1)S(1)} %all_to_all.43.refs_0_), channel_id=1, source_target_pairs={{0,64},{8,456},{64,0},{72,136},{128,192},{136,72},{192,128},{200,2... | collective-permute-start | bytes 1671176 | tf_op jit(solution)/shard_map/ppermute | solution.py:426
  148.7 2.1 %collective-permute-start.4 = (bf16[16,136,128]{2,1,0:T(8,128)(2,1)S(1)}, bf16[16,136,128]{2,1,0:T(8,128)(2,1)S(1)}, u32[]{:S(2)}, u32[]{:S(2)}) collective-permute-start(bf16[16,136,128]{2,1,0:T(8,128)(2,1)S(1)} %all_to_all.43.refs_0_), channel_id=1, source_target_pairs={{0,8},{8,0},{1,9},{9,1},{2,10},{10,2},{3,11},{11,3},{4,12},{12,4},... | collective-permute-start | bytes 1671176 | tf_op jit(solution)/shard_map/ppermute | solution.py:427
  150.8 0.9 assemble.3
  151.8 4.5 %collective-permute-done.2.refs_0_ = bf16[16,136,128]{2,1,0:T(8,128)(2,1)S(1)} collective-permute-done((bf16[16,136,128]{2,1,0:T(8,128)(2,1)S(1)}, bf16[16,136,128]{2,1,0:T(8,128)(2,1)S(1)}, u32[]{:S(2)}, u32[]{:S(2)}) %collective-permute-start.2) | collective-permute-done | bytes 557088 | tf_op jit(solution)/shard_map/ppermute | solution.py:426
  156.3 3.3 %collective-permute-start.3 = (bf16[16,136,128]{2,1,0:T(8,128)(2,1)S(1)}, bf16[16,136,128]{2,1,0:T(8,128)(2,1)S(1)}, u32[]{:S(2)}, u32[]{:S(2)}) collective-permute-start(bf16[16,136,128]{2,1,0:T(8,128)(2,1)S(1)} %collective-permute-done.2.refs_0_), channel_id=1, source_target_pairs={{0,8},{8,0},{1,9},{9,1},{2,10},{10,2},{3,11},{11,3},{4,12},{12,4},... | collective-permute-start | bytes 1671176 | tf_op jit(solution)/shard_map/ppermute | solution.py:430
  159.5 0.0 collective-permute-done.4.refs_1_
  159.6 1.1 assemble.4
  160.7 0.4 collective-permute-done.3.refs_0_
  161.1 0.9 assemble.5
  (8 shorter events, 0.1 us)
Async XLA Ops:
  21.4 10.7 %copy-start.2 = (s32[512]{0:T(512)S(1)}, s32[512]{0:T(512)}, u32[]{:S(2)}) copy-start(s32[512]{0:T(512)} %param.7) | copy-start | bytes 6148
  44.5 11.3 %copy-start = (bf16[512,1568]{0,1:T(8,128)(2,1)S(1)}, bf16[512,1568]{0,1:T(8,128)(2,1)}, u32[]{:S(2)}) copy-start(bf16[512,1568]{0,1:T(8,128)(2,1)} %param.4) | copy-start | bytes 4816900
  44.5 11.3 %copy-start.1 = (bf16[512,512]{1,0:T(8,128)(2,1)S(1)}, bf16[512,512]{1,0:T(8,128)(2,1)}, u32[]{:S(2)}) copy-start(bf16[512,512]{1,0:T(8,128)(2,1)} %class_ref.5) | copy-start | bytes 1572868
  56.7 12.4 %collective-permute-start = (bf16[32,136,128]{2,1,0:T(8,128)(2,1)S(1)}, bf16[32,136,128]{2,1,0:T(8,128)(2,1)S(1)}, u32[]{:S(2)}, u32[]{:S(2)}) collective-permute-start(bf16[32,136,128]{2,1,0:T(8,128)(2,1)S(1)} %parts.3), channel_id=1, source_target_pairs={{0,8},{8,0},{1,9},{9,1},{2,10},{10,2},{3,11},{11,3},{4,12},{12,4},... | collective-permute-start | bytes 3342344 | tf_op jit(solution)/shard_map/ppermute | solution.py:418
  69.3 18.2 %collective-permute-start.1 = (bf16[16,136,128]{2,1,0:T(8,128)(2,1)S(1)}, bf16[16,136,128]{2,1,0:T(8,128)(2,1)S(1)}, u32[]{:S(2)}, u32[]{:S(2)}) collective-permute-start(bf16[16,136,128]{2,1,0:T(8,128)(2,1)S(1)} %slice.27), channel_id=1, source_target_pairs={{0,64},{8,456},{64,0},{72,136},{128,192},{136,72},{192,128},{200,2... | collective-permute-start | bytes 1671176 | tf_op jit(solution)/shard_map/ppermute | solution.py:420
  144.8 11.5 %collective-permute-start.2 = (bf16[16,136,128]{2,1,0:T(8,128)(2,1)S(1)}, bf16[16,136,128]{2,1,0:T(8,128)(2,1)S(1)}, u32[]{:S(2)}, u32[]{:S(2)}) collective-permute-start(bf16[16,136,128]{2,1,0:T(8,128)(2,1)S(1)} %all_to_all.43.refs_0_), channel_id=1, source_target_pairs={{0,64},{8,456},{64,0},{72,136},{128,192},{136,72},{192,128},{200,2... | collective-permute-start | bytes 1671176 | tf_op jit(solution)/shard_map/ppermute | solution.py:426
  148.7 10.9 %collective-permute-start.4 = (bf16[16,136,128]{2,1,0:T(8,128)(2,1)S(1)}, bf16[16,136,128]{2,1,0:T(8,128)(2,1)S(1)}, u32[]{:S(2)}, u32[]{:S(2)}) collective-permute-start(bf16[16,136,128]{2,1,0:T(8,128)(2,1)S(1)} %all_to_all.43.refs_0_), channel_id=1, source_target_pairs={{0,8},{8,0},{1,9},{9,1},{2,10},{10,2},{3,11},{11,3},{4,12},{12,4},... | collective-permute-start | bytes 1671176 | tf_op jit(solution)/shard_map/ppermute | solution.py:427
  156.3 4.8 %collective-permute-start.3 = (bf16[16,136,128]{2,1,0:T(8,128)(2,1)S(1)}, bf16[16,136,128]{2,1,0:T(8,128)(2,1)S(1)}, u32[]{:S(2)}, u32[]{:S(2)}) collective-permute-start(bf16[16,136,128]{2,1,0:T(8,128)(2,1)S(1)} %collective-permute-done.2.refs_0_), channel_id=1, source_target_pairs={{0,8},{8,0},{1,9},{9,1},{2,10},{10,2},{3,11},{11,3},{4,12},{12,4},... | collective-permute-start | bytes 1671176 | tf_op jit(solution)/shard_map/ppermute | solution.py:430

commit v6 on v5

--- a/solution.py
+++ b/solution.py
@@ -247,69 +247,65 @@
 
 
 def parts_kernel(
-    other, place_ref, features_ref, grads_ref, units_ref, others_ref, class_ref, out_ref
+    other_half, other_parity,
+    place_ref, features_ref, grads_ref, units_ref, others_ref, class_ref, out_ref
 ):
-    blocks = out_ref.shape[0]
-    some = blocks // 2
+    some = out_ref.shape[0]
     classes, width = class_ref.shape
     inputs = features_ref.shape[0]
-    rows, groups, main = block_sizes(inputs, width, blocks)
+    rows, groups, main = block_sizes(inputs, width, 2 * some)
     base = groups * rows
-    half = half_of(place_ref, other)
+    half, parity = half_of(place_ref, other_half), parity_of(place_ref, other_parity)
+    quarter = 2 * half + parity
     grads = grads_ref[:, :width]
+
+    first = pl.multiple_of(quarter * (some * rows), LANES)
+    part = jnp.dot(
+        features_ref[pl.ds(first, some * rows), :], grads, preferred_element_type=jnp.float32
+    )
+    part = part.astype(out_ref.dtype).reshape(some, rows, width)
+    for group in range(groups):
+        out_ref[:, group * rows : (group + 1) * rows, :] = part[
+            :, :, group * LANES : (group + 1) * LANES
+        ]
+
     scales = grads_ref[:, width:].astype(jnp.float32)
     pull_scale, target_scale = unpacked_column(scales, 0), unpacked_column(scales, 1)
+    count = classes // 4
+    first = pl.multiple_of(quarter * count, LANES)
+    others = others_ref[:, pl.ds(first, count)]
+    cos_grad = jnp.where(others < 0.0, -target_scale, others * pull_scale)
+    part = across(cos_grad.astype(jnp.bfloat16), units_ref[...])
+    class_f = class_ref[pl.ds(first, count), :].astype(jnp.float32)
+    class_norm = row_norm(class_f)
+    class_unit = class_f / class_norm
+    part = part - class_unit * jnp.sum(class_unit * part, axis=1, keepdims=True)
+    part = (part / class_norm).astype(out_ref.dtype).reshape(some, 8, width)
+    for group in range(groups):
+        out_ref[:, base + group * 8 : base + (group + 1) * 8, :] = part[
+            :, :, group * LANES : (group + 1) * LANES
+        ]
+
     each = (inputs - main) // 2
     over = jnp.dot(
         features_ref[pl.ds(pl.multiple_of(main + half * each, each), each), :],
         grads,
         preferred_element_type=jnp.float32,
     ).astype(out_ref.dtype)
-    count = classes // 4
-
-    for at, parity in ((0, parity_of(place_ref, True)), (some, parity_of(place_ref, False))):
-        here = slice(at, at + some)
-        first = pl.multiple_of((2 * half + parity) * (some * rows), LANES)
-        part = jnp.dot(
-            features_ref[pl.ds(first, some * rows), :], grads, preferred_element_type=jnp.float32
-        )
-        part = part.astype(out_ref.dtype).reshape(some, rows, width)
-        for group in range(groups):
-            out_ref[here, group * rows : (group + 1) * rows, :] = part[
-                :, :, group * LANES : (group + 1) * LANES
-            ]
-
-        first = pl.multiple_of((2 * half + parity) * count, LANES)
-        others = others_ref[:, pl.ds(first, count)]
-        cos_grad = jnp.where(others < 0.0, -target_scale, others * pull_scale)
-        part = across(cos_grad.astype(jnp.bfloat16), units_ref[...])
-        class_f = class_ref[pl.ds(first, count), :].astype(jnp.float32)
-        class_norm = row_norm(class_f)
-        class_unit = class_f / class_norm
-        part = part - class_unit * jnp.sum(class_unit * part, axis=1, keepdims=True)
-        part = (part / class_norm).astype(out_ref.dtype).reshape(some, 8, width)
-        for group in range(groups):
-            out_ref[here, base + group * 8 : base + (group + 1) * 8, :] = part[
-                :, :, group * LANES : (group + 1) * LANES
-            ]
-
-        strip = jnp.where(parity == 0, over[:8], over[8:])
-        for group in range(groups):
-            out_ref[at + group, base + groups * 8 :, :] = strip[
-                :, group * LANES : (group + 1) * LANES
-            ]
-        out_ref[at + groups : at + some, base + groups * 8 :, :] = jnp.zeros(
-            (some - groups, 8, LANES), out_ref.dtype
-        )
-
-
-def parts(other, place, dtype, blocks, features, grads, units, others, class_weight):
-    rows, groups, _ = block_sizes(features.shape[0], class_weight.shape[1], blocks)
+    strip = jnp.where(parity == 0, over[:8], over[8:])
+    for group in range(groups):
+        out_ref[group, base + groups * 8 :, :] = strip[:, group * LANES : (group + 1) * LANES]
+    out_ref[groups:, base + groups * 8 :, :] = jnp.zeros((some - groups, 8, LANES), out_ref.dtype)
+
+
+def parts(quarter, place, dtype, blocks, features, grads, units, others, class_weight):
+    width = class_weight.shape[1]
+    rows, groups, _ = block_sizes(features.shape[0], width, blocks)
     return call(
-        functools.partial(parts_kernel, other),
+        functools.partial(parts_kernel, *quarter),
         "parts",
         (place, features, grads, units, others, class_weight),
-        [((blocks, groups * (rows + 8) + 8, LANES), dtype)],
+        [((blocks // 2, groups * (rows + 8) + 8, LANES), dtype)],
     )[0]
 
 
@@ -415,10 +411,16 @@
     neighbour = ("zh", "zl", "core")
 
     operands = (blocks, features, grads, units, others, class_weight)
-    theirs = lax.ppermute(parts(True, place, jnp.bfloat16, *operands), "core", swap)
-    total = parts(False, place, jnp.float32, *operands) + theirs.astype(jnp.float32)
-    got = lax.ppermute(total[:chips].astype(jnp.bfloat16), neighbour, pairs)
-    mine = (total[chips:] + got.astype(jnp.float32)).astype(jnp.bfloat16)
+    theirs = parts((True, True), place, jnp.bfloat16, *operands)
+    theirs = lax.ppermute(theirs, "core", swap)
+    sent = parts((False, True), place, jnp.float32, *operands) + theirs.astype(jnp.float32)
+    sent, later = lax.optimization_barrier((sent.astype(jnp.bfloat16), place))
+    got = lax.ppermute(sent, neighbour, pairs)
+    theirs = parts((True, False), later, jnp.bfloat16, *operands)
+    theirs = lax.ppermute(theirs, "core", swap)
+    mine = parts((False, False), later, jnp.float32, *operands) + got.astype(jnp.float32)
+    mine = lax.optimization_barrier(mine)
+    mine = (mine + theirs.astype(jnp.float32)).astype(jnp.bfloat16)
     done = jnp.sum(exchange(mine, CHIPS).astype(jnp.float32), axis=0).astype(jnp.bfloat16)
 
     sizes = (inputs, classes, width)

time: 162 us -> 162 us (level)
  waiting for transfers between devices: 13.3 us -> 10.3 us
    ppermute x2 -> x3, waiting for transfers between devices: 8.33 us -> 4.88 us  [the longest x1 3.87 us: shards(): got = lax.ppermute(sent, neighbour, pairs)]
    ppermute x2 -> x3, starting transfers between devices: 21.3 us -> 23.2 us  [the longest x2 11.9 us: shards(): theirs = lax.ppermute(theirs, 'core', swap)]
    pallas_call x4 -> x6, Pallas kernels: 3.85 us -> 4.18 us  [call(): pl.pallas_call(kernel, in_specs=specs, out_specs=[VMEM] * len(results), o...]
  transfers between devices with their start and end apart: 5 -> 6, of which waited for: 4 -> 4; matrix products, arithmetic and copies ran while one was open for 0% -> 0% of each run, Pallas kernels for 2% -> 2%
where the time goes in v6:
time: 162 us; the launch traced here: 161 us
  blocking collectives  107 us (66%)
  starting transfers between devices  32.1 us (20%)
  waiting for transfers between devices  10.3 us (6%)
  Pallas kernels  10.2 us (6%)
    all_to_all x6, blocking collectives, exchange(): return lax.all_to_all(blocks, axes, 0, 0, tiled=True)  107 us
    ppermute x2, starting transfers between devices, shards(): theirs = lax.ppermute(theirs, 'core', swap)  11.9 us
    ppermute x1, starting transfers between devices, shards(): got = lax.ppermute(sent, neighbour, pairs)  11.3 us
    ppermute x1, waiting for transfers between devices, shards(): next_mine = lax.ppermute(mine, neighbour, pairs)  4.94 us
    pallas_call x6, Pallas kernels, call(): pl.pallas_call(kernel, in_specs=specs, out_specs=[VMEM] * len(results), o...  4.18 us
    ppermute x1, waiting for transfers between devices, shards(): got = lax.ppermute(sent, neighbour, pairs)  3.87 us
    ppermute x1, starting transfers between devices, shards(): next_mine = lax.ppermute(mine, neighbour, pairs)  3.31 us
  transfers between devices with their start and end apart: 6, of which 4 were waited for; matrix products, arithmetic and copies ran while one was open for 0% of the time, Pallas kernels for 2%

profile of v6, /device:TPU:1, one launch (start us, length us, event | category | flops | bytes accessed | tf_op | source)
XLA Modules:
  0.0 161.4 jit_solution(6426343757936047417)
XLA Ops:
  0.6 3.0 %embed.1 = (bf16[512,1024]{1,0:T(8,128)(2,1)S(1)}, bf16[512,512]{1,0:T(8,128)(2,1)S(1)}) custom-call(s32[1]{0:T(128)} %bitcast.place_ref, bf16[1568,512]{1,0:T(8,128)(2,1)} %bitcast.7, bf16[1568,512]{1,0:T(8,128)(2,1)} %fc_ref.1, bf16[512,512]{1,0:T(8,128)(2,1)} %class_ref.9, s32[1,512]{1,0:T(1,128)} %bitcast.23), custom_call_target="tpu_custom_call" | custom-call | tf_op jit(solution)/shard_map/embed/pallas_call | solution.py:153
  3.7 17.7 %all_to_all.38 = bf16[8,64,1024]{2,1,0:T(8,128)(2,1)S(1)} all-to-all(bf16[8,64,1024]{2,1,0:T(8,128)(2,1)S(1)} %bitcast.21), channel_id=1, replica_groups=mesh['zh'=4,'zl'=2,'yh'=4,'core'=2,'x'=4,'yl'=2] {'x','yl'}, dimensions={0} | all-to-all | bytes 2097152 | tf_op jit(solution)/shard_map/all_to_all | solution.py:27
  21.4 0.2 convert_reduce_fusion
  21.6 0.1 fusion
  21.7 0.1 divide_convert_fusion
  21.9 10.3 %all_to_all.39 = bf16[8,64,512]{2,1,0:T(8,128)(2,1)S(1)} all-to-all(bf16[8,64,512]{2,1,0:T(8,128)(2,1)S(1)} %broadcast_in_dim.7), channel_id=1, replica_groups=mesh['zh'=4,'zl'=2,'yh'=4,'core'=2,'x'=4,'yl'=2] {'x','yl'}, dimensions={0} | all-to-all | bytes 1048576 | tf_op jit(solution)/shard_map/all_to_all | solution.py:27
  32.1 1.6 %cosines.1 = (bf16[512,640]{1,0:T(8,128)(2,1)S(1)}, f32[512,512]{1,0:T(8,128)S(1)}) custom-call(s32[1]{0:T(128)} %bitcast.place_ref, bf16[512,512]{1,0:T(8,128)(2,1)S(1)} %bitcast.12, bf16[512,512]{1,0:T(8,128)(2,1)S(1)} %get-tuple-element.16.class_ref, s32[1,512]{1,0:T(1,128)S(1)} %bitcast.24), custom_call_target="tpu_custom_call" | custom-call | tf_op jit(solution)/shard_map/cosines/pallas_call | solution.py:80
  33.7 10.8 %all_to_all.40.pulls_ref = bf16[8,64,640]{2,1,0:T(8,128)(2,1)S(1)} all-to-all(bf16[8,64,640]{2,1,0:T(8,128)(2,1)S(1)} %bitcast.22), channel_id=1, replica_groups=mesh['zh'=4,'zl'=2,'yh'=4,'core'=2,'x'=4,'yl'=2] {'x','yl'}, dimensions={0} | all-to-all | bytes 1310720 | tf_op jit(solution)/shard_map/all_to_all | solution.py:27
  44.5 0.4 raw_grads.1
  44.9 10.9 %all_to_all.41 = bf16[8,64,640]{2,1,0:T(8,128)(2,1)S(1)} all-to-all(bf16[8,64,640]{2,1,0:T(8,128)(2,1)S(1)} %raw_grads.1), channel_id=1, replica_groups=mesh['zh'=4,'zl'=2,'yh'=4,'core'=2,'x'=4,'yl'=2] {'x','yl'}, dimensions={0} | all-to-all | bytes 1310720 | tf_op jit(solution)/shard_map/all_to_all | solution.py:27
  55.8 0.5 parts.5
  56.3 10.0 %collective-permute-start = (bf16[16,136,128]{2,1,0:T(8,128)(2,1)S(1)}, bf16[16,136,128]{2,1,0:T(8,128)(2,1)S(1)}, u32[]{:S(2)}, u32[]{:S(2)}) collective-permute-start(bf16[16,136,128]{2,1,0:T(8,128)(2,1)S(1)} %parts.5), channel_id=1, source_target_pairs={{0,8},{8,0},{1,9},{9,1},{2,10},{10,2},{3,11},{11,3},{4,12},{12,4},... | collective-permute-start | bytes 1671176 | tf_op jit(solution)/shard_map/ppermute | solution.py:415
  66.4 0.5 parts.4
  66.9 1.0 collective-permute-done
  67.9 0.1 add_convert_fusion.1
  68.0 11.3 %collective-permute-start.1 = (bf16[16,136,128]{2,1,0:T(8,128)(2,1)S(1)}, bf16[16,136,128]{2,1,0:T(8,128)(2,1)S(1)}, u32[]{:S(2)}, u32[]{:S(2)}) collective-permute-start(bf16[16,136,128]{2,1,0:T(8,128)(2,1)S(1)} %add_convert_fusion.1), channel_id=1, source_target_pairs={{0,64},{8,456},{64,0},{72,136},{128,192},{136,72},{192,128},{200,2... | collective-permute-start | bytes 1671176 | tf_op jit(solution)/shard_map/ppermute | solution.py:418
  79.3 0.5 parts.7
  79.9 1.9 %collective-permute-start.2 = (bf16[16,136,128]{2,1,0:T(8,128)(2,1)S(1)}, bf16[16,136,128]{2,1,0:T(8,128)(2,1)S(1)}, u32[]{:S(2)}, u32[]{:S(2)}) collective-permute-start(bf16[16,136,128]{2,1,0:T(8,128)(2,1)S(1)} %parts.7), channel_id=1, source_target_pairs={{0,8},{8,0},{1,9},{9,1},{2,10},{10,2},{3,11},{11,3},{4,12},{12,4},... | collective-permute-start | bytes 1671176 | tf_op jit(solution)/shard_map/ppermute | solution.py:420
  81.8 0.5 parts.6
  82.3 3.9 %collective-permute-done.1 = bf16[16,136,128]{2,1,0:T(8,128)(2,1)S(1)} collective-permute-done((bf16[16,136,128]{2,1,0:T(8,128)(2,1)S(1)}, bf16[16,136,128]{2,1,0:T(8,128)(2,1)S(1)}, u32[]{:S(2)}, u32[]{:S(2)}) %collective-permute-start.1) | collective-permute-done | bytes 557088 | tf_op jit(solution)/shard_map/ppermute | solution.py:418
  86.2 0.1 convert_add_fusion
  86.3 0.1 add_convert_fusion
  86.5 29.0 %all_to_all.42 = bf16[16,136,128]{2,1,0:T(8,128)(2,1)S(1)} all-to-all(bf16[16,136,128]{2,1,0:T(8,128)(2,1)S(1)} %add_convert_fusion), channel_id=1, replica_groups=mesh['zh'=4,'zl'=2,'yh'=4,'core'=2,'x'=4,'yl'=2] {'zh','yh'}, dimensions={0} | all-to-all | bytes 1114112 | tf_op jit(solution)/shard_map/all_to_all | solution.py:27
  115.6 28.6 %all_to_all.43.refs_0_ = bf16[16,136,128]{2,1,0:T(8,128)(2,1)S(1)} all-to-all(bf16[16,136,128]{2,1,0:T(8,128)(2,1)S(1)} %broadcast_in_dim.8), channel_id=1, replica_groups=mesh['zh'=4,'zl'=2,'yh'=4,'core'=2,'x'=4,'yl'=2] {'zh','yh'}, dimensions={0} | all-to-all | bytes 1114112 | tf_op jit(solution)/shard_map/all_to_all | solution.py:27
  144.2 3.3 %collective-permute-start.3 = (bf16[16,136,128]{2,1,0:T(8,128)(2,1)S(1)}, bf16[16,136,128]{2,1,0:T(8,128)(2,1)S(1)}, u32[]{:S(2)}, u32[]{:S(2)}) collective-permute-start(bf16[16,136,128]{2,1,0:T(8,128)(2,1)S(1)} %all_to_all.43.refs_0_), channel_id=1, source_target_pairs={{0,64},{8,456},{64,0},{72,136},{128,192},{136,72},{192,128},{200,2... | collective-permute-start | bytes 1671176 | tf_op jit(solution)/shard_map/ppermute | solution.py:428
  147.5 2.3 %collective-permute-start.5 = (bf16[16,136,128]{2,1,0:T(8,128)(2,1)S(1)}, bf16[16,136,128]{2,1,0:T(8,128)(2,1)S(1)}, u32[]{:S(2)}, u32[]{:S(2)}) collective-permute-start(bf16[16,136,128]{2,1,0:T(8,128)(2,1)S(1)} %all_to_all.43.refs_0_), channel_id=1, source_target_pairs={{0,8},{8,0},{1,9},{9,1},{2,10},{10,2},{3,11},{11,3},{4,12},{12,4},... | collective-permute-start | bytes 1671176 | tf_op jit(solution)/shard_map/ppermute | solution.py:429
  149.9 0.9 assemble.3
  150.8 4.9 %collective-permute-done.3.refs_0_ = bf16[16,136,128]{2,1,0:T(8,128)(2,1)S(1)} collective-permute-done((bf16[16,136,128]{2,1,0:T(8,128)(2,1)S(1)}, bf16[16,136,128]{2,1,0:T(8,128)(2,1)S(1)}, u32[]{:S(2)}, u32[]{:S(2)}) %collective-permute-start.3) | collective-permute-done | bytes 557088 | tf_op jit(solution)/shard_map/ppermute | solution.py:428
  155.7 3.2 %collective-permute-start.4 = (bf16[16,136,128]{2,1,0:T(8,128)(2,1)S(1)}, bf16[16,136,128]{2,1,0:T(8,128)(2,1)S(1)}, u32[]{:S(2)}, u32[]{:S(2)}) collective-permute-start(bf16[16,136,128]{2,1,0:T(8,128)(2,1)S(1)} %collective-permute-done.3.refs_0_), channel_id=1, source_target_pairs={{0,8},{8,0},{1,9},{9,1},{2,10},{10,2},{3,11},{11,3},{4,12},{12,4},... | collective-permute-start | bytes 1671176 | tf_op jit(solution)/shard_map/ppermute | solution.py:432
  159.0 1.1 assemble.4
  160.1 0.4 collective-permute-done.4.refs_0_
  160.5 0.9 assemble.5
  (12 shorter events, 0.2 us)
Async XLA Ops:
  21.6 10.6 %copy-start.2 = (s32[512]{0:T(512)S(1)}, s32[512]{0:T(512)}, u32[]{:S(2)}) copy-start(s32[512]{0:T(512)} %param.7) | copy-start | bytes 6148
  44.5 11.3 %copy-start = (bf16[512,1568]{0,1:T(8,128)(2,1)S(1)}, bf16[512,1568]{0,1:T(8,128)(2,1)}, u32[]{:S(2)}) copy-start(bf16[512,1568]{0,1:T(8,128)(2,1)} %param.4) | copy-start | bytes 4816900
  44.5 11.3 %copy-start.1 = (bf16[512,512]{1,0:T(8,128)(2,1)S(1)}, bf16[512,512]{1,0:T(8,128)(2,1)}, u32[]{:S(2)}) copy-start(bf16[512,512]{1,0:T(8,128)(2,1)} %class_ref.9) | copy-start | bytes 1572868
  56.3 11.6 %collective-permute-start = (bf16[16,136,128]{2,1,0:T(8,128)(2,1)S(1)}, bf16[16,136,128]{2,1,0:T(8,128)(2,1)S(1)}, u32[]{:S(2)}, u32[]{:S(2)}) collective-permute-start(bf16[16,136,128]{2,1,0:T(8,128)(2,1)S(1)} %parts.5), channel_id=1, source_target_pairs={{0,8},{8,0},{1,9},{9,1},{2,10},{10,2},{3,11},{11,3},{4,12},{12,4},... | collective-permute-start | bytes 1671176 | tf_op jit(solution)/shard_map/ppermute | solution.py:415
  68.0 18.2 %collective-permute-start.1 = (bf16[16,136,128]{2,1,0:T(8,128)(2,1)S(1)}, bf16[16,136,128]{2,1,0:T(8,128)(2,1)S(1)}, u32[]{:S(2)}, u32[]{:S(2)}) collective-permute-start(bf16[16,136,128]{2,1,0:T(8,128)(2,1)S(1)} %add_convert_fusion.1), channel_id=1, source_target_pairs={{0,64},{8,456},{64,0},{72,136},{128,192},{136,72},{192,128},{200,2... | collective-permute-start | bytes 1671176 | tf_op jit(solution)/shard_map/ppermute | solution.py:418
  79.9 6.5 %collective-permute-start.2 = (bf16[16,136,128]{2,1,0:T(8,128)(2,1)S(1)}, bf16[16,136,128]{2,1,0:T(8,128)(2,1)S(1)}, u32[]{:S(2)}, u32[]{:S(2)}) collective-permute-start(bf16[16,136,128]{2,1,0:T(8,128)(2,1)S(1)} %parts.7), channel_id=1, source_target_pairs={{0,8},{8,0},{1,9},{9,1},{2,10},{10,2},{3,11},{11,3},{4,12},{12,4},... | collective-permute-start | bytes 1671176 | tf_op jit(solution)/shard_map/ppermute | solution.py:420
  144.2 11.5 %collective-permute-start.3 = (bf16[16,136,128]{2,1,0:T(8,128)(2,1)S(1)}, bf16[16,136,128]{2,1,0:T(8,128)(2,1)S(1)}, u32[]{:S(2)}, u32[]{:S(2)}) collective-permute-start(bf16[16,136,128]{2,1,0:T(8,128)(2,1)S(1)} %all_to_all.43.refs_0_), channel_id=1, source_target_pairs={{0,64},{8,456},{64,0},{72,136},{128,192},{136,72},{192,128},{200,2... | collective-permute-start | bytes 1671176 | tf_op jit(solution)/shard_map/ppermute | solution.py:428
  147.5 11.4 %collective-permute-start.5 = (bf16[16,136,128]{2,1,0:T(8,128)(2,1)S(1)}, bf16[16,136,128]{2,1,0:T(8,128)(2,1)S(1)}, u32[]{:S(2)}, u32[]{:S(2)}) collective-permute-start(bf16[16,136,128]{2,1,0:T(8,128)(2,1)S(1)} %all_to_all.43.refs_0_), channel_id=1, source_target_pairs={{0,8},{8,0},{1,9},{9,1},{2,10},{10,2},{3,11},{11,3},{4,12},{12,4},... | collective-permute-start | bytes 1671176 | tf_op jit(solution)/shard_map/ppermute | solution.py:429
  155.7 4.8 %collective-permute-start.4 = (bf16[16,136,128]{2,1,0:T(8,128)(2,1)S(1)}, bf16[16,136,128]{2,1,0:T(8,128)(2,1)S(1)}, u32[]{:S(2)}, u32[]{:S(2)}) collective-permute-start(bf16[16,136,128]{2,1,0:T(8,128)(2,1)S(1)} %collective-permute-done.3.refs_0_), channel_id=1, source_target_pairs={{0,8},{8,0},{1,9},{9,1},{2,10},{10,2},{3,11},{11,3},{4,12},{12,4},... | collective-permute-start | bytes 1671176 | tf_op jit(solution)/shard_map/ppermute | solution.py:432

commit v7 on v6

--- a/solution.py
+++ b/solution.py
@@ -17,7 +17,9 @@
 CLS = ("x", "yl")
 CHIPS = ("zh", "yh")
 LANES = 128
-CHUNKS = 3
+CHUNKS = 2
+MARK = 1024.0
+STEP = 256
 LIMIT = 24 << 20
 VMEM = pl.BlockSpec(memory_space=pltpu.VMEM)
 SMEM = pl.BlockSpec(memory_space=pltpu.SMEM)
@@ -47,7 +49,7 @@
             term = rest.astype(jnp.bfloat16).astype(jnp.float32)
             block = jnp.where(lane == 3 * at + part, term, block)
             rest = rest - term
-    return block.astype(jnp.bfloat16)
+    return block
 
 
 def unpacked_column(block, at):
@@ -171,10 +173,20 @@
     )(place, *arrays)
 
 
+def target_terms(cosine):
+    sine = jnp.sqrt(1.0 + SOFTEN - cosine * cosine)
+    logit = SCALE * (cosine * math.cos(MARGIN) - sine * math.sin(MARGIN))
+    slope = SCALE * (math.cos(MARGIN) + math.sin(MARGIN) * cosine / sine)
+    return logit, slope
+
+
 def cosine_kernel(place_ref, units_ref, class_ref, labels_ref, pull_ref, others_ref):
     faces, width = units_ref.shape
     classes = class_ref.shape[0]
-    step = 128
+    peers = pull_ref.shape[0]
+    owned = faces // peers
+    step = STEP
+    first = first_of(place_ref, classes)
     labels = spread_labels(labels_ref[...])
     for at in range(0, faces, step):
         here = slice(at, at + step)
@@ -184,61 +196,81 @@
             (((1,), (1,)), ((), ())),
             preferred_element_type=jnp.float32,
         )
-        is_target = target_mask(first_of(place_ref, classes), labels[here, :], step, classes)
+        label = labels[here, :]
+        is_target = target_mask(first, label, step, classes)
         powers = jnp.exp(SCALE * cosine)
         others = jnp.where(is_target, 0.0, powers)
-        others_ref[here, :] = jnp.where(is_target, -1.0, powers)
         pull = jnp.dot(
             others.astype(jnp.bfloat16), class_ref[...], preferred_element_type=jnp.float32
         )
-        pull_ref[here, :width] = pull.astype(jnp.bfloat16)
-        pull_ref[here, width:] = packed_columns(jnp.sum(others, axis=1, keepdims=True))
-
-
-def cosines(place, units, class_unit, labels):
+        pull_ref[at // owned : (at + step) // owned, :owned, :] = pull.astype(
+            jnp.bfloat16
+        ).reshape(step // owned, owned, width)
+        cos_t = jnp.sum(jnp.where(is_target, cosine, 0.0), axis=1, keepdims=True)
+        logit, slope = target_terms(cos_t)
+        others_ref[here, :] = jnp.where(is_target, -(slope + MARK), powers)
+        mine = ((label >= first) & (label < first + classes))[:, :1]
+        power_t = jnp.where(mine, jnp.exp(logit), 0.0)
+        sums = packed_columns(jnp.sum(others, axis=1, keepdims=True), power_t)
+        sums = jnp.transpose(sums)[:8].astype(jnp.bfloat16)
+        for peer in range(peers):
+            pull_ref[peer, owned:, here] = sums
+
+
+def cosines(place, units, class_unit, labels, peers):
     faces, width = units.shape
     classes = class_unit.shape[0]
     return call(
         cosine_kernel,
         "cosines",
         (place, units, class_unit, labels),
-        [((faces, width + LANES), jnp.bfloat16), ((faces, classes), jnp.float32)],
-    )
-
-
-def raw_grad_kernel(loss_weight, pulls_ref, raw_ref, target_ref, sent_ref):
-    width = raw_ref.shape[1]
-    pulls = jnp.sum(pulls_ref[...].astype(jnp.float32), axis=0)
-    pull, rest = pulls[:, :width], unpacked_column(pulls[:, width:], 0)
+        [
+            ((peers, faces // peers + 8, width), jnp.bfloat16),
+            ((faces, classes), jnp.float32),
+        ],
+    )
+
+
+def raw_grad_kernel(
+    loss_weight, place_ref, pulls_ref, raw_ref, target_ref, sent_ref, scales_ref
+):
+    owned, width = raw_ref.shape
+    pulls = pulls_ref[0].astype(jnp.float32)
+    for peer in range(1, pulls_ref.shape[0]):
+        pulls = pulls + pulls_ref[peer].astype(jnp.float32)
+    sums = jnp.concatenate([pulls[owned:], jnp.zeros((LANES - 8, width), jnp.float32)], axis=0)
+    sums = jnp.transpose(sums)
+    rest, power_t = unpacked_column(sums, 0), unpacked_column(sums, 1)
+    inverse = loss_weight / (rest + power_t)
+    lane = lax.broadcasted_iota(jnp.int32, sums.shape, 1)
+    scales_ref[...] = jnp.where(lane == 0, SCALE * inverse, rest * inverse)
+    own = pl.ds(pl.multiple_of(lax.div(place_ref[0], 4) * owned, owned), owned)
+    scales = scales_ref[own, :]
+    pull_scale, rest_scale = scales[:, 0:1], scales[:, 1:2]
+
     raw_embed, target = raw_ref[...], target_ref[...]
     embed_norm = row_norm(raw_embed)
     unit_f = raw_embed / embed_norm
     unit = unit_f.astype(jnp.bfloat16).astype(jnp.float32)
-    cos_t = jnp.sum(unit * target, axis=1, keepdims=True)
-    sine_t = jnp.sqrt(1.0 + SOFTEN - cos_t * cos_t)
-    power_t = jnp.exp(SCALE * (cos_t * math.cos(MARGIN) - sine_t * math.sin(MARGIN)))
-    slope_t = SCALE * (math.cos(MARGIN) + math.sin(MARGIN) * cos_t / sine_t)
-    inverse = loss_weight / (rest + power_t)
-    pull_scale = SCALE * inverse
-    target_scale = rest * inverse * slope_t
-    unit_grad = pull * pull_scale - target * target_scale
+    _, slope = target_terms(jnp.sum(unit * target, axis=1, keepdims=True))
+    unit_grad = pulls[:owned] * pull_scale - target * (rest_scale * slope)
     raw_grad = (
         unit_grad - unit_f * jnp.sum(unit_f * unit_grad, axis=1, keepdims=True)
     ) / embed_norm
     raw_grad = raw_grad.astype(jnp.bfloat16)
-    scales = packed_columns(pull_scale, target_scale)
     for copy in range(sent_ref.shape[0]):
-        sent_ref[copy, :, :width] = raw_grad
-        sent_ref[copy, :, width:] = scales
-
-
-def raw_grads(loss_weight, pulls, raw_embed, target_unit):
+        sent_ref[copy] = raw_grad
+
+
+def raw_grads(loss_weight, place, pulls, raw_embed, target_unit):
+    peers = pulls.shape[0]
+    owned, width = raw_embed.shape
     return call(
         functools.partial(raw_grad_kernel, loss_weight),
         "raw_grads",
-        (pulls, raw_embed, target_unit),
-        [(pulls.shape, jnp.bfloat16)],
-    )[0]
+        (place, pulls, raw_embed, target_unit),
+        [((peers, owned, width), jnp.bfloat16), ((peers * owned, LANES), jnp.float32)],
+    )
 
 
 def block_sizes(inputs, width, blocks):
@@ -248,7 +280,7 @@
 
 def parts_kernel(
     other_half, other_parity,
-    place_ref, features_ref, grads_ref, units_ref, others_ref, class_ref, out_ref
+    place_ref, features_ref, grads_ref, scales_ref, units_ref, others_ref, class_ref, out_ref
 ):
     some = out_ref.shape[0]
     classes, width = class_ref.shape
@@ -257,7 +289,7 @@
     base = groups * rows
     half, parity = half_of(place_ref, other_half), parity_of(place_ref, other_parity)
     quarter = 2 * half + parity
-    grads = grads_ref[:, :width]
+    grads = grads_ref[...]
 
     first = pl.multiple_of(quarter * (some * rows), LANES)
     part = jnp.dot(
@@ -269,12 +301,12 @@
             :, :, group * LANES : (group + 1) * LANES
         ]
 
-    scales = grads_ref[:, width:].astype(jnp.float32)
-    pull_scale, target_scale = unpacked_column(scales, 0), unpacked_column(scales, 1)
+    scales = scales_ref[...]
+    pull_scale, rest_scale = scales[:, 0:1], scales[:, 1:2]
     count = classes // 4
     first = pl.multiple_of(quarter * count, LANES)
     others = others_ref[:, pl.ds(first, count)]
-    cos_grad = jnp.where(others < 0.0, -target_scale, others * pull_scale)
+    cos_grad = jnp.where(others < 0.0, (others + MARK) * rest_scale, others * pull_scale)
     part = across(cos_grad.astype(jnp.bfloat16), units_ref[...])
     class_f = class_ref[pl.ds(first, count), :].astype(jnp.float32)
     class_norm = row_norm(class_f)
@@ -298,13 +330,13 @@
     out_ref[groups:, base + groups * 8 :, :] = jnp.zeros((some - groups, 8, LANES), out_ref.dtype)
 
 
-def parts(quarter, place, dtype, blocks, features, grads, units, others, class_weight):
+def parts(quarter, place, dtype, blocks, features, grads, scales, units, others, class_weight):
     width = class_weight.shape[1]
     rows, groups, _ = block_sizes(features.shape[0], width, blocks)
     return call(
         functools.partial(parts_kernel, *quarter),
         "parts",
-        (place, features, grads, units, others, class_weight),
+        (place, features, grads, scales, units, others, class_weight),
         [((blocks // 2, groups * (rows + 8) + 8, LANES), dtype)],
     )[0]
 
@@ -397,10 +429,10 @@
     units = exchange(jnp.broadcast_to(unit, (n_cls,) + unit.shape), CLS)
     units = units.reshape(faces, width)
 
-    pull, others = cosines(place, units, class_unit, labels)
-    got = exchange(pull, CLS).reshape(n_cls, faces // n_cls, width + LANES)
-    sent = raw_grads(loss_weight, got, raw_embed, target_unit)
-    grads = exchange(sent, CLS).reshape(faces, width + LANES)
+    pull, others = cosines(place, units, class_unit, labels, n_cls)
+    got = exchange(pull, CLS)
+    sent, scales = raw_grads(loss_weight, place, got, raw_embed, target_unit)
+    grads = exchange(sent, CLS).reshape(faces, width)
 
     swap = [(0, 1), (1, 0)]
     length = 2 * lax.axis_size("zh")
@@ -410,7 +442,7 @@
         pairs.append((2 * z + 1, 2 * ((z + 2 * (z % 2) - 1) % length) + 1))
     neighbour = ("zh", "zl", "core")
 
-    operands = (blocks, features, grads, units, others, class_weight)
+    operands = (blocks, features, grads, scales, units, others, class_weight)
     theirs = parts((True, True), place, jnp.bfloat16, *operands)
     theirs = lax.ppermute(theirs, "core", swap)
     sent = parts((False, True), place, jnp.float32, *operands) + theirs.astype(jnp.float32)

time: 162 us -> 159 us (0.981)
  blocking collectives: 107 us -> 104 us
    all_to_all x6, blocking collectives: 107 us -> 104 us  [exchange(): return lax.all_to_all(blocks, axes, 0, 0, tiled=True)]
where the time goes in v7:
time: 159 us; the launch traced here: 158 us
  blocking collectives  104 us (65%)
  starting transfers between devices  32.8 us (21%)
  Pallas kernels  10 us (6%)
  waiting for transfers between devices  9.32 us (6%)
    all_to_all x6, blocking collectives, exchange(): return lax.all_to_all(blocks, axes, 0, 0, tiled=True)  104 us
    ppermute x2, starting transfers between devices, shards(): theirs = lax.ppermute(theirs, 'core', swap)  11.9 us
    ppermute x1, starting transfers between devices, shards(): got = lax.ppermute(sent, neighbour, pairs)  11.1 us
    pallas_call x6, Pallas kernels, call(): pl.pallas_call(kernel, in_specs=specs, out_specs=[VMEM] * len(results), o...  4.14 us
    ppermute x1, waiting for transfers between devices, shards(): next_mine = lax.ppermute(mine, neighbour, pairs)  4.05 us
    ppermute x1, waiting for transfers between devices, shards(): got = lax.ppermute(sent, neighbour, pairs)  3.85 us
    ppermute x1, starting transfers between devices, shards(): next_mine = lax.ppermute(mine, neighbour, pairs)  3.53 us
    ppermute x1, starting transfers between devices, shards(): across_next = lax.ppermute(next_mine, 'core', swap)  3.37 us
  transfers between devices with their start and end apart: 6, of which 4 were waited for; matrix products, arithmetic and copies ran while one was open for 0% of the time, Pallas kernels for 2%

profile of v7, /device:TPU:1, one launch (start us, length us, event | category | flops | bytes accessed | tf_op | source)
XLA Modules:
  0.0 158.1 jit_solution(4949345241710058741)
XLA Ops:
  0.6 2.9 %embed.1 = (bf16[512,1024]{1,0:T(8,128)(2,1)S(1)}, bf16[512,512]{1,0:T(8,128)(2,1)S(1)}) custom-call(s32[1]{0:T(128)} %bitcast.place_ref, bf16[1568,512]{1,0:T(8,128)(2,1)} %bitcast.6, bf16[1568,512]{1,0:T(8,128)(2,1)} %fc_ref.1, bf16[512,512]{1,0:T(8,128)(2,1)} %class_ref.9, s32[1,512]{1,0:T(1,128)} %bitcast.21), custom_call_target="tpu_custom_call" | custom-call | tf_op jit(solution)/shard_map/embed/pallas_call | solution.py:155
  3.6 17.7 %all_to_all.34 = bf16[8,64,1024]{2,1,0:T(8,128)(2,1)S(1)} all-to-all(bf16[8,64,1024]{2,1,0:T(8,128)(2,1)S(1)} %bitcast.20), channel_id=1, replica_groups=mesh['zh'=4,'zl'=2,'yh'=4,'core'=2,'x'=4,'yl'=2] {'x','yl'}, dimensions={0} | all-to-all | bytes 2097152 | tf_op jit(solution)/shard_map/all_to_all | solution.py:29
  21.3 0.2 convert_reduce_fusion
  21.5 0.1 fusion
  21.6 0.1 divide_convert_fusion
  21.8 10.3 %all_to_all.35 = bf16[8,64,512]{2,1,0:T(8,128)(2,1)S(1)} all-to-all(bf16[8,64,512]{2,1,0:T(8,128)(2,1)S(1)} %broadcast_in_dim.7), channel_id=1, replica_groups=mesh['zh'=4,'zl'=2,'yh'=4,'core'=2,'x'=4,'yl'=2] {'x','yl'}, dimensions={0} | all-to-all | bytes 1048576 | tf_op jit(solution)/shard_map/all_to_all | solution.py:29
  32.0 1.3 cosines.1
  33.3 10.5 %all_to_all.36.pulls_ref = bf16[8,72,512]{2,1,0:T(8,128)(2,1)S(1)} all-to-all(bf16[8,72,512]{2,1,0:T(8,128)(2,1)S(1)} %get-tuple-element.19), channel_id=1, replica_groups=mesh['zh'=4,'zl'=2,'yh'=4,'core'=2,'x'=4,'yl'=2] {'x','yl'}, dimensions={0} | all-to-all | bytes 1179648 | tf_op jit(solution)/shard_map/all_to_all | solution.py:29
  43.8 0.6 raw_grads.1
  44.4 10.0 %all_to_all.37 = bf16[8,64,512]{2,1,0:T(8,128)(2,1)S(1)} all-to-all(bf16[8,64,512]{2,1,0:T(8,128)(2,1)S(1)} %get-tuple-element.20), channel_id=1, replica_groups=mesh['zh'=4,'zl'=2,'yh'=4,'core'=2,'x'=4,'yl'=2] {'x','yl'}, dimensions={0} | all-to-all | bytes 1048576 | tf_op jit(solution)/shard_map/all_to_all | solution.py:29
  54.4 0.6 parts.5
  55.0 10.0 %collective-permute-start = (bf16[16,136,128]{2,1,0:T(8,128)(2,1)S(1)}, bf16[16,136,128]{2,1,0:T(8,128)(2,1)S(1)}, u32[]{:S(2)}, u32[]{:S(2)}) collective-permute-start(bf16[16,136,128]{2,1,0:T(8,128)(2,1)S(1)} %parts.5), channel_id=1, source_target_pairs={{0,8},{8,0},{1,9},{9,1},{2,10},{10,2},{3,11},{11,3},{4,12},{12,4},... | collective-permute-start | bytes 1671176 | tf_op jit(solution)/shard_map/ppermute | solution.py:447
  65.0 0.6 parts.4
  65.5 1.0 collective-permute-done
  66.5 0.1 add_convert_fusion.1
  66.6 11.1 %collective-permute-start.1 = (bf16[16,136,128]{2,1,0:T(8,128)(2,1)S(1)}, bf16[16,136,128]{2,1,0:T(8,128)(2,1)S(1)}, u32[]{:S(2)}, u32[]{:S(2)}) collective-permute-start(bf16[16,136,128]{2,1,0:T(8,128)(2,1)S(1)} %add_convert_fusion.1), channel_id=1, source_target_pairs={{0,64},{8,456},{64,0},{72,136},{128,192},{136,72},{192,128},{200,2... | collective-permute-start | bytes 1671176 | tf_op jit(solution)/shard_map/ppermute | solution.py:450
  77.7 0.6 parts.7
  78.3 1.9 %collective-permute-start.2 = (bf16[16,136,128]{2,1,0:T(8,128)(2,1)S(1)}, bf16[16,136,128]{2,1,0:T(8,128)(2,1)S(1)}, u32[]{:S(2)}, u32[]{:S(2)}) collective-permute-start(bf16[16,136,128]{2,1,0:T(8,128)(2,1)S(1)} %parts.7), channel_id=1, source_target_pairs={{0,8},{8,0},{1,9},{9,1},{2,10},{10,2},{3,11},{11,3},{4,12},{12,4},... | collective-permute-start | bytes 1671176 | tf_op jit(solution)/shard_map/ppermute | solution.py:452
  80.2 0.6 parts.6
  80.8 3.9 %collective-permute-done.1 = bf16[16,136,128]{2,1,0:T(8,128)(2,1)S(1)} collective-permute-done((bf16[16,136,128]{2,1,0:T(8,128)(2,1)S(1)}, bf16[16,136,128]{2,1,0:T(8,128)(2,1)S(1)}, u32[]{:S(2)}, u32[]{:S(2)}) %collective-permute-start.1) | collective-permute-done | bytes 557088 | tf_op jit(solution)/shard_map/ppermute | solution.py:450
  84.6 0.1 convert_add_fusion
  84.7 0.1 add_convert_fusion
  84.9 28.7 %all_to_all.38 = bf16[16,136,128]{2,1,0:T(8,128)(2,1)S(1)} all-to-all(bf16[16,136,128]{2,1,0:T(8,128)(2,1)S(1)} %add_convert_fusion), channel_id=1, replica_groups=mesh['zh'=4,'zl'=2,'yh'=4,'core'=2,'x'=4,'yl'=2] {'zh','yh'}, dimensions={0} | all-to-all | bytes 1114112 | tf_op jit(solution)/shard_map/all_to_all | solution.py:29
  113.8 27.0 %all_to_all.39.refs_0_ = bf16[16,136,128]{2,1,0:T(8,128)(2,1)S(1)} all-to-all(bf16[16,136,128]{2,1,0:T(8,128)(2,1)S(1)} %broadcast_in_dim.8), channel_id=1, replica_groups=mesh['zh'=4,'zl'=2,'yh'=4,'core'=2,'x'=4,'yl'=2] {'zh','yh'}, dimensions={0} | all-to-all | bytes 1114112 | tf_op jit(solution)/shard_map/all_to_all | solution.py:29
  140.7 3.5 %collective-permute-start.3 = (bf16[16,136,128]{2,1,0:T(8,128)(2,1)S(1)}, bf16[16,136,128]{2,1,0:T(8,128)(2,1)S(1)}, u32[]{:S(2)}, u32[]{:S(2)}) collective-permute-start(bf16[16,136,128]{2,1,0:T(8,128)(2,1)S(1)} %all_to_all.39.refs_0_), channel_id=1, source_target_pairs={{0,64},{8,456},{64,0},{72,136},{128,192},{136,72},{192,128},{200,2... | collective-permute-start | bytes 1671176 | tf_op jit(solution)/shard_map/ppermute | solution.py:460
  144.3 3.0 %collective-permute-start.5 = (bf16[16,136,128]{2,1,0:T(8,128)(2,1)S(1)}, bf16[16,136,128]{2,1,0:T(8,128)(2,1)S(1)}, u32[]{:S(2)}, u32[]{:S(2)}) collective-permute-start(bf16[16,136,128]{2,1,0:T(8,128)(2,1)S(1)} %all_to_all.39.refs_0_), channel_id=1, source_target_pairs={{0,8},{8,0},{1,9},{9,1},{2,10},{10,2},{3,11},{11,3},{4,12},{12,4},... | collective-permute-start | bytes 1671176 | tf_op jit(solution)/shard_map/ppermute | solution.py:461
  147.2 0.9 assemble.3
  148.2 4.1 %collective-permute-done.3.refs_0_ = bf16[16,136,128]{2,1,0:T(8,128)(2,1)S(1)} collective-permute-done((bf16[16,136,128]{2,1,0:T(8,128)(2,1)S(1)}, bf16[16,136,128]{2,1,0:T(8,128)(2,1)S(1)}, u32[]{:S(2)}, u32[]{:S(2)}) %collective-permute-start.3) | collective-permute-done | bytes 557088 | tf_op jit(solution)/shard_map/ppermute | solution.py:460
  152.2 3.4 %collective-permute-start.4 = (bf16[16,136,128]{2,1,0:T(8,128)(2,1)S(1)}, bf16[16,136,128]{2,1,0:T(8,128)(2,1)S(1)}, u32[]{:S(2)}, u32[]{:S(2)}) collective-permute-start(bf16[16,136,128]{2,1,0:T(8,128)(2,1)S(1)} %collective-permute-done.3.refs_0_), channel_id=1, source_target_pairs={{0,8},{8,0},{1,9},{9,1},{2,10},{10,2},{3,11},{11,3},{4,12},{12,4},... | collective-permute-start | bytes 1671176 | tf_op jit(solution)/shard_map/ppermute | solution.py:464
  155.6 1.1 assemble.4
  156.7 0.4 collective-permute-done.4.refs_0_
  157.2 0.9 assemble.5
  (12 shorter events, 0.2 us)
Async XLA Ops:
  21.5 10.6 %copy-start.2 = (s32[512]{0:T(512)S(1)}, s32[512]{0:T(512)}, u32[]{:S(2)}) copy-start(s32[512]{0:T(512)} %param.7) | copy-start | bytes 6148
  33.3 21.1 %copy-start.1 = (bf16[512,512]{1,0:T(8,128)(2,1)S(1)}, bf16[512,512]{1,0:T(8,128)(2,1)}, u32[]{:S(2)}) copy-start(bf16[512,512]{1,0:T(8,128)(2,1)} %class_ref.9) | copy-start | bytes 1572868
  43.8 10.5 %copy-start = (bf16[512,1568]{0,1:T(8,128)(2,1)S(1)}, bf16[512,1568]{0,1:T(8,128)(2,1)}, u32[]{:S(2)}) copy-start(bf16[512,1568]{0,1:T(8,128)(2,1)} %param.4) | copy-start | bytes 4816900
  55.0 11.6 %collective-permute-start = (bf16[16,136,128]{2,1,0:T(8,128)(2,1)S(1)}, bf16[16,136,128]{2,1,0:T(8,128)(2,1)S(1)}, u32[]{:S(2)}, u32[]{:S(2)}) collective-permute-start(bf16[16,136,128]{2,1,0:T(8,128)(2,1)S(1)} %parts.5), channel_id=1, source_target_pairs={{0,8},{8,0},{1,9},{9,1},{2,10},{10,2},{3,11},{11,3},{4,12},{12,4},... | collective-permute-start | bytes 1671176 | tf_op jit(solution)/shard_map/ppermute | solution.py:447
  66.6 18.0 %collective-permute-start.1 = (bf16[16,136,128]{2,1,0:T(8,128)(2,1)S(1)}, bf16[16,136,128]{2,1,0:T(8,128)(2,1)S(1)}, u32[]{:S(2)}, u32[]{:S(2)}) collective-permute-start(bf16[16,136,128]{2,1,0:T(8,128)(2,1)S(1)} %add_convert_fusion.1), channel_id=1, source_target_pairs={{0,64},{8,456},{64,0},{72,136},{128,192},{136,72},{192,128},{200,2... | collective-permute-start | bytes 1671176 | tf_op jit(solution)/shard_map/ppermute | solution.py:450
  78.3 6.4 %collective-permute-start.2 = (bf16[16,136,128]{2,1,0:T(8,128)(2,1)S(1)}, bf16[16,136,128]{2,1,0:T(8,128)(2,1)S(1)}, u32[]{:S(2)}, u32[]{:S(2)}) collective-permute-start(bf16[16,136,128]{2,1,0:T(8,128)(2,1)S(1)} %parts.7), channel_id=1, source_target_pairs={{0,8},{8,0},{1,9},{9,1},{2,10},{10,2},{3,11},{11,3},{4,12},{12,4},... | collective-permute-start | bytes 1671176 | tf_op jit(solution)/shard_map/ppermute | solution.py:452
  140.7 11.5 %collective-permute-start.3 = (bf16[16,136,128]{2,1,0:T(8,128)(2,1)S(1)}, bf16[16,136,128]{2,1,0:T(8,128)(2,1)S(1)}, u32[]{:S(2)}, u32[]{:S(2)}) collective-permute-start(bf16[16,136,128]{2,1,0:T(8,128)(2,1)S(1)} %all_to_all.39.refs_0_), channel_id=1, source_target_pairs={{0,64},{8,456},{64,0},{72,136},{128,192},{136,72},{192,128},{200,2... | collective-permute-start | bytes 1671176 | tf_op jit(solution)/shard_map/ppermute | solution.py:460
  144.3 11.3 %collective-permute-start.5 = (bf16[16,136,128]{2,1,0:T(8,128)(2,1)S(1)}, bf16[16,136,128]{2,1,0:T(8,128)(2,1)S(1)}, u32[]{:S(2)}, u32[]{:S(2)}) collective-permute-start(bf16[16,136,128]{2,1,0:T(8,128)(2,1)S(1)} %all_to_all.39.refs_0_), channel_id=1, source_target_pairs={{0,8},{8,0},{1,9},{9,1},{2,10},{10,2},{3,11},{11,3},{4,12},{12,4},... | collective-permute-start | bytes 1671176 | tf_op jit(solution)/shard_map/ppermute | solution.py:461
  152.2 4.9 %collective-permute-start.4 = (bf16[16,136,128]{2,1,0:T(8,128)(2,1)S(1)}, bf16[16,136,128]{2,1,0:T(8,128)(2,1)S(1)}, u32[]{:S(2)}, u32[]{:S(2)}) collective-permute-start(bf16[16,136,128]{2,1,0:T(8,128)(2,1)S(1)} %collective-permute-done.3.refs_0_), channel_id=1, source_target_pairs={{0,8},{8,0},{1,9},{9,1},{2,10},{10,2},{3,11},{11,3},{4,12},{12,4},... | collective-permute-start | bytes 1671176 | tf_op jit(solution)/shard_map/ppermute | solution.py:464

commit v8 on v7

--- a/solution.py
+++ b/solution.py
@@ -131,7 +131,7 @@
     chosen = jnp.where(chosen, 1.0, 0.0).astype(jnp.bfloat16)
     copies[1].wait()
     class_f = weight_ref[...].astype(jnp.float32)
-    unit_ref[...] = (class_f / row_norm(class_f)).astype(jnp.bfloat16)
+    unit_ref[...] = (class_f * (1.0 / row_norm(class_f))).astype(jnp.bfloat16)
     target_part = jnp.dot(chosen, unit_ref[...], preferred_element_type=jnp.float32)
     sent_ref[:, width:] = target_part.astype(jnp.bfloat16)
 
@@ -171,6 +171,30 @@
         compiler_params=pltpu.CompilerParams(vmem_limit_bytes=LIMIT),
         name="embed",
     )(place, *arrays)
+
+
+def units_kernel(got_ref, raw_ref, target_ref, sent_ref):
+    width = raw_ref.shape[1]
+    got = got_ref[0].astype(jnp.float32)
+    for peer in range(1, got_ref.shape[0]):
+        got = got + got_ref[peer].astype(jnp.float32)
+    raw_embed = got[:, :width]
+    raw_ref[...] = raw_embed
+    target_ref[...] = got[:, width:]
+    unit = (raw_embed * (1.0 / row_norm(raw_embed))).astype(jnp.bfloat16)
+    for copy in range(sent_ref.shape[0]):
+        sent_ref[copy] = unit
+
+
+def unit_rows(got):
+    peers, owned, both = got.shape
+    rows = (owned, both // 2)
+    return call(
+        units_kernel,
+        "units",
+        (got,),
+        [(rows, jnp.float32), (rows, jnp.float32), ((peers,) + rows, jnp.bfloat16)],
+    )
 
 
 def target_terms(cosine):
@@ -249,14 +273,14 @@
     pull_scale, rest_scale = scales[:, 0:1], scales[:, 1:2]
 
     raw_embed, target = raw_ref[...], target_ref[...]
-    embed_norm = row_norm(raw_embed)
-    unit_f = raw_embed / embed_norm
+    inverse_norm = 1.0 / row_norm(raw_embed)
+    unit_f = raw_embed * inverse_norm
     unit = unit_f.astype(jnp.bfloat16).astype(jnp.float32)
     _, slope = target_terms(jnp.sum(unit * target, axis=1, keepdims=True))
     unit_grad = pulls[:owned] * pull_scale - target * (rest_scale * slope)
     raw_grad = (
         unit_grad - unit_f * jnp.sum(unit_f * unit_grad, axis=1, keepdims=True)
-    ) / embed_norm
+    ) * inverse_norm
     raw_grad = raw_grad.astype(jnp.bfloat16)
     for copy in range(sent_ref.shape[0]):
         sent_ref[copy] = raw_grad
@@ -309,10 +333,9 @@
     cos_grad = jnp.where(others < 0.0, (others + MARK) * rest_scale, others * pull_scale)
     part = across(cos_grad.astype(jnp.bfloat16), units_ref[...])
     class_f = class_ref[pl.ds(first, count), :].astype(jnp.float32)
-    class_norm = row_norm(class_f)
-    class_unit = class_f / class_norm
-    part = part - class_unit * jnp.sum(class_unit * part, axis=1, keepdims=True)
-    part = (part / class_norm).astype(out_ref.dtype).reshape(some, 8, width)
+    inverse = 1.0 / row_norm(class_f)
+    along = jnp.sum(class_f * part, axis=1, keepdims=True) * (inverse * inverse)
+    part = ((part - class_f * along) * inverse).astype(out_ref.dtype).reshape(some, 8, width)
     for group in range(groups):
         out_ref[:, base + group * 8 : base + (group + 1) * 8, :] = part[
             :, :, group * LANES : (group + 1) * LANES
@@ -364,16 +387,22 @@
         half, parity = half_of(place_ref, piece[0]), parity_of(place_ref, piece[1])
         count = source.shape[0]
         block = (2 * half + parity) * some
-        fc_here = slice(done * rows, (done + count) * rows)
+        for at in range(0, count, count // 2):
+            fc_here = slice((done + at) * rows, (done + at + count // 2) * rows)
+            for group in range(groups):
+                values = source[
+                    at : at + count // 2, group * rows : (group + 1) * rows, :
+                ].astype(jnp.float32)
+                fc_rows[fc_here, group * LANES : (group + 1) * LANES] = values.reshape(
+                    count // 2 * rows, LANES
+                ).astype(jnp.bfloat16)
+            send(fc_rows.at[fc_here, :], fc_ref, (block + at) * rows, count // 2 * rows)
         class_here = slice(done * 8, (done + count) * 8)
         for group in range(groups):
             lanes = slice(group * LANES, (group + 1) * LANES)
-            values = source[:, group * rows : (group + 1) * rows, :].astype(jnp.float32)
-            fc_rows[fc_here, lanes] = values.reshape(count * rows, LANES).astype(jnp.bfloat16)
             values = source[:, base + group * 8 : base + (group + 1) * 8, :].astype(jnp.float32)
             class_rows[class_here, lanes] = values.reshape(count * 8, LANES).astype(jnp.bfloat16)
             over_rows[number, :, lanes] = source[group, base + groups * 8 :, :]
-        send(fc_rows.at[fc_here, :], fc_ref, block * rows, count * rows)
         send(class_rows.at[class_here, :], class_ref, block * 8, count * 8)
         send(over_rows.at[number], fc_ref, main + half * each + parity * 8, 8)
         done += count
@@ -398,7 +427,7 @@
             pltpu.VMEM((total * rows, width), jnp.bfloat16),
             pltpu.VMEM((total * 8, width), jnp.bfloat16),
             pltpu.VMEM((len(pieces), 8, width), jnp.bfloat16),
-            pltpu.SemaphoreType.DMA((3 * len(pieces),)),
+            pltpu.SemaphoreType.DMA((4 * len(pieces),)),
         ],
         input_output_aliases={1 + len(pieces) + at: at for at in range(len(into))},
         cost_estimate=pl.CostEstimate(
@@ -423,10 +452,8 @@
 
     sent, class_unit = embed(place, features, fc_weight, class_weight, labels)
     got = exchange(sent, CLS).reshape(n_cls, faces // n_cls, 2 * width)
-    got = jnp.sum(got.astype(jnp.float32), axis=0)
-    raw_embed, target_unit = got[:, :width], got[:, width:]
-    unit = (raw_embed / row_norm(raw_embed)).astype(jnp.bfloat16)
-    units = exchange(jnp.broadcast_to(unit, (n_cls,) + unit.shape), CLS)
+    raw_embed, target_unit, sent = unit_rows(got)
+    units = exchange(sent, CLS)
     units = units.reshape(faces, width)
 
     pull, others = cosines(place, units, class_unit, labels, n_cls)

time: 159 us -> 158 us (level)
    pallas_call x6 -> x7, Pallas kernels: 4.14 us -> 4.37 us  [call(): pl.pallas_call(kernel, in_specs=specs, out_specs=[VMEM] * len(results), o...]
where the time goes in v8:
time: 158 us
  blocking collectives  104 us (66%)
  starting transfers between devices  32.7 us (21%)
  Pallas kernels  10.1 us (6%)
  waiting for transfers between devices  9.53 us (6%)
    all_to_all x6, blocking collectives, exchange(): return lax.all_to_all(blocks, axes, 0, 0, tiled=True)  104 us
    ppermute x2, starting transfers between devices, shards(): theirs = lax.ppermute(theirs, 'core', swap)  11.9 us
    ppermute x1, starting transfers between devices, shards(): got = lax.ppermute(sent, neighbour, pairs)  11.1 us
    pallas_call x7, Pallas kernels, call(): pl.pallas_call(kernel, in_specs=specs, out_specs=[VMEM] * len(results), o...  4.37 us
    ppermute x1, waiting for transfers between devices, shards(): next_mine = lax.ppermute(mine, neighbour, pairs)  4.25 us
    ppermute x1, waiting for transfers between devices, shards(): got = lax.ppermute(sent, neighbour, pairs)  3.83 us
    ppermute x1, starting transfers between devices, shards(): next_mine = lax.ppermute(mine, neighbour, pairs)  3.39 us
    ppermute x1, starting transfers between devices, shards(): across_next = lax.ppermute(next_mine, 'core', swap)  3.36 us
  transfers between devices with their start and end apart: 6, of which 4 were waited for; matrix products, arithmetic and copies ran while one was open for 0% of the time, Pallas kernels for 2%

profile of v8, /device:TPU:1, one launch (start us, length us, event | category | flops | bytes accessed | tf_op | source)
XLA Modules:
  0.0 157.8 jit_solution(5968404735893556087)
XLA Ops:
  0.6 2.9 %embed.1 = (bf16[512,1024]{1,0:T(8,128)(2,1)S(1)}, bf16[512,512]{1,0:T(8,128)(2,1)S(1)}) custom-call(s32[1]{0:T(128)} %bitcast.place_ref, bf16[1568,512]{1,0:T(8,128)(2,1)} %bitcast.6, bf16[1568,512]{1,0:T(8,128)(2,1)} %fc_ref.1, bf16[512,512]{1,0:T(8,128)(2,1)} %class_ref.9, s32[1,512]{1,0:T(1,128)} %bitcast.21), custom_call_target="tpu_custom_call" | custom-call | tf_op jit(solution)/shard_map/embed/pallas_call | solution.py:155
  3.6 17.7 %all_to_all.34.got_ref = bf16[8,64,1024]{2,1,0:T(8,128)(2,1)S(1)} all-to-all(bf16[8,64,1024]{2,1,0:T(8,128)(2,1)S(1)} %bitcast.20), channel_id=1, replica_groups=mesh['zh'=4,'zl'=2,'yh'=4,'core'=2,'x'=4,'yl'=2] {'x','yl'}, dimensions={0} | all-to-all | bytes 2097152 | tf_op jit(solution)/shard_map/all_to_all | solution.py:29
  21.3 0.2 units.1
  21.5 10.3 %all_to_all.35 = bf16[8,64,512]{2,1,0:T(8,128)(2,1)S(1)} all-to-all(bf16[8,64,512]{2,1,0:T(8,128)(2,1)S(1)} %get-tuple-element.21), channel_id=1, replica_groups=mesh['zh'=4,'zl'=2,'yh'=4,'core'=2,'x'=4,'yl'=2] {'x','yl'}, dimensions={0} | all-to-all | bytes 1048576 | tf_op jit(solution)/shard_map/all_to_all | solution.py:29
  31.8 1.3 cosines.1
  33.1 10.5 %all_to_all.36.pulls_ref = bf16[8,72,512]{2,1,0:T(8,128)(2,1)S(1)} all-to-all(bf16[8,72,512]{2,1,0:T(8,128)(2,1)S(1)} %get-tuple-element.23), channel_id=1, replica_groups=mesh['zh'=4,'zl'=2,'yh'=4,'core'=2,'x'=4,'yl'=2] {'x','yl'}, dimensions={0} | all-to-all | bytes 1179648 | tf_op jit(solution)/shard_map/all_to_all | solution.py:29
  43.6 0.6 raw_grads.1
  44.2 10.0 %all_to_all.37 = bf16[8,64,512]{2,1,0:T(8,128)(2,1)S(1)} all-to-all(bf16[8,64,512]{2,1,0:T(8,128)(2,1)S(1)} %get-tuple-element.26), channel_id=1, replica_groups=mesh['zh'=4,'zl'=2,'yh'=4,'core'=2,'x'=4,'yl'=2] {'x','yl'}, dimensions={0} | all-to-all | bytes 1048576 | tf_op jit(solution)/shard_map/all_to_all | solution.py:29
  54.1 0.6 parts.5
  54.7 10.0 %collective-permute-start = (bf16[16,136,128]{2,1,0:T(8,128)(2,1)S(1)}, bf16[16,136,128]{2,1,0:T(8,128)(2,1)S(1)}, u32[]{:S(2)}, u32[]{:S(2)}) collective-permute-start(bf16[16,136,128]{2,1,0:T(8,128)(2,1)S(1)} %parts.5), channel_id=1, source_target_pairs={{0,8},{8,0},{1,9},{9,1},{2,10},{10,2},{3,11},{11,3},{4,12},{12,4},... | collective-permute-start | bytes 1671176 | tf_op jit(solution)/shard_map/ppermute | solution.py:474
  64.7 0.6 parts.4
  65.3 1.0 collective-permute-done
  66.3 0.1 add_convert_fusion.1
  66.4 11.1 %collective-permute-start.1 = (bf16[16,136,128]{2,1,0:T(8,128)(2,1)S(1)}, bf16[16,136,128]{2,1,0:T(8,128)(2,1)S(1)}, u32[]{:S(2)}, u32[]{:S(2)}) collective-permute-start(bf16[16,136,128]{2,1,0:T(8,128)(2,1)S(1)} %add_convert_fusion.1), channel_id=1, source_target_pairs={{0,64},{8,456},{64,0},{72,136},{128,192},{136,72},{192,128},{200,2... | collective-permute-start | bytes 1671176 | tf_op jit(solution)/shard_map/ppermute | solution.py:477
  77.5 0.6 parts.7
  78.1 1.9 %collective-permute-start.2 = (bf16[16,136,128]{2,1,0:T(8,128)(2,1)S(1)}, bf16[16,136,128]{2,1,0:T(8,128)(2,1)S(1)}, u32[]{:S(2)}, u32[]{:S(2)}) collective-permute-start(bf16[16,136,128]{2,1,0:T(8,128)(2,1)S(1)} %parts.7), channel_id=1, source_target_pairs={{0,8},{8,0},{1,9},{9,1},{2,10},{10,2},{3,11},{11,3},{4,12},{12,4},... | collective-permute-start | bytes 1671176 | tf_op jit(solution)/shard_map/ppermute | solution.py:479
  80.0 0.6 parts.6
  80.6 3.8 %collective-permute-done.1 = bf16[16,136,128]{2,1,0:T(8,128)(2,1)S(1)} collective-permute-done((bf16[16,136,128]{2,1,0:T(8,128)(2,1)S(1)}, bf16[16,136,128]{2,1,0:T(8,128)(2,1)S(1)}, u32[]{:S(2)}, u32[]{:S(2)}) %collective-permute-start.1) | collective-permute-done | bytes 557088 | tf_op jit(solution)/shard_map/ppermute | solution.py:477
  84.4 0.1 convert_add_fusion
  84.5 0.1 add_convert_fusion
  84.6 28.7 %all_to_all.38 = bf16[16,136,128]{2,1,0:T(8,128)(2,1)S(1)} all-to-all(bf16[16,136,128]{2,1,0:T(8,128)(2,1)S(1)} %add_convert_fusion), channel_id=1, replica_groups=mesh['zh'=4,'zl'=2,'yh'=4,'core'=2,'x'=4,'yl'=2] {'zh','yh'}, dimensions={0} | all-to-all | bytes 1114112 | tf_op jit(solution)/shard_map/all_to_all | solution.py:29
  113.3 0.1 reduce_sum.12
  113.4 0.1 broadcast_in_dim.3
  113.5 27.1 %all_to_all.39.refs_0_ = bf16[16,136,128]{2,1,0:T(8,128)(2,1)S(1)} all-to-all(bf16[16,136,128]{2,1,0:T(8,128)(2,1)S(1)} %broadcast_in_dim.3), channel_id=1, replica_groups=mesh['zh'=4,'zl'=2,'yh'=4,'core'=2,'x'=4,'yl'=2] {'zh','yh'}, dimensions={0} | all-to-all | bytes 1114112 | tf_op jit(solution)/shard_map/all_to_all | solution.py:29
  140.5 3.4 %collective-permute-start.3 = (bf16[16,136,128]{2,1,0:T(8,128)(2,1)S(1)}, bf16[16,136,128]{2,1,0:T(8,128)(2,1)S(1)}, u32[]{:S(2)}, u32[]{:S(2)}) collective-permute-start(bf16[16,136,128]{2,1,0:T(8,128)(2,1)S(1)} %all_to_all.39.refs_0_), channel_id=1, source_target_pairs={{0,64},{8,456},{64,0},{72,136},{128,192},{136,72},{192,128},{200,2... | collective-permute-start | bytes 1671176 | tf_op jit(solution)/shard_map/ppermute | solution.py:487
  143.9 3.0 %collective-permute-start.5 = (bf16[16,136,128]{2,1,0:T(8,128)(2,1)S(1)}, bf16[16,136,128]{2,1,0:T(8,128)(2,1)S(1)}, u32[]{:S(2)}, u32[]{:S(2)}) collective-permute-start(bf16[16,136,128]{2,1,0:T(8,128)(2,1)S(1)} %all_to_all.39.refs_0_), channel_id=1, source_target_pairs={{0,8},{8,0},{1,9},{9,1},{2,10},{10,2},{3,11},{11,3},{4,12},{12,4},... | collective-permute-start | bytes 1671176 | tf_op jit(solution)/shard_map/ppermute | solution.py:488
  146.9 0.9 assemble.3
  147.8 4.2 %collective-permute-done.3.refs_0_ = bf16[16,136,128]{2,1,0:T(8,128)(2,1)S(1)} collective-permute-done((bf16[16,136,128]{2,1,0:T(8,128)(2,1)S(1)}, bf16[16,136,128]{2,1,0:T(8,128)(2,1)S(1)}, u32[]{:S(2)}, u32[]{:S(2)}) %collective-permute-start.3) | collective-permute-done | bytes 557088 | tf_op jit(solution)/shard_map/ppermute | solution.py:487
  152.0 3.4 %collective-permute-start.4 = (bf16[16,136,128]{2,1,0:T(8,128)(2,1)S(1)}, bf16[16,136,128]{2,1,0:T(8,128)(2,1)S(1)}, u32[]{:S(2)}, u32[]{:S(2)}) collective-permute-start(bf16[16,136,128]{2,1,0:T(8,128)(2,1)S(1)} %collective-permute-done.3.refs_0_), channel_id=1, source_target_pairs={{0,8},{8,0},{1,9},{9,1},{2,10},{10,2},{3,11},{11,3},{4,12},{12,4},... | collective-permute-start | bytes 1671176 | tf_op jit(solution)/shard_map/ppermute | solution.py:491
  155.4 1.1 assemble.4
  156.5 0.5 collective-permute-done.4.refs_0_
  156.9 0.9 assemble.5
  (8 shorter events, 0.0 us)
Async XLA Ops:
  21.3 10.5 %copy-start.2 = (s32[512]{0:T(512)S(1)}, s32[512]{0:T(512)}, u32[]{:S(2)}) copy-start(s32[512]{0:T(512)} %param.7) | copy-start | bytes 6148
  33.1 21.1 %copy-start.1 = (bf16[512,512]{1,0:T(8,128)(2,1)S(1)}, bf16[512,512]{1,0:T(8,128)(2,1)}, u32[]{:S(2)}) copy-start(bf16[512,512]{1,0:T(8,128)(2,1)} %class_ref.9) | copy-start | bytes 1572868
  43.6 10.5 %copy-start = (bf16[512,1568]{0,1:T(8,128)(2,1)S(1)}, bf16[512,1568]{0,1:T(8,128)(2,1)}, u32[]{:S(2)}) copy-start(bf16[512,1568]{0,1:T(8,128)(2,1)} %param.4) | copy-start | bytes 4816900
  54.7 11.6 %collective-permute-start = (bf16[16,136,128]{2,1,0:T(8,128)(2,1)S(1)}, bf16[16,136,128]{2,1,0:T(8,128)(2,1)S(1)}, u32[]{:S(2)}, u32[]{:S(2)}) collective-permute-start(bf16[16,136,128]{2,1,0:T(8,128)(2,1)S(1)} %parts.5), channel_id=1, source_target_pairs={{0,8},{8,0},{1,9},{9,1},{2,10},{10,2},{3,11},{11,3},{4,12},{12,4},... | collective-permute-start | bytes 1671176 | tf_op jit(solution)/shard_map/ppermute | solution.py:474
  66.4 18.0 %collective-permute-start.1 = (bf16[16,136,128]{2,1,0:T(8,128)(2,1)S(1)}, bf16[16,136,128]{2,1,0:T(8,128)(2,1)S(1)}, u32[]{:S(2)}, u32[]{:S(2)}) collective-permute-start(bf16[16,136,128]{2,1,0:T(8,128)(2,1)S(1)} %add_convert_fusion.1), channel_id=1, source_target_pairs={{0,64},{8,456},{64,0},{72,136},{128,192},{136,72},{192,128},{200,2... | collective-permute-start | bytes 1671176 | tf_op jit(solution)/shard_map/ppermute | solution.py:477
  78.1 6.4 %collective-permute-start.2 = (bf16[16,136,128]{2,1,0:T(8,128)(2,1)S(1)}, bf16[16,136,128]{2,1,0:T(8,128)(2,1)S(1)}, u32[]{:S(2)}, u32[]{:S(2)}) collective-permute-start(bf16[16,136,128]{2,1,0:T(8,128)(2,1)S(1)} %parts.7), channel_id=1, source_target_pairs={{0,8},{8,0},{1,9},{9,1},{2,10},{10,2},{3,11},{11,3},{4,12},{12,4},... | collective-permute-start | bytes 1671176 | tf_op jit(solution)/shard_map/ppermute | solution.py:479
  140.5 11.5 %collective-permute-start.3 = (bf16[16,136,128]{2,1,0:T(8,128)(2,1)S(1)}, bf16[16,136,128]{2,1,0:T(8,128)(2,1)S(1)}, u32[]{:S(2)}, u32[]{:S(2)}) collective-permute-start(bf16[16,136,128]{2,1,0:T(8,128)(2,1)S(1)} %all_to_all.39.refs_0_), channel_id=1, source_target_pairs={{0,64},{8,456},{64,0},{72,136},{128,192},{136,72},{192,128},{200,2... | collective-permute-start | bytes 1671176 | tf_op jit(solution)/shard_map/ppermute | solution.py:487
  143.9 11.4 %collective-permute-start.5 = (bf16[16,136,128]{2,1,0:T(8,128)(2,1)S(1)}, bf16[16,136,128]{2,1,0:T(8,128)(2,1)S(1)}, u32[]{:S(2)}, u32[]{:S(2)}) collective-permute-start(bf16[16,136,128]{2,1,0:T(8,128)(2,1)S(1)} %all_to_all.39.refs_0_), channel_id=1, source_target_pairs={{0,8},{8,0},{1,9},{9,1},{2,10},{10,2},{3,11},{11,3},{4,12},{12,4},... | collective-permute-start | bytes 1671176 | tf_op jit(solution)/shard_map/ppermute | solution.py:488
  152.0 4.9 %collective-permute-start.4 = (bf16[16,136,128]{2,1,0:T(8,128)(2,1)S(1)}, bf16[16,136,128]{2,1,0:T(8,128)(2,1)S(1)}, u32[]{:S(2)}, u32[]{:S(2)}) collective-permute-start(bf16[16,136,128]{2,1,0:T(8,128)(2,1)S(1)} %collective-permute-done.3.refs_0_), channel_id=1, source_target_pairs={{0,8},{8,0},{1,9},{9,1},{2,10},{10,2},{3,11},{11,3},{4,12},{12,4},... | collective-permute-start | bytes 1671176 | tf_op jit(solution)/shard_map/ppermute | solution.py:491

commit v9 on v8

--- a/solution.py
+++ b/solution.py
@@ -102,18 +102,57 @@
     return jnp.transpose(jnp.broadcast_to(labels_row, (LANES, faces)))
 
 
-def embed_kernel(
-    place_ref, features_ref, fc_ref, class_ref, labels_ref, sent_ref, unit_ref,
-    left_ref, right_ref, total_ref, weight_ref, row_ref, sems
-):
-    width = fc_ref.shape[1]
-    inputs, faces = features_ref.shape
-    classes = class_ref.shape[0]
+def bit_of(place_ref, level):
+    return lax.rem(lax.div(place_ref[0], 4 << level), 2)
+
+
+def targets_kernel(place_ref, class_ref, labels_ref, keep_ref, send_ref, unit_ref, rows_ref):
+    classes, width = class_ref.shape
+    faces = labels_ref.shape[1]
+    class_f = class_ref[...].astype(jnp.float32)
+    unit_ref[...] = (class_f * (1.0 / row_norm(class_f))).astype(jnp.bfloat16)
+    labels = spread_labels(labels_ref[...])
+    chosen = target_mask(first_of(place_ref, classes), labels, faces, classes)
+    chosen = jnp.where(chosen, 1.0, 0.0).astype(jnp.bfloat16)
+    rows = jnp.dot(chosen, unit_ref[...], preferred_element_type=jnp.float32)
+    rows_ref[...] = rows.astype(jnp.bfloat16).reshape(rows_ref.shape)
+    bit = bit_of(place_ref, 0)
+    for at in range(keep_ref.shape[0]):
+        keep_ref[at] = rows_ref[2 * at + bit]
+        send_ref[at] = rows_ref[2 * at + 1 - bit]
+
+
+def target_rows(place, class_weight, labels, peers):
+    classes, width = class_weight.shape
+    faces = labels.shape[1]
+    half = ((peers // 2, faces // peers, width), jnp.bfloat16)
+    return call(
+        targets_kernel,
+        "targets",
+        (place, class_weight, labels),
+        [half, half, ((classes, width), jnp.bfloat16)],
+        scratch_shapes=[pltpu.VMEM((peers, faces // peers, width), jnp.bfloat16)],
+    )
+
+
+def halve_kernel(level, place_ref, kept_ref, got_ref, keep_ref, send_ref):
+    bit = bit_of(place_ref, level)
+    for at in range(keep_ref.shape[0]):
+        keep_ref[at] = kept_ref[2 * at + bit] + got_ref[2 * at + bit]
+        send_ref[at] = kept_ref[2 * at + 1 - bit] + got_ref[2 * at + 1 - bit]
+
+
+def halve(level, place, kept, got):
+    half = ((kept.shape[0] // 2,) + kept.shape[1:], kept.dtype)
+    return call(
+        functools.partial(halve_kernel, level), "halve", (place, kept, got), [half, half]
+    )
+
+
+def embed_kernel(features_ref, fc_ref, sent_ref, left_ref, right_ref, total_ref, sems):
+    inputs = features_ref.shape[0]
     ends = [inputs * at // CHUNKS // LANES * LANES for at in range(CHUNKS)] + [inputs]
-    copies = [
-        pltpu.make_async_copy(labels_ref, row_ref, sems.at[0]),
-        pltpu.make_async_copy(class_ref, weight_ref, sems.at[1]),
-    ]
+    copies = []
     for at in range(CHUNKS):
         rows = pl.ds(ends[at], ends[at + 1] - ends[at])
         for source, target in ((features_ref, left_ref), (fc_ref, right_ref)):
@@ -124,20 +163,9 @@
             )
     for copy in copies:
         copy.start()
-
-    copies[0].wait()
-    labels = spread_labels(row_ref[...])
-    chosen = target_mask(first_of(place_ref, classes), labels, faces, classes)
-    chosen = jnp.where(chosen, 1.0, 0.0).astype(jnp.bfloat16)
-    copies[1].wait()
-    class_f = weight_ref[...].astype(jnp.float32)
-    unit_ref[...] = (class_f * (1.0 / row_norm(class_f))).astype(jnp.bfloat16)
-    target_part = jnp.dot(chosen, unit_ref[...], preferred_element_type=jnp.float32)
-    sent_ref[:, width:] = target_part.astype(jnp.bfloat16)
-
     for at in range(CHUNKS):
-        copies[2 + 2 * at].wait()
-        copies[3 + 2 * at].wait()
+        copies[2 * at].wait()
+        copies[2 * at + 1].wait()
         here = slice(ends[at], ends[at + 1])
         part = across(left_ref[here, :], right_ref[here, :])
         if at > 0:
@@ -145,55 +173,43 @@
         if at < CHUNKS - 1:
             total_ref[...] = part
         else:
-            sent_ref[:, :width] = part.astype(jnp.bfloat16)
-
-
-def embed(place, features, fc_weight, class_weight, labels):
+            sent_ref[...] = part.astype(jnp.bfloat16)
+
+
+def embed(features, fc_weight):
     inputs, faces = features.shape
-    classes, width = class_weight.shape
-    arrays = [placed(array, pltpu.HBM) for array in (features, fc_weight, class_weight, labels)]
+    width = fc_weight.shape[1]
+    arrays = [placed(array, pltpu.HBM) for array in (features, fc_weight)]
     return pl.pallas_call(
         embed_kernel,
-        in_specs=[SMEM] + [pl.BlockSpec(memory_space=pltpu.HBM)] * len(arrays),
-        out_specs=[VMEM, VMEM],
-        out_shape=[
-            pltpu.VMEM((faces, 2 * width), jnp.bfloat16),
-            pltpu.VMEM((classes, width), jnp.bfloat16),
-        ],
+        in_specs=[pl.BlockSpec(memory_space=pltpu.HBM)] * len(arrays),
+        out_specs=VMEM,
+        out_shape=pltpu.VMEM((faces, width), jnp.bfloat16),
         scratch_shapes=[
             pltpu.VMEM((inputs, faces), jnp.bfloat16),
             pltpu.VMEM((inputs, width), jnp.bfloat16),
             pltpu.VMEM((faces, width), jnp.float32),
-            pltpu.VMEM((classes, width), jnp.bfloat16),
-            pltpu.VMEM((1, faces), jnp.int32),
-            pltpu.SemaphoreType.DMA((2 + 2 * CHUNKS,)),
+            pltpu.SemaphoreType.DMA((2 * CHUNKS,)),
         ],
         compiler_params=pltpu.CompilerParams(vmem_limit_bytes=LIMIT),
         name="embed",
-    )(place, *arrays)
-
-
-def units_kernel(got_ref, raw_ref, target_ref, sent_ref):
-    width = raw_ref.shape[1]
-    got = got_ref[0].astype(jnp.float32)
+    )(*arrays)
+
+
+def units_kernel(got_ref, raw_ref, sent_ref):
+    raw_embed = got_ref[0].astype(jnp.float32)
     for peer in range(1, got_ref.shape[0]):
-        got = got + got_ref[peer].astype(jnp.float32)
-    raw_embed = got[:, :width]
+        raw_embed = raw_embed + got_ref[peer].astype(jnp.float32)
     raw_ref[...] = raw_embed
-    target_ref[...] = got[:, width:]
     unit = (raw_embed * (1.0 / row_norm(raw_embed))).astype(jnp.bfloat16)
     for copy in range(sent_ref.shape[0]):
         sent_ref[copy] = unit
 
 
 def unit_rows(got):
-    peers, owned, both = got.shape
-    rows = (owned, both // 2)
+    rows = got.shape[1:]
     return call(
-        units_kernel,
-        "units",
-        (got,),
-        [(rows, jnp.float32), (rows, jnp.float32), ((peers,) + rows, jnp.bfloat16)],
+        units_kernel, "units", (got,), [(rows, jnp.float32), (got.shape, jnp.bfloat16)]
     )
 
 
@@ -256,7 +272,7 @@
 
 
 def raw_grad_kernel(
-    loss_weight, place_ref, pulls_ref, raw_ref, target_ref, sent_ref, scales_ref
+    loss_weight, place_ref, pulls_ref, raw_ref, kept_ref, got_ref, sent_ref, scales_ref
 ):
     owned, width = raw_ref.shape
     pulls = pulls_ref[0].astype(jnp.float32)
@@ -272,7 +288,8 @@
     scales = scales_ref[own, :]
     pull_scale, rest_scale = scales[:, 0:1], scales[:, 1:2]
 
-    raw_embed, target = raw_ref[...], target_ref[...]
+    raw_embed = raw_ref[...]
+    target = (kept_ref[0] + got_ref[0]).astype(jnp.float32)
     inverse_norm = 1.0 / row_norm(raw_embed)
     unit_f = raw_embed * inverse_norm
     unit = unit_f.astype(jnp.bfloat16).astype(jnp.float32)
@@ -286,13 +303,13 @@
         sent_ref[copy] = raw_grad
 
 
-def raw_grads(loss_weight, place, pulls, raw_embed, target_unit):
+def raw_grads(loss_weight, place, pulls, raw_embed, kept, got):
     peers = pulls.shape[0]
     owned, width = raw_embed.shape
     return call(
         functools.partial(raw_grad_kernel, loss_weight),
         "raw_grads",
-        (place, pulls, raw_embed, target_unit),
+        (place, pulls, raw_embed, kept, got),
         [((peers, owned, width), jnp.bfloat16), ((peers * owned, LANES), jnp.float32)],
     )
 
@@ -450,15 +467,23 @@
     place = place.reshape(1)
     labels = labels.reshape(1, faces)
 
-    sent, class_unit = embed(place, features, fc_weight, class_weight, labels)
-    got = exchange(sent, CLS).reshape(n_cls, faces // n_cls, 2 * width)
-    raw_embed, target_unit, sent = unit_rows(got)
+    swap = [(0, 1), (1, 0)]
+    kept, away, class_unit = target_rows(place, class_weight, labels, n_cls)
+    away = lax.ppermute(away, "yl", swap)
+    got = exchange(embed(features, fc_weight), CLS).reshape(n_cls, faces // n_cls, width)
+    got, kept, away = lax.optimization_barrier((got, kept, away))
+    raw_embed, sent = unit_rows(got)
+    kept, away = halve(1, place, kept, away)
+    away = lax.ppermute(away, "x", [(x, x ^ 1) for x in range(4)])
     units = exchange(sent, CLS)
+    units, kept, away = lax.optimization_barrier((units, kept, away))
     units = units.reshape(faces, width)
 
     pull, others = cosines(place, units, class_unit, labels, n_cls)
+    kept, away = halve(2, place, kept, away)
+    away = lax.ppermute(away, "x", [(x, x ^ 2) for x in range(4)])
     got = exchange(pull, CLS)
-    sent, scales = raw_grads(loss_weight, place, got, raw_embed, target_unit)
+    sent, scales = raw_grads(loss_weight, place, got, raw_embed, kept, away)
     grads = exchange(sent, CLS).reshape(faces, width)
 
     swap = [(0, 1), (1, 0)]

time: 158 us -> 168 us (1.063)
  blocking collectives: 104 us -> 66.8 us
  starting transfers between devices: 32.7 us -> 62.1 us
  waiting for transfers between devices: 9.53 us -> 22.3 us
  Pallas kernels: 10.1 us -> 14 us
    all_to_all x6 -> x3, blocking collectives: 104 us -> 66.8 us  [exchange(): return lax.all_to_all(blocks, axes, 0, 0, tiled=True)]
    all_to_all x0 -> x3, starting transfers between devices: none -> 15.5 us  [exchange(): return lax.all_to_all(blocks, axes, 0, 0, tiled=True)]
    ppermute x0 -> x3, starting transfers between devices: none -> 11.6 us  [the longest x1 4.87 us: shards(): away = lax.ppermute(away, 'x', [(x, x ^ 2) for x in range(4)])]
    ppermute x0 -> x3, waiting for transfers between devices: none -> 11.4 us  [the longest x1 5.36 us: shards(): away = lax.ppermute(away, 'yl', swap)]
    pallas_call x7 -> x10, Pallas kernels: 4.37 us -> 7.76 us  [call(): pl.pallas_call(kernel, in_specs=specs, out_specs=[VMEM] * len(results), o...]
  transfers between devices with their start and end apart: 6 -> 12, of which waited for: 4 -> 9; matrix products, arithmetic and copies ran while one was open for 0% -> 0% of each run, Pallas kernels for 2% -> 3%
where the time goes in v9:
time: 168 us
  blocking collectives  66.8 us (40%)
  starting transfers between devices  62.1 us (37%)
  waiting for transfers between devices  22.3 us (13%)
  Pallas kernels  14 us (8%)
    all_to_all x3, blocking collectives, exchange(): return lax.all_to_all(blocks, axes, 0, 0, tiled=True)  66.8 us
    all_to_all x3, starting transfers between devices, exchange(): return lax.all_to_all(blocks, axes, 0, 0, tiled=True)  15.5 us
    ppermute x1, starting transfers between devices, shards(): got = lax.ppermute(sent, neighbour, pairs)  12.7 us
    ppermute x2, starting transfers between devices, shards(): theirs = lax.ppermute(theirs, 'core', swap)  12.7 us
    pallas_call x10, Pallas kernels, call(): pl.pallas_call(kernel, in_specs=specs, out_specs=[VMEM] * len(results), o...  7.76 us
    ppermute x1, waiting for transfers between devices, shards(): away = lax.ppermute(away, 'yl', swap)  5.36 us
    ppermute x1, starting transfers between devices, shards(): away = lax.ppermute(away, 'x', [(x, x ^ 2) for x in range(4)])  4.87 us
    ppermute x1, waiting for transfers between devices, shards(): next_mine = lax.ppermute(mine, neighbour, pairs)  4.4 us
  transfers between devices with their start and end apart: 12, of which 9 were waited for; matrix products, arithmetic and copies ran while one was open for 0% of the time, Pallas kernels for 3%

profile of v9, /device:TPU:1, one launch (start us, length us, event | category | flops | bytes accessed | tf_op | source)
XLA Modules:
  0.0 167.6 jit_solution(11833934746213375794)
XLA Ops:
  0.6 3.4 %embed.1 = bf16[512,512]{1,0:T(8,128)(2,1)} custom-call(bf16[1568,512]{1,0:T(8,128)(2,1)} %bitcast.6, bf16[1568,512]{1,0:T(8,128)(2,1)} %fc_ref.1), custom_call_target="tpu_custom_call" | custom-call | tf_op jit(solution)/shard_map/embed/pallas_call | solution.py:183
  4.1 6.0 %all-to-all-start = ((bf16[8,64,512]{2,1,0:T(8,128)(2,1)}), bf16[8,64,512]{2,1,0:T(8,128)(2,1)S(1)}, u32[]{:S(2)}, u32[]{:S(2)}) async-start(bf16[8,64,512]{2,1,0:T(8,128)(2,1)} %bitcast.2), calls=%async_computation | async-start | bytes 1048576 | tf_op jit(solution)/shard_map/all_to_all | solution.py:29
  10.1 0.7 targets.1
  10.8 3.4 %collective-permute-start = (bf16[4,64,512]{2,1,0:T(8,128)(2,1)S(1)}, bf16[4,64,512]{2,1,0:T(8,128)(2,1)S(1)}, u32[]{:S(2)}, u32[]{:S(2)}) collective-permute-start(bf16[4,64,512]{2,1,0:T(8,128)(2,1)S(1)} %get-tuple-element.31), channel_id=1, source_target_pairs={{0,1},{1,0},{2,3},{3,2},{4,5},{5,4},{6,7},{7,6},{8,9},{9,8},{10,11... | collective-permute-start | bytes 786440 | tf_op jit(solution)/shard_map/ppermute | solution.py:472
  14.2 5.4 %collective-permute-done.got_ref = bf16[4,64,512]{2,1,0:T(8,128)(2,1)S(1)} collective-permute-done((bf16[4,64,512]{2,1,0:T(8,128)(2,1)S(1)}, bf16[4,64,512]{2,1,0:T(8,128)(2,1)S(1)}, u32[]{:S(2)}, u32[]{:S(2)}) %collective-permute-start) | collective-permute-done | bytes 262176 | tf_op jit(solution)/shard_map/ppermute | solution.py:472
  19.6 1.0 units.1
  20.5 5.3 %all-to-all-start.1 = ((bf16[8,64,512]{2,1,0:T(8,128)(2,1)}), bf16[8,64,512]{2,1,0:T(8,128)(2,1)S(1)}, u32[]{:S(2)}, u32[]{:S(2)}) async-start(bf16[8,64,512]{2,1,0:T(8,128)(2,1)} %get-tuple-element.33), calls=%async_computation.1 | async-start | bytes 1048576 | tf_op jit(solution)/shard_map/all_to_all | solution.py:29
  25.8 3.4 %collective-permute-start.1 = (bf16[2,64,512]{2,1,0:T(8,128)(2,1)S(1)}, bf16[2,64,512]{2,1,0:T(8,128)(2,1)S(1)}, u32[]{:S(2)}, u32[]{:S(2)}) collective-permute-start(bf16[2,64,512]{2,1,0:T(8,128)(2,1)S(1)} %get-tuple-element.37), channel_id=1, source_target_pairs={{0,2},{2,0},{4,6},{6,4},{1,3},{3,1},{5,7},{7,5},{8,10},{10,8},{12,... | collective-permute-start | bytes 393224 | tf_op jit(solution)/shard_map/ppermute | solution.py:477
  29.2 3.6 %collective-permute-done.1.got_ref = bf16[2,64,512]{2,1,0:T(8,128)(2,1)S(1)} collective-permute-done((bf16[2,64,512]{2,1,0:T(8,128)(2,1)S(1)}, bf16[2,64,512]{2,1,0:T(8,128)(2,1)S(1)}, u32[]{:S(2)}, u32[]{:S(2)}) %collective-permute-start.1) | collective-permute-done | bytes 131104 | tf_op jit(solution)/shard_map/ppermute | solution.py:477
  33.3 2.1 %cosines.1 = (bf16[8,72,512]{2,1,0:T(8,128)(2,1)}, f32[512,512]{1,0:T(8,128)S(1)}) custom-call(s32[1]{0:T(128)} %bitcast.place_ref, bf16[512,512]{1,0:T(8,128)(2,1)S(1)} %bitcast.11, bf16[512,512]{1,0:T(8,128)(2,1)S(1)} %get-tuple-element.39.class_ref, s32[1,512]{1,0:T(1,128)S(1)} %bitcast.21), custom_call_target="tpu_custom_call" | custom-call | tf_op jit(solution)/shard_map/cosines/pallas_call | solution.py:82
  35.5 4.2 %all-to-all-start.2 = ((bf16[8,72,512]{2,1,0:T(8,128)(2,1)}), bf16[8,72,512]{2,1,0:T(8,128)(2,1)}, u32[]{:S(2)}, u32[]{:S(2)}) async-start(bf16[8,72,512]{2,1,0:T(8,128)(2,1)} %get-tuple-element.40), calls=%async_computation.2 | async-start | bytes 1179648 | tf_op jit(solution)/shard_map/all_to_all | solution.py:29
  39.7 4.9 %collective-permute-start.2 = (bf16[1,64,512]{2,1,0:T(8,128)(2,1)S(1)}, bf16[1,64,512]{2,1,0:T(8,128)(2,1)S(1)}, u32[]{:S(2)}, u32[]{:S(2)}) collective-permute-start(bf16[1,64,512]{2,1,0:T(8,128)(2,1)S(1)} %get-tuple-element.45), channel_id=1, source_target_pairs={{0,4},{2,6},{4,0},{6,2},{1,5},{3,7},{5,1},{7,3},{8,12},{10,14},{12... | collective-permute-start | bytes 196616 | tf_op jit(solution)/shard_map/ppermute | solution.py:484
  44.6 2.5 %collective-permute-done.2.got_ref = bf16[1,64,512]{2,1,0:T(8,128)(2,1)S(1)} collective-permute-done((bf16[1,64,512]{2,1,0:T(8,128)(2,1)S(1)}, bf16[1,64,512]{2,1,0:T(8,128)(2,1)S(1)}, u32[]{:S(2)}, u32[]{:S(2)}) %collective-permute-start.2) | collective-permute-done | bytes 65568 | tf_op jit(solution)/shard_map/ppermute | solution.py:484
  47.1 0.7 all-to-all-done.2.pulls_ref
  47.8 1.0 copy-done.4
  48.7 1.7 raw_grads.1
  50.4 10.9 %all_to_all.34 = bf16[8,64,512]{2,1,0:T(8,128)(2,1)S(1)} all-to-all(bf16[8,64,512]{2,1,0:T(8,128)(2,1)S(1)} %get-tuple-element.46), channel_id=1, replica_groups=mesh['zh'=4,'zl'=2,'yh'=4,'core'=2,'x'=4,'yl'=2] {'x','yl'}, dimensions={0} | all-to-all | bytes 1048576 | tf_op jit(solution)/shard_map/all_to_all | solution.py:29
  61.9 10.8 %collective-permute-start.3 = (bf16[16,136,128]{2,1,0:T(8,128)(2,1)S(1)}, bf16[16,136,128]{2,1,0:T(8,128)(2,1)S(1)}, u32[]{:S(2)}, u32[]{:S(2)}) collective-permute-start(bf16[16,136,128]{2,1,0:T(8,128)(2,1)S(1)} %parts.5), channel_id=1, source_target_pairs={{0,8},{8,0},{1,9},{9,1},{2,10},{10,2},{3,11},{11,3},{4,12},{12,4},... | collective-permute-start | bytes 1671176 | tf_op jit(solution)/shard_map/ppermute | solution.py:499
  72.7 0.6 parts.4
  73.3 1.0 collective-permute-done.3
  74.4 12.7 %collective-permute-start.4 = (bf16[16,136,128]{2,1,0:T(8,128)(2,1)S(1)}, bf16[16,136,128]{2,1,0:T(8,128)(2,1)S(1)}, u32[]{:S(2)}, u32[]{:S(2)}) collective-permute-start(bf16[16,136,128]{2,1,0:T(8,128)(2,1)S(1)} %add_convert_fusion.1), channel_id=1, source_target_pairs={{0,64},{8,456},{64,0},{72,136},{128,192},{136,72},{192,128},{200,2... | collective-permute-start | bytes 1671176 | tf_op jit(solution)/shard_map/ppermute | solution.py:502
  87.7 1.9 %collective-permute-start.5 = (bf16[16,136,128]{2,1,0:T(8,128)(2,1)S(1)}, bf16[16,136,128]{2,1,0:T(8,128)(2,1)S(1)}, u32[]{:S(2)}, u32[]{:S(2)}) collective-permute-start(bf16[16,136,128]{2,1,0:T(8,128)(2,1)S(1)} %parts.7), channel_id=1, source_target_pairs={{0,8},{8,0},{1,9},{9,1},{2,10},{10,2},{3,11},{11,3},{4,12},{12,4},... | collective-permute-start | bytes 1671176 | tf_op jit(solution)/shard_map/ppermute | solution.py:504
  90.2 3.8 %collective-permute-done.4 = bf16[16,136,128]{2,1,0:T(8,128)(2,1)S(1)} collective-permute-done((bf16[16,136,128]{2,1,0:T(8,128)(2,1)S(1)}, bf16[16,136,128]{2,1,0:T(8,128)(2,1)S(1)}, u32[]{:S(2)}, u32[]{:S(2)}) %collective-permute-start.4) | collective-permute-done | bytes 557088 | tf_op jit(solution)/shard_map/ppermute | solution.py:502
  94.3 28.9 %all_to_all.35 = bf16[16,136,128]{2,1,0:T(8,128)(2,1)S(1)} all-to-all(bf16[16,136,128]{2,1,0:T(8,128)(2,1)S(1)} %add_convert_fusion), channel_id=1, replica_groups=mesh['zh'=4,'zl'=2,'yh'=4,'core'=2,'x'=4,'yl'=2] {'zh','yh'}, dimensions={0} | all-to-all | bytes 1114112 | tf_op jit(solution)/shard_map/all_to_all | solution.py:29
  123.4 26.9 %all_to_all.36.refs_0_ = bf16[16,136,128]{2,1,0:T(8,128)(2,1)S(1)} all-to-all(bf16[16,136,128]{2,1,0:T(8,128)(2,1)S(1)} %broadcast_in_dim.3), channel_id=1, replica_groups=mesh['zh'=4,'zl'=2,'yh'=4,'core'=2,'x'=4,'yl'=2] {'zh','yh'}, dimensions={0} | all-to-all | bytes 1114112 | tf_op jit(solution)/shard_map/all_to_all | solution.py:29
  150.3 3.2 %collective-permute-start.6 = (bf16[16,136,128]{2,1,0:T(8,128)(2,1)S(1)}, bf16[16,136,128]{2,1,0:T(8,128)(2,1)S(1)}, u32[]{:S(2)}, u32[]{:S(2)}) collective-permute-start(bf16[16,136,128]{2,1,0:T(8,128)(2,1)S(1)} %all_to_all.36.refs_0_), channel_id=1, source_target_pairs={{0,64},{8,456},{64,0},{72,136},{128,192},{136,72},{192,128},{200,2... | collective-permute-start | bytes 1671176 | tf_op jit(solution)/shard_map/ppermute | solution.py:512
  153.5 3.0 %collective-permute-start.8 = (bf16[16,136,128]{2,1,0:T(8,128)(2,1)S(1)}, bf16[16,136,128]{2,1,0:T(8,128)(2,1)S(1)}, u32[]{:S(2)}, u32[]{:S(2)}) collective-permute-start(bf16[16,136,128]{2,1,0:T(8,128)(2,1)S(1)} %all_to_all.36.refs_0_), channel_id=1, source_target_pairs={{0,8},{8,0},{1,9},{9,1},{2,10},{10,2},{3,11},{11,3},{4,12},{12,4},... | collective-permute-start | bytes 1671176 | tf_op jit(solution)/shard_map/ppermute | solution.py:513
  156.5 0.9 assemble.3
  157.4 4.4 %collective-permute-done.6.refs_0_ = bf16[16,136,128]{2,1,0:T(8,128)(2,1)S(1)} collective-permute-done((bf16[16,136,128]{2,1,0:T(8,128)(2,1)S(1)}, bf16[16,136,128]{2,1,0:T(8,128)(2,1)S(1)}, u32[]{:S(2)}, u32[]{:S(2)}) %collective-permute-start.6) | collective-permute-done | bytes 557088 | tf_op jit(solution)/shard_map/ppermute | solution.py:512
  161.8 3.4 %collective-permute-start.7 = (bf16[16,136,128]{2,1,0:T(8,128)(2,1)S(1)}, bf16[16,136,128]{2,1,0:T(8,128)(2,1)S(1)}, u32[]{:S(2)}, u32[]{:S(2)}) collective-permute-start(bf16[16,136,128]{2,1,0:T(8,128)(2,1)S(1)} %collective-permute-done.6.refs_0_), channel_id=1, source_target_pairs={{0,8},{8,0},{1,9},{9,1},{2,10},{10,2},{3,11},{11,3},{4,12},{12,4},... | collective-permute-start | bytes 1671176 | tf_op jit(solution)/shard_map/ppermute | solution.py:516
  165.2 1.1 assemble.4
  166.7 0.9 assemble.5
  (26 shorter events, 3.3 us)
Async XLA Ops:
  0.6 9.5 %copy-start.5 = (s32[512]{0:T(512)S(1)}, s32[512]{0:T(512)}, u32[]{:S(2)}) copy-start(s32[512]{0:T(512)} %param.7) | copy-start | bytes 6148
  4.1 6.0 %copy-start.1 = (bf16[512,512]{1,0:T(8,128)(2,1)S(1)}, bf16[512,512]{1,0:T(8,128)(2,1)}, u32[]{:S(2)}) copy-start(bf16[512,512]{1,0:T(8,128)(2,1)} %class_ref.9) | copy-start | bytes 1572868
  4.1 15.5 %all-to-all-start = ((bf16[8,64,512]{2,1,0:T(8,128)(2,1)}), bf16[8,64,512]{2,1,0:T(8,128)(2,1)S(1)}, u32[]{:S(2)}, u32[]{:S(2)}) async-start(bf16[8,64,512]{2,1,0:T(8,128)(2,1)} %bitcast.2), calls=%async_computation | async-start | bytes 1048576 | tf_op jit(solution)/shard_map/all_to_all | solution.py:29
  10.8 8.7 %collective-permute-start = (bf16[4,64,512]{2,1,0:T(8,128)(2,1)S(1)}, bf16[4,64,512]{2,1,0:T(8,128)(2,1)S(1)}, u32[]{:S(2)}, u32[]{:S(2)}) collective-permute-start(bf16[4,64,512]{2,1,0:T(8,128)(2,1)S(1)} %get-tuple-element.31), channel_id=1, source_target_pairs={{0,1},{1,0},{2,3},{3,2},{4,5},{5,4},{6,7},{7,6},{8,9},{9,8},{10,11... | collective-permute-start | bytes 786440 | tf_op jit(solution)/shard_map/ppermute | solution.py:472
  20.5 14.9 %copy-start.3 = (f32[64,512]{1,0:T(8,128)}, f32[64,512]{1,0:T(8,128)S(1)}, u32[]{:S(2)}) copy-start(f32[64,512]{1,0:T(8,128)S(1)} %get-tuple-element.41.raw_ref) | copy-start | bytes 393220
  20.5 12.8 %all-to-all-start.1 = ((bf16[8,64,512]{2,1,0:T(8,128)(2,1)}), bf16[8,64,512]{2,1,0:T(8,128)(2,1)S(1)}, u32[]{:S(2)}, u32[]{:S(2)}) async-start(bf16[8,64,512]{2,1,0:T(8,128)(2,1)} %get-tuple-element.33), calls=%async_computation.1 | async-start | bytes 1048576 | tf_op jit(solution)/shard_map/all_to_all | solution.py:29
  25.8 7.0 %collective-permute-start.1 = (bf16[2,64,512]{2,1,0:T(8,128)(2,1)S(1)}, bf16[2,64,512]{2,1,0:T(8,128)(2,1)S(1)}, u32[]{:S(2)}, u32[]{:S(2)}) collective-permute-start(bf16[2,64,512]{2,1,0:T(8,128)(2,1)S(1)} %get-tuple-element.37), channel_id=1, source_target_pairs={{0,2},{2,0},{4,6},{6,4},{1,3},{3,1},{5,7},{7,5},{8,10},{10,8},{12,... | collective-permute-start | bytes 393224 | tf_op jit(solution)/shard_map/ppermute | solution.py:477
  35.5 12.3 %all-to-all-start.2 = ((bf16[8,72,512]{2,1,0:T(8,128)(2,1)}), bf16[8,72,512]{2,1,0:T(8,128)(2,1)}, u32[]{:S(2)}, u32[]{:S(2)}) async-start(bf16[8,72,512]{2,1,0:T(8,128)(2,1)} %get-tuple-element.40), calls=%async_computation.2 | async-start | bytes 1179648 | tf_op jit(solution)/shard_map/all_to_all | solution.py:29
  39.7 21.7 %copy-start = (bf16[512,1568]{0,1:T(8,128)(2,1)S(1)}, bf16[512,1568]{0,1:T(8,128)(2,1)}, u32[]{:S(2)}) copy-start(bf16[512,1568]{0,1:T(8,128)(2,1)} %param.4) | copy-start | bytes 4816900
  39.7 7.3 %collective-permute-start.2 = (bf16[1,64,512]{2,1,0:T(8,128)(2,1)S(1)}, bf16[1,64,512]{2,1,0:T(8,128)(2,1)S(1)}, u32[]{:S(2)}, u32[]{:S(2)}) collective-permute-start(bf16[1,64,512]{2,1,0:T(8,128)(2,1)S(1)} %get-tuple-element.45), channel_id=1, source_target_pairs={{0,4},{2,6},{4,0},{6,2},{1,5},{3,7},{5,1},{7,3},{8,12},{10,14},{12... | collective-permute-start | bytes 196616 | tf_op jit(solution)/shard_map/ppermute | solution.py:484
  47.8 13.6 %copy-start.2 = (bf16[512,512]{1,0:T(8,128)(2,1)S(1)}, bf16[512,512]{1,0:T(8,128)(2,1)}, u32[]{:S(2)}) copy-start(bf16[512,512]{1,0:T(8,128)(2,1)} %class_ref.9) | copy-start | bytes 1572868
  47.8 1.0 copy-start.4
  61.9 12.4 %collective-permute-start.3 = (bf16[16,136,128]{2,1,0:T(8,128)(2,1)S(1)}, bf16[16,136,128]{2,1,0:T(8,128)(2,1)S(1)}, u32[]{:S(2)}, u32[]{:S(2)}) collective-permute-start(bf16[16,136,128]{2,1,0:T(8,128)(2,1)S(1)} %parts.5), channel_id=1, source_target_pairs={{0,8},{8,0},{1,9},{9,1},{2,10},{10,2},{3,11},{11,3},{4,12},{12,4},... | collective-permute-start | bytes 1671176 | tf_op jit(solution)/shard_map/ppermute | solution.py:499
  74.4 19.6 %collective-permute-start.4 = (bf16[16,136,128]{2,1,0:T(8,128)(2,1)S(1)}, bf16[16,136,128]{2,1,0:T(8,128)(2,1)S(1)}, u32[]{:S(2)}, u32[]{:S(2)}) collective-permute-start(bf16[16,136,128]{2,1,0:T(8,128)(2,1)S(1)} %add_convert_fusion.1), channel_id=1, source_target_pairs={{0,64},{8,456},{64,0},{72,136},{128,192},{136,72},{192,128},{200,2... | collective-permute-start | bytes 1671176 | tf_op jit(solution)/shard_map/ppermute | solution.py:502
  87.7 6.4 %collective-permute-start.5 = (bf16[16,136,128]{2,1,0:T(8,128)(2,1)S(1)}, bf16[16,136,128]{2,1,0:T(8,128)(2,1)S(1)}, u32[]{:S(2)}, u32[]{:S(2)}) collective-permute-start(bf16[16,136,128]{2,1,0:T(8,128)(2,1)S(1)} %parts.7), channel_id=1, source_target_pairs={{0,8},{8,0},{1,9},{9,1},{2,10},{10,2},{3,11},{11,3},{4,12},{12,4},... | collective-permute-start | bytes 1671176 | tf_op jit(solution)/shard_map/ppermute | solution.py:504
  150.3 11.5 %collective-permute-start.6 = (bf16[16,136,128]{2,1,0:T(8,128)(2,1)S(1)}, bf16[16,136,128]{2,1,0:T(8,128)(2,1)S(1)}, u32[]{:S(2)}, u32[]{:S(2)}) collective-permute-start(bf16[16,136,128]{2,1,0:T(8,128)(2,1)S(1)} %all_to_all.36.refs_0_), channel_id=1, source_target_pairs={{0,64},{8,456},{64,0},{72,136},{128,192},{136,72},{192,128},{200,2... | collective-permute-start | bytes 1671176 | tf_op jit(solution)/shard_map/ppermute | solution.py:512
  153.5 11.7 %collective-permute-start.8 = (bf16[16,136,128]{2,1,0:T(8,128)(2,1)S(1)}, bf16[16,136,128]{2,1,0:T(8,128)(2,1)S(1)}, u32[]{:S(2)}, u32[]{:S(2)}) collective-permute-start(bf16[16,136,128]{2,1,0:T(8,128)(2,1)S(1)} %all_to_all.36.refs_0_), channel_id=1, source_target_pairs={{0,8},{8,0},{1,9},{9,1},{2,10},{10,2},{3,11},{11,3},{4,12},{12,4},... | collective-permute-start | bytes 1671176 | tf_op jit(solution)/shard_map/ppermute | solution.py:513
  161.8 4.9 %collective-permute-start.7 = (bf16[16,136,128]{2,1,0:T(8,128)(2,1)S(1)}, bf16[16,136,128]{2,1,0:T(8,128)(2,1)S(1)}, u32[]{:S(2)}, u32[]{:S(2)}) collective-permute-start(bf16[16,136,128]{2,1,0:T(8,128)(2,1)S(1)} %collective-permute-done.6.refs_0_), channel_id=1, source_target_pairs={{0,8},{8,0},{1,9},{9,1},{2,10},{10,2},{3,11},{11,3},{4,12},{12,4},... | collective-permute-start | bytes 1671176 | tf_op jit(solution)/shard_map/ppermute | solution.py:516

commit v10 on v8

--- a/solution.py
+++ b/solution.py
@@ -19,7 +19,7 @@
 LANES = 128
 CHUNKS = 2
 MARK = 1024.0
-STEP = 256
+STEP = 512
 LIMIT = 24 << 20
 VMEM = pl.BlockSpec(memory_space=pltpu.VMEM)
 SMEM = pl.BlockSpec(memory_space=pltpu.SMEM)
@@ -364,6 +364,19 @@
     )[0]
 
 
+def total_kernel(got_ref, sent_ref):
+    total = got_ref[0].astype(jnp.float32)
+    for peer in range(1, got_ref.shape[0]):
+        total = total + got_ref[peer].astype(jnp.float32)
+    total = total.astype(jnp.bfloat16)
+    for copy in range(sent_ref.shape[0]):
+        sent_ref[copy] = total
+
+
+def totals(got):
+    return call(total_kernel, "totals", (got,), [(got.shape, jnp.bfloat16)])[0]
+
+
 def assemble_kernel(pieces, blocks, place_ref, *refs):
     sources = refs[: len(pieces)]
     fc_ref, class_ref, fc_rows, class_rows, over_rows, sems = refs[-6:]
@@ -480,10 +493,8 @@
     mine = parts((False, False), later, jnp.float32, *operands) + got.astype(jnp.float32)
     mine = lax.optimization_barrier(mine)
     mine = (mine + theirs.astype(jnp.float32)).astype(jnp.bfloat16)
-    done = jnp.sum(exchange(mine, CHIPS).astype(jnp.float32), axis=0).astype(jnp.bfloat16)
-
     sizes = (inputs, classes, width)
-    mine = exchange(jnp.broadcast_to(done, (chips,) + done.shape), CHIPS)
+    mine = exchange(totals(exchange(mine, CHIPS)), CHIPS)
     next_mine = lax.ppermute(mine, neighbour, pairs)
     across_mine = lax.ppermute(mine, "core", swap)
     written = assemble(place, blocks, sizes, {(False, False): mine}, ())

time: 158 us -> 158 us (level)
    pallas_call x7 -> x8, Pallas kernels: 4.37 us -> 4.44 us  [call(): pl.pallas_call(kernel, in_specs=specs, out_specs=[VMEM] * len(results), o...]
where the time goes in v10:
time: 158 us
  blocking collectives  104 us (66%)
  starting transfers between devices  32.5 us (21%)
  Pallas kernels  10.2 us (6%)
  waiting for transfers between devices  9.77 us (6%)
    all_to_all x6, blocking collectives, exchange(): return lax.all_to_all(blocks, axes, 0, 0, tiled=True)  104 us
    ppermute x2, starting transfers between devices, shards(): theirs = lax.ppermute(theirs, 'core', swap)  11.9 us
    ppermute x1, starting transfers between devices, shards(): got = lax.ppermute(sent, neighbour, pairs)  11.1 us
    ppermute x1, waiting for transfers between devices, shards(): next_mine = lax.ppermute(mine, neighbour, pairs)  4.48 us
    pallas_call x8, Pallas kernels, call(): pl.pallas_call(kernel, in_specs=specs, out_specs=[VMEM] * len(results), o...  4.44 us
    ppermute x1, waiting for transfers between devices, shards(): got = lax.ppermute(sent, neighbour, pairs)  3.84 us
    ppermute x1, starting transfers between devices, shards(): across_next = lax.ppermute(next_mine, 'core', swap)  3.36 us
    ppermute x1, starting transfers between devices, shards(): across_mine = lax.ppermute(mine, 'core', swap)  3.26 us
  transfers between devices with their start and end apart: 6, of which 4 were waited for; matrix products, arithmetic and copies ran while one was open for 0% of the time, Pallas kernels for 2%

profile of v10, /device:TPU:1, one launch (start us, length us, event | category | flops | bytes accessed | tf_op | source)
XLA Modules:
  0.0 157.8 jit_solution(5632367617343547587)
XLA Ops:
  0.6 2.9 %embed.1 = (bf16[512,1024]{1,0:T(8,128)(2,1)S(1)}, bf16[512,512]{1,0:T(8,128)(2,1)S(1)}) custom-call(s32[1]{0:T(128)} %bitcast.place_ref, bf16[1568,512]{1,0:T(8,128)(2,1)} %bitcast.6, bf16[1568,512]{1,0:T(8,128)(2,1)} %fc_ref.1, bf16[512,512]{1,0:T(8,128)(2,1)} %class_ref.9, s32[1,512]{1,0:T(1,128)} %bitcast.21), custom_call_target="tpu_custom_call" | custom-call | tf_op jit(solution)/shard_map/embed/pallas_call | solution.py:155
  3.6 17.7 %all_to_all.34.got_ref = bf16[8,64,1024]{2,1,0:T(8,128)(2,1)S(1)} all-to-all(bf16[8,64,1024]{2,1,0:T(8,128)(2,1)S(1)} %bitcast.20), channel_id=1, replica_groups=mesh['zh'=4,'zl'=2,'yh'=4,'core'=2,'x'=4,'yl'=2] {'x','yl'}, dimensions={0} | all-to-all | bytes 2097152 | tf_op jit(solution)/shard_map/all_to_all | solution.py:29
  21.3 0.2 units.1
  21.5 10.3 %all_to_all.35 = bf16[8,64,512]{2,1,0:T(8,128)(2,1)S(1)} all-to-all(bf16[8,64,512]{2,1,0:T(8,128)(2,1)S(1)} %get-tuple-element.21), channel_id=1, replica_groups=mesh['zh'=4,'zl'=2,'yh'=4,'core'=2,'x'=4,'yl'=2] {'x','yl'}, dimensions={0} | all-to-all | bytes 1048576 | tf_op jit(solution)/shard_map/all_to_all | solution.py:29
  31.8 1.3 cosines.1
  33.1 10.5 %all_to_all.36.pulls_ref = bf16[8,72,512]{2,1,0:T(8,128)(2,1)S(1)} all-to-all(bf16[8,72,512]{2,1,0:T(8,128)(2,1)S(1)} %get-tuple-element.23), channel_id=1, replica_groups=mesh['zh'=4,'zl'=2,'yh'=4,'core'=2,'x'=4,'yl'=2] {'x','yl'}, dimensions={0} | all-to-all | bytes 1179648 | tf_op jit(solution)/shard_map/all_to_all | solution.py:29
  43.6 0.6 raw_grads.1
  44.2 10.0 %all_to_all.37 = bf16[8,64,512]{2,1,0:T(8,128)(2,1)S(1)} all-to-all(bf16[8,64,512]{2,1,0:T(8,128)(2,1)S(1)} %get-tuple-element.26), channel_id=1, replica_groups=mesh['zh'=4,'zl'=2,'yh'=4,'core'=2,'x'=4,'yl'=2] {'x','yl'}, dimensions={0} | all-to-all | bytes 1048576 | tf_op jit(solution)/shard_map/all_to_all | solution.py:29
  54.1 0.6 parts.5
  54.7 10.0 %collective-permute-start = (bf16[16,136,128]{2,1,0:T(8,128)(2,1)S(1)}, bf16[16,136,128]{2,1,0:T(8,128)(2,1)S(1)}, u32[]{:S(2)}, u32[]{:S(2)}) collective-permute-start(bf16[16,136,128]{2,1,0:T(8,128)(2,1)S(1)} %parts.5), channel_id=1, source_target_pairs={{0,8},{8,0},{1,9},{9,1},{2,10},{10,2},{3,11},{11,3},{4,12},{12,4},... | collective-permute-start | bytes 1671176 | tf_op jit(solution)/shard_map/ppermute | solution.py:487
  64.7 0.6 parts.4
  65.3 1.0 collective-permute-done
  66.3 0.1 add_convert_fusion.1
  66.4 11.1 %collective-permute-start.1 = (bf16[16,136,128]{2,1,0:T(8,128)(2,1)S(1)}, bf16[16,136,128]{2,1,0:T(8,128)(2,1)S(1)}, u32[]{:S(2)}, u32[]{:S(2)}) collective-permute-start(bf16[16,136,128]{2,1,0:T(8,128)(2,1)S(1)} %add_convert_fusion.1), channel_id=1, source_target_pairs={{0,64},{8,456},{64,0},{72,136},{128,192},{136,72},{192,128},{200,2... | collective-permute-start | bytes 1671176 | tf_op jit(solution)/shard_map/ppermute | solution.py:490
  77.5 0.6 parts.7
  78.0 1.9 %collective-permute-start.2 = (bf16[16,136,128]{2,1,0:T(8,128)(2,1)S(1)}, bf16[16,136,128]{2,1,0:T(8,128)(2,1)S(1)}, u32[]{:S(2)}, u32[]{:S(2)}) collective-permute-start(bf16[16,136,128]{2,1,0:T(8,128)(2,1)S(1)} %parts.7), channel_id=1, source_target_pairs={{0,8},{8,0},{1,9},{9,1},{2,10},{10,2},{3,11},{11,3},{4,12},{12,4},... | collective-permute-start | bytes 1671176 | tf_op jit(solution)/shard_map/ppermute | solution.py:492
  80.0 0.6 parts.6
  80.5 3.8 %collective-permute-done.1 = bf16[16,136,128]{2,1,0:T(8,128)(2,1)S(1)} collective-permute-done((bf16[16,136,128]{2,1,0:T(8,128)(2,1)S(1)}, bf16[16,136,128]{2,1,0:T(8,128)(2,1)S(1)}, u32[]{:S(2)}, u32[]{:S(2)}) %collective-permute-start.1) | collective-permute-done | bytes 557088 | tf_op jit(solution)/shard_map/ppermute | solution.py:490
  84.4 0.1 convert_add_fusion
  84.5 0.0 collective-permute-done.2
  84.5 0.1 add_convert_fusion
  84.6 28.9 %all_to_all.38.got_ref = bf16[16,136,128]{2,1,0:T(8,128)(2,1)S(1)} all-to-all(bf16[16,136,128]{2,1,0:T(8,128)(2,1)S(1)} %add_convert_fusion), channel_id=1, replica_groups=mesh['zh'=4,'zl'=2,'yh'=4,'core'=2,'x'=4,'yl'=2] {'zh','yh'}, dimensions={0} | all-to-all | bytes 1114112 | tf_op jit(solution)/shard_map/all_to_all | solution.py:29
  113.5 0.1 totals.1
  113.6 26.9 %all_to_all.39.refs_0_ = bf16[16,136,128]{2,1,0:T(8,128)(2,1)S(1)} all-to-all(bf16[16,136,128]{2,1,0:T(8,128)(2,1)S(1)} %totals.1), channel_id=1, replica_groups=mesh['zh'=4,'zl'=2,'yh'=4,'core'=2,'x'=4,'yl'=2] {'zh','yh'}, dimensions={0} | all-to-all | bytes 1114112 | tf_op jit(solution)/shard_map/all_to_all | solution.py:29
  140.5 2.8 %collective-permute-start.3 = (bf16[16,136,128]{2,1,0:T(8,128)(2,1)S(1)}, bf16[16,136,128]{2,1,0:T(8,128)(2,1)S(1)}, u32[]{:S(2)}, u32[]{:S(2)}) collective-permute-start(bf16[16,136,128]{2,1,0:T(8,128)(2,1)S(1)} %all_to_all.39.refs_0_), channel_id=1, source_target_pairs={{0,64},{8,456},{64,0},{72,136},{128,192},{136,72},{192,128},{200,2... | collective-permute-start | bytes 1671176 | tf_op jit(solution)/shard_map/ppermute | solution.py:498
  143.4 3.3 %collective-permute-start.5 = (bf16[16,136,128]{2,1,0:T(8,128)(2,1)S(1)}, bf16[16,136,128]{2,1,0:T(8,128)(2,1)S(1)}, u32[]{:S(2)}, u32[]{:S(2)}) collective-permute-start(bf16[16,136,128]{2,1,0:T(8,128)(2,1)S(1)} %all_to_all.39.refs_0_), channel_id=1, source_target_pairs={{0,8},{8,0},{1,9},{9,1},{2,10},{10,2},{3,11},{11,3},{4,12},{12,4},... | collective-permute-start | bytes 1671176 | tf_op jit(solution)/shard_map/ppermute | solution.py:499
  146.6 0.9 assemble.3
  147.5 4.5 %collective-permute-done.3.refs_0_ = bf16[16,136,128]{2,1,0:T(8,128)(2,1)S(1)} collective-permute-done((bf16[16,136,128]{2,1,0:T(8,128)(2,1)S(1)}, bf16[16,136,128]{2,1,0:T(8,128)(2,1)S(1)}, u32[]{:S(2)}, u32[]{:S(2)}) %collective-permute-start.3) | collective-permute-done | bytes 557088 | tf_op jit(solution)/shard_map/ppermute | solution.py:498
  152.0 3.4 %collective-permute-start.4 = (bf16[16,136,128]{2,1,0:T(8,128)(2,1)S(1)}, bf16[16,136,128]{2,1,0:T(8,128)(2,1)S(1)}, u32[]{:S(2)}, u32[]{:S(2)}) collective-permute-start(bf16[16,136,128]{2,1,0:T(8,128)(2,1)S(1)} %collective-permute-done.3.refs_0_), channel_id=1, source_target_pairs={{0,8},{8,0},{1,9},{9,1},{2,10},{10,2},{3,11},{11,3},{4,12},{12,4},... | collective-permute-start | bytes 1671176 | tf_op jit(solution)/shard_map/ppermute | solution.py:502
  155.4 1.1 assemble.4
  156.5 0.5 collective-permute-done.4.refs_0_
  156.9 0.9 assemble.5
  (7 shorter events, 0.0 us)
Async XLA Ops:
  21.3 10.5 %copy-start.2 = (s32[512]{0:T(512)S(1)}, s32[512]{0:T(512)}, u32[]{:S(2)}) copy-start(s32[512]{0:T(512)} %param.7) | copy-start | bytes 6148
  33.1 21.1 %copy-start.1 = (bf16[512,512]{1,0:T(8,128)(2,1)S(1)}, bf16[512,512]{1,0:T(8,128)(2,1)}, u32[]{:S(2)}) copy-start(bf16[512,512]{1,0:T(8,128)(2,1)} %class_ref.9) | copy-start | bytes 1572868
  43.6 10.5 %copy-start = (bf16[512,1568]{0,1:T(8,128)(2,1)S(1)}, bf16[512,1568]{0,1:T(8,128)(2,1)}, u32[]{:S(2)}) copy-start(bf16[512,1568]{0,1:T(8,128)(2,1)} %param.4) | copy-start | bytes 4816900
  54.7 11.6 %collective-permute-start = (bf16[16,136,128]{2,1,0:T(8,128)(2,1)S(1)}, bf16[16,136,128]{2,1,0:T(8,128)(2,1)S(1)}, u32[]{:S(2)}, u32[]{:S(2)}) collective-permute-start(bf16[16,136,128]{2,1,0:T(8,128)(2,1)S(1)} %parts.5), channel_id=1, source_target_pairs={{0,8},{8,0},{1,9},{9,1},{2,10},{10,2},{3,11},{11,3},{4,12},{12,4},... | collective-permute-start | bytes 1671176 | tf_op jit(solution)/shard_map/ppermute | solution.py:487
  66.4 18.0 %collective-permute-start.1 = (bf16[16,136,128]{2,1,0:T(8,128)(2,1)S(1)}, bf16[16,136,128]{2,1,0:T(8,128)(2,1)S(1)}, u32[]{:S(2)}, u32[]{:S(2)}) collective-permute-start(bf16[16,136,128]{2,1,0:T(8,128)(2,1)S(1)} %add_convert_fusion.1), channel_id=1, source_target_pairs={{0,64},{8,456},{64,0},{72,136},{128,192},{136,72},{192,128},{200,2... | collective-permute-start | bytes 1671176 | tf_op jit(solution)/shard_map/ppermute | solution.py:490
  78.0 6.4 %collective-permute-start.2 = (bf16[16,136,128]{2,1,0:T(8,128)(2,1)S(1)}, bf16[16,136,128]{2,1,0:T(8,128)(2,1)S(1)}, u32[]{:S(2)}, u32[]{:S(2)}) collective-permute-start(bf16[16,136,128]{2,1,0:T(8,128)(2,1)S(1)} %parts.7), channel_id=1, source_target_pairs={{0,8},{8,0},{1,9},{9,1},{2,10},{10,2},{3,11},{11,3},{4,12},{12,4},... | collective-permute-start | bytes 1671176 | tf_op jit(solution)/shard_map/ppermute | solution.py:492
  140.5 11.5 %collective-permute-start.3 = (bf16[16,136,128]{2,1,0:T(8,128)(2,1)S(1)}, bf16[16,136,128]{2,1,0:T(8,128)(2,1)S(1)}, u32[]{:S(2)}, u32[]{:S(2)}) collective-permute-start(bf16[16,136,128]{2,1,0:T(8,128)(2,1)S(1)} %all_to_all.39.refs_0_), channel_id=1, source_target_pairs={{0,64},{8,456},{64,0},{72,136},{128,192},{136,72},{192,128},{200,2... | collective-permute-start | bytes 1671176 | tf_op jit(solution)/shard_map/ppermute | solution.py:498
  143.4 12.0 %collective-permute-start.5 = (bf16[16,136,128]{2,1,0:T(8,128)(2,1)S(1)}, bf16[16,136,128]{2,1,0:T(8,128)(2,1)S(1)}, u32[]{:S(2)}, u32[]{:S(2)}) collective-permute-start(bf16[16,136,128]{2,1,0:T(8,128)(2,1)S(1)} %all_to_all.39.refs_0_), channel_id=1, source_target_pairs={{0,8},{8,0},{1,9},{9,1},{2,10},{10,2},{3,11},{11,3},{4,12},{12,4},... | collective-permute-start | bytes 1671176 | tf_op jit(solution)/shard_map/ppermute | solution.py:499
  152.0 4.9 %collective-permute-start.4 = (bf16[16,136,128]{2,1,0:T(8,128)(2,1)S(1)}, bf16[16,136,128]{2,1,0:T(8,128)(2,1)S(1)}, u32[]{:S(2)}, u32[]{:S(2)}) collective-permute-start(bf16[16,136,128]{2,1,0:T(8,128)(2,1)S(1)} %collective-permute-done.3.refs_0_), channel_id=1, source_target_pairs={{0,8},{8,0},{1,9},{9,1},{2,10},{10,2},{3,11},{11,3},{4,12},{12,4},... | collective-permute-start | bytes 1671176 | tf_op jit(solution)/shard_map/ppermute | solution.py:502

commit v11 on v10

--- a/solution.py
+++ b/solution.py
@@ -495,14 +495,17 @@
     mine = (mine + theirs.astype(jnp.float32)).astype(jnp.bfloat16)
     sizes = (inputs, classes, width)
     mine = exchange(totals(exchange(mine, CHIPS)), CHIPS)
+    crossed = []
+    for z in range(length):
+        crossed.append((2 * z, 2 * ((z + 2 * (z % 2) - 1) % length) + 1))
+        crossed.append((2 * z + 1, 2 * (z ^ 1)))
     next_mine = lax.ppermute(mine, neighbour, pairs)
+    next_across = lax.ppermute(mine, neighbour, crossed)
     across_mine = lax.ppermute(mine, "core", swap)
     written = assemble(place, blocks, sizes, {(False, False): mine}, ())
-    next_mine, written = lax.optimization_barrier((next_mine, written))
-    across_next = lax.ppermute(next_mine, "core", swap)
     pieces = {(False, True): next_mine, (True, False): across_mine}
     written = assemble(place, blocks, sizes, pieces, written)
-    return tuple(assemble(place, blocks, sizes, {(True, True): across_next}, written))
+    return tuple(assemble(place, blocks, sizes, {(True, True): next_across}, written))
 
 
 def solution(mesh):

time: 158 us -> 163 us (1.032)
  waiting for transfers between devices: 9.77 us -> 14.8 us
    ppermute x1, waiting for transfers between devices: 4.48 us -> 7.86 us  [shards(): next_mine = lax.ppermute(mine, neighbour, pairs)]
    ppermute x1, waiting for transfers between devices: 0.47 us -> 2.16 us  [shards(): next_across = lax.ppermute(mine, neighbour, crossed)]
where the time goes in v11:
time: 163 us; the launch traced here: 162 us
  blocking collectives  104 us (64%)
  starting transfers between devices  31.9 us (20%)
  waiting for transfers between devices  14.8 us (9%)
  Pallas kernels  10.2 us (6%)
    all_to_all x6, blocking collectives, exchange(): return lax.all_to_all(blocks, axes, 0, 0, tiled=True)  104 us
    ppermute x2, starting transfers between devices, shards(): theirs = lax.ppermute(theirs, 'core', swap)  11.9 us
    ppermute x1, starting transfers between devices, shards(): got = lax.ppermute(sent, neighbour, pairs)  11.1 us
    ppermute x1, waiting for transfers between devices, shards(): next_mine = lax.ppermute(mine, neighbour, pairs)  7.86 us
    pallas_call x8, Pallas kernels, call(): pl.pallas_call(kernel, in_specs=specs, out_specs=[VMEM] * len(results), o...  4.44 us
    ppermute x1, waiting for transfers between devices, shards(): got = lax.ppermute(sent, neighbour, pairs)  3.84 us
    ppermute x1, starting transfers between devices, shards(): across_mine = lax.ppermute(mine, 'core', swap)  3.43 us
  transfers between devices with their start and end apart: 6, of which 4 were waited for; matrix products, arithmetic and copies ran while one was open for 0% of the time, Pallas kernels for 2%

profile of v11, /device:TPU:1, one launch (start us, length us, event | category | flops | bytes accessed | tf_op | source)
XLA Modules:
  0.0 162.3 jit_solution(11498238443267786373)
XLA Ops:
  0.6 2.9 %embed.1 = (bf16[512,1024]{1,0:T(8,128)(2,1)S(1)}, bf16[512,512]{1,0:T(8,128)(2,1)S(1)}) custom-call(s32[1]{0:T(128)} %bitcast.place_ref, bf16[1568,512]{1,0:T(8,128)(2,1)} %bitcast.6, bf16[1568,512]{1,0:T(8,128)(2,1)} %fc_ref.1, bf16[512,512]{1,0:T(8,128)(2,1)} %class_ref.9, s32[1,512]{1,0:T(1,128)} %bitcast.21), custom_call_target="tpu_custom_call" | custom-call | tf_op jit(solution)/shard_map/embed/pallas_call | solution.py:155
  3.6 17.7 %all_to_all.34.got_ref = bf16[8,64,1024]{2,1,0:T(8,128)(2,1)S(1)} all-to-all(bf16[8,64,1024]{2,1,0:T(8,128)(2,1)S(1)} %bitcast.20), channel_id=1, replica_groups=mesh['zh'=4,'zl'=2,'yh'=4,'core'=2,'x'=4,'yl'=2] {'x','yl'}, dimensions={0} | all-to-all | bytes 2097152 | tf_op jit(solution)/shard_map/all_to_all | solution.py:29
  21.3 0.2 units.1
  21.5 10.3 %all_to_all.35 = bf16[8,64,512]{2,1,0:T(8,128)(2,1)S(1)} all-to-all(bf16[8,64,512]{2,1,0:T(8,128)(2,1)S(1)} %get-tuple-element.18), channel_id=1, replica_groups=mesh['zh'=4,'zl'=2,'yh'=4,'core'=2,'x'=4,'yl'=2] {'x','yl'}, dimensions={0} | all-to-all | bytes 1048576 | tf_op jit(solution)/shard_map/all_to_all | solution.py:29
  31.8 1.3 cosines.1
  33.1 10.5 %all_to_all.36.pulls_ref = bf16[8,72,512]{2,1,0:T(8,128)(2,1)S(1)} all-to-all(bf16[8,72,512]{2,1,0:T(8,128)(2,1)S(1)} %get-tuple-element.20), channel_id=1, replica_groups=mesh['zh'=4,'zl'=2,'yh'=4,'core'=2,'x'=4,'yl'=2] {'x','yl'}, dimensions={0} | all-to-all | bytes 1179648 | tf_op jit(solution)/shard_map/all_to_all | solution.py:29
  43.6 0.6 raw_grads.1
  44.2 10.0 %all_to_all.37 = bf16[8,64,512]{2,1,0:T(8,128)(2,1)S(1)} all-to-all(bf16[8,64,512]{2,1,0:T(8,128)(2,1)S(1)} %get-tuple-element.23), channel_id=1, replica_groups=mesh['zh'=4,'zl'=2,'yh'=4,'core'=2,'x'=4,'yl'=2] {'x','yl'}, dimensions={0} | all-to-all | bytes 1048576 | tf_op jit(solution)/shard_map/all_to_all | solution.py:29
  54.1 0.6 parts.5
  54.7 10.0 %collective-permute-start = (bf16[16,136,128]{2,1,0:T(8,128)(2,1)S(1)}, bf16[16,136,128]{2,1,0:T(8,128)(2,1)S(1)}, u32[]{:S(2)}, u32[]{:S(2)}) collective-permute-start(bf16[16,136,128]{2,1,0:T(8,128)(2,1)S(1)} %parts.5), channel_id=1, source_target_pairs={{0,8},{8,0},{1,9},{9,1},{2,10},{10,2},{3,11},{11,3},{4,12},{12,4},... | collective-permute-start | bytes 1671176 | tf_op jit(solution)/shard_map/ppermute | solution.py:487
  64.7 0.6 parts.4
  65.3 1.0 collective-permute-done
  66.3 0.1 add_convert_fusion.1
  66.4 11.1 %collective-permute-start.1 = (bf16[16,136,128]{2,1,0:T(8,128)(2,1)S(1)}, bf16[16,136,128]{2,1,0:T(8,128)(2,1)S(1)}, u32[]{:S(2)}, u32[]{:S(2)}) collective-permute-start(bf16[16,136,128]{2,1,0:T(8,128)(2,1)S(1)} %add_convert_fusion.1), channel_id=1, source_target_pairs={{0,64},{8,456},{64,0},{72,136},{128,192},{136,72},{192,128},{200,2... | collective-permute-start | bytes 1671176 | tf_op jit(solution)/shard_map/ppermute | solution.py:490
  77.5 0.6 parts.7
  78.0 1.9 %collective-permute-start.2 = (bf16[16,136,128]{2,1,0:T(8,128)(2,1)S(1)}, bf16[16,136,128]{2,1,0:T(8,128)(2,1)S(1)}, u32[]{:S(2)}, u32[]{:S(2)}) collective-permute-start(bf16[16,136,128]{2,1,0:T(8,128)(2,1)S(1)} %parts.7), channel_id=1, source_target_pairs={{0,8},{8,0},{1,9},{9,1},{2,10},{10,2},{3,11},{11,3},{4,12},{12,4},... | collective-permute-start | bytes 1671176 | tf_op jit(solution)/shard_map/ppermute | solution.py:492
  80.0 0.6 parts.6
  80.5 3.8 %collective-permute-done.1 = bf16[16,136,128]{2,1,0:T(8,128)(2,1)S(1)} collective-permute-done((bf16[16,136,128]{2,1,0:T(8,128)(2,1)S(1)}, bf16[16,136,128]{2,1,0:T(8,128)(2,1)S(1)}, u32[]{:S(2)}, u32[]{:S(2)}) %collective-permute-start.1) | collective-permute-done | bytes 557088 | tf_op jit(solution)/shard_map/ppermute | solution.py:490
  84.4 0.1 convert_add_fusion
  84.5 0.0 collective-permute-done.2
  84.5 0.1 add_convert_fusion
  84.6 28.9 %all_to_all.38.got_ref = bf16[16,136,128]{2,1,0:T(8,128)(2,1)S(1)} all-to-all(bf16[16,136,128]{2,1,0:T(8,128)(2,1)S(1)} %add_convert_fusion), channel_id=1, replica_groups=mesh['zh'=4,'zl'=2,'yh'=4,'core'=2,'x'=4,'yl'=2] {'zh','yh'}, dimensions={0} | all-to-all | bytes 1114112 | tf_op jit(solution)/shard_map/all_to_all | solution.py:29
  113.5 0.1 totals.1
  113.6 26.9 %all_to_all.39.refs_0_ = bf16[16,136,128]{2,1,0:T(8,128)(2,1)S(1)} all-to-all(bf16[16,136,128]{2,1,0:T(8,128)(2,1)S(1)} %totals.1), channel_id=1, replica_groups=mesh['zh'=4,'zl'=2,'yh'=4,'core'=2,'x'=4,'yl'=2] {'zh','yh'}, dimensions={0} | all-to-all | bytes 1114112 | tf_op jit(solution)/shard_map/all_to_all | solution.py:29
  140.5 3.4 %collective-permute-start.5 = (bf16[16,136,128]{2,1,0:T(8,128)(2,1)S(1)}, bf16[16,136,128]{2,1,0:T(8,128)(2,1)S(1)}, u32[]{:S(2)}, u32[]{:S(2)}) collective-permute-start(bf16[16,136,128]{2,1,0:T(8,128)(2,1)S(1)} %all_to_all.39.refs_0_), channel_id=1, source_target_pairs={{0,8},{8,0},{1,9},{9,1},{2,10},{10,2},{3,11},{11,3},{4,12},{12,4},... | collective-permute-start | bytes 1671176 | tf_op jit(solution)/shard_map/ppermute | solution.py:504
  144.0 2.6 %collective-permute-start.4 = (bf16[16,136,128]{2,1,0:T(8,128)(2,1)S(1)}, bf16[16,136,128]{2,1,0:T(8,128)(2,1)S(1)}, u32[]{:S(2)}, u32[]{:S(2)}) collective-permute-start(bf16[16,136,128]{2,1,0:T(8,128)(2,1)S(1)} %all_to_all.39.refs_0_), channel_id=1, source_target_pairs={{0,64},{8,456},{64,0},{72,136},{128,192},{136,72},{192,128},{200,2... | collective-permute-start | bytes 1671176 | tf_op jit(solution)/shard_map/ppermute | solution.py:502
  146.6 2.9 %collective-permute-start.3 = (bf16[16,136,128]{2,1,0:T(8,128)(2,1)S(1)}, bf16[16,136,128]{2,1,0:T(8,128)(2,1)S(1)}, u32[]{:S(2)}, u32[]{:S(2)}) collective-permute-start(bf16[16,136,128]{2,1,0:T(8,128)(2,1)S(1)} %all_to_all.39.refs_0_), channel_id=1, source_target_pairs={{0,456},{8,64},{64,136},{72,0},{128,72},{136,192},{192,264},{200,1... | collective-permute-start | bytes 1671176 | tf_op jit(solution)/shard_map/ppermute | solution.py:503
  149.4 0.9 assemble.3
  150.3 7.9 %collective-permute-done.4.refs_0_ = bf16[16,136,128]{2,1,0:T(8,128)(2,1)S(1)} collective-permute-done((bf16[16,136,128]{2,1,0:T(8,128)(2,1)S(1)}, bf16[16,136,128]{2,1,0:T(8,128)(2,1)S(1)}, u32[]{:S(2)}, u32[]{:S(2)}) %collective-permute-start.4) | collective-permute-done | bytes 557088 | tf_op jit(solution)/shard_map/ppermute | solution.py:502
  158.2 1.1 assemble.4
  159.3 2.2 %collective-permute-done.3.refs_0_ = bf16[16,136,128]{2,1,0:T(8,128)(2,1)S(1)} collective-permute-done((bf16[16,136,128]{2,1,0:T(8,128)(2,1)S(1)}, bf16[16,136,128]{2,1,0:T(8,128)(2,1)S(1)}, u32[]{:S(2)}, u32[]{:S(2)}) %collective-permute-start.3) | collective-permute-done | bytes 557088 | tf_op jit(solution)/shard_map/ppermute | solution.py:503
  161.4 0.9 assemble.5
  (7 shorter events, 0.0 us)
Async XLA Ops:
  21.3 10.5 %copy-start.2 = (s32[512]{0:T(512)S(1)}, s32[512]{0:T(512)}, u32[]{:S(2)}) copy-start(s32[512]{0:T(512)} %param.7) | copy-start | bytes 6148
  33.1 21.1 %copy-start.1 = (bf16[512,512]{1,0:T(8,128)(2,1)S(1)}, bf16[512,512]{1,0:T(8,128)(2,1)}, u32[]{:S(2)}) copy-start(bf16[512,512]{1,0:T(8,128)(2,1)} %class_ref.9) | copy-start | bytes 1572868
  43.6 10.5 %copy-start = (bf16[512,1568]{0,1:T(8,128)(2,1)S(1)}, bf16[512,1568]{0,1:T(8,128)(2,1)}, u32[]{:S(2)}) copy-start(bf16[512,1568]{0,1:T(8,128)(2,1)} %param.4) | copy-start | bytes 4816900
  54.7 11.6 %collective-permute-start = (bf16[16,136,128]{2,1,0:T(8,128)(2,1)S(1)}, bf16[16,136,128]{2,1,0:T(8,128)(2,1)S(1)}, u32[]{:S(2)}, u32[]{:S(2)}) collective-permute-start(bf16[16,136,128]{2,1,0:T(8,128)(2,1)S(1)} %parts.5), channel_id=1, source_target_pairs={{0,8},{8,0},{1,9},{9,1},{2,10},{10,2},{3,11},{11,3},{4,12},{12,4},... | collective-permute-start | bytes 1671176 | tf_op jit(solution)/shard_map/ppermute | solution.py:487
  66.4 18.0 %collective-permute-start.1 = (bf16[16,136,128]{2,1,0:T(8,128)(2,1)S(1)}, bf16[16,136,128]{2,1,0:T(8,128)(2,1)S(1)}, u32[]{:S(2)}, u32[]{:S(2)}) collective-permute-start(bf16[16,136,128]{2,1,0:T(8,128)(2,1)S(1)} %add_convert_fusion.1), channel_id=1, source_target_pairs={{0,64},{8,456},{64,0},{72,136},{128,192},{136,72},{192,128},{200,2... | collective-permute-start | bytes 1671176 | tf_op jit(solution)/shard_map/ppermute | solution.py:490
  78.0 6.4 %collective-permute-start.2 = (bf16[16,136,128]{2,1,0:T(8,128)(2,1)S(1)}, bf16[16,136,128]{2,1,0:T(8,128)(2,1)S(1)}, u32[]{:S(2)}, u32[]{:S(2)}) collective-permute-start(bf16[16,136,128]{2,1,0:T(8,128)(2,1)S(1)} %parts.7), channel_id=1, source_target_pairs={{0,8},{8,0},{1,9},{9,1},{2,10},{10,2},{3,11},{11,3},{4,12},{12,4},... | collective-permute-start | bytes 1671176 | tf_op jit(solution)/shard_map/ppermute | solution.py:492
  140.5 9.8 %collective-permute-start.5 = (bf16[16,136,128]{2,1,0:T(8,128)(2,1)S(1)}, bf16[16,136,128]{2,1,0:T(8,128)(2,1)S(1)}, u32[]{:S(2)}, u32[]{:S(2)}) collective-permute-start(bf16[16,136,128]{2,1,0:T(8,128)(2,1)S(1)} %all_to_all.39.refs_0_), channel_id=1, source_target_pairs={{0,8},{8,0},{1,9},{9,1},{2,10},{10,2},{3,11},{11,3},{4,12},{12,4},... | collective-permute-start | bytes 1671176 | tf_op jit(solution)/shard_map/ppermute | solution.py:504
  144.0 14.2 %collective-permute-start.4 = (bf16[16,136,128]{2,1,0:T(8,128)(2,1)S(1)}, bf16[16,136,128]{2,1,0:T(8,128)(2,1)S(1)}, u32[]{:S(2)}, u32[]{:S(2)}) collective-permute-start(bf16[16,136,128]{2,1,0:T(8,128)(2,1)S(1)} %all_to_all.39.refs_0_), channel_id=1, source_target_pairs={{0,64},{8,456},{64,0},{72,136},{128,192},{136,72},{192,128},{200,2... | collective-permute-start | bytes 1671176 | tf_op jit(solution)/shard_map/ppermute | solution.py:502
  146.6 14.9 %collective-permute-start.3 = (bf16[16,136,128]{2,1,0:T(8,128)(2,1)S(1)}, bf16[16,136,128]{2,1,0:T(8,128)(2,1)S(1)}, u32[]{:S(2)}, u32[]{:S(2)}) collective-permute-start(bf16[16,136,128]{2,1,0:T(8,128)(2,1)S(1)} %all_to_all.39.refs_0_), channel_id=1, source_target_pairs={{0,456},{8,64},{64,136},{72,0},{128,72},{136,192},{192,264},{200,1... | collective-permute-start | bytes 1671176 | tf_op jit(solution)/shard_map/ppermute | solution.py:503

commit v12 on v10

--- a/solution.py
+++ b/solution.py
@@ -15,7 +15,7 @@
 EPSILON = 1e-06
 
 CLS = ("x", "yl")
-CHIPS = ("zh", "yh")
+CHIPS = ("ya", "za", "yb", "zb")
 LANES = 128
 CHUNKS = 2
 MARK = 1024.0
@@ -475,12 +475,12 @@
     grads = exchange(sent, CLS).reshape(faces, width)
 
     swap = [(0, 1), (1, 0)]
-    length = 2 * lax.axis_size("zh")
+    neighbour = ("za", "zb", "zl", "core")
+    length = lax.axis_size(neighbour) // 2
     pairs = []
     for z in range(length):
         pairs.append((2 * z, 2 * (z ^ 1)))
         pairs.append((2 * z + 1, 2 * ((z + 2 * (z % 2) - 1) % length) + 1))
-    neighbour = ("zh", "zl", "core")
 
     operands = (blocks, features, grads, scales, units, others, class_weight)
     theirs = parts((True, True), place, jnp.bfloat16, *operands)
@@ -506,8 +506,9 @@
 
 
 def solution(mesh):
-    fine = Mesh(mesh.devices.reshape(4, 2, 4, 2, 4, 2), ("zh", "zl", "yh", "core", "x", "yl"))
-    dp = ("zh", "zl", "yh", "core")
+    names = ("za", "zb", "zl", "ya", "yb", "core", "x", "yl")
+    fine = Mesh(mesh.devices.reshape(2, 2, 2, 2, 2, 2, 4, 2), names)
+    dp = names[:6]
     specs = (P(dp, CLS), P(CLS, None), P(CLS, None), P(dp))
     return jax.shard_map(
         shards,

time: 158 us -> 159 us (level)
  no operation moved by 1% of the time
where the time goes in v12:
time: 159 us
  blocking collectives  105 us (66%)
  starting transfers between devices  31.9 us (20%)
  waiting for transfers between devices  10.4 us (7%)
  Pallas kernels  10.2 us (6%)
    all_to_all x6, blocking collectives, exchange(): return lax.all_to_all(blocks, axes, 0, 0, tiled=True)  105 us
    ppermute x2, starting transfers between devices, shards(): theirs = lax.ppermute(theirs, 'core', swap)  11.9 us
    ppermute x1, starting transfers between devices, shards(): got = lax.ppermute(sent, neighbour, pairs)  11.1 us
    ppermute x1, waiting for transfers between devices, shards(): next_mine = lax.ppermute(mine, neighbour, pairs)  5.14 us
    pallas_call x8, Pallas kernels, call(): pl.pallas_call(kernel, in_specs=specs, out_specs=[VMEM] * len(results), o...  4.44 us
    ppermute x1, waiting for transfers between devices, shards(): got = lax.ppermute(sent, neighbour, pairs)  3.84 us
    ppermute x1, starting transfers between devices, shards(): across_next = lax.ppermute(next_mine, 'core', swap)  3.47 us
    ppermute x1, starting transfers between devices, shards(): across_mine = lax.ppermute(mine, 'core', swap)  3.23 us
  transfers between devices with their start and end apart: 6, of which 4 were waited for; matrix products, arithmetic and copies ran while one was open for 0% of the time, Pallas kernels for 2%

profile of v12, /device:TPU:1, one launch (start us, length us, event | category | flops | bytes accessed | tf_op | source)
XLA Modules:
  0.0 158.9 jit_solution(8716300616298661686)
XLA Ops:
  0.6 2.9 %embed.1 = (bf16[512,1024]{1,0:T(8,128)(2,1)S(1)}, bf16[512,512]{1,0:T(8,128)(2,1)S(1)}) custom-call(s32[1]{0:T(128)} %bitcast.place_ref, bf16[1568,512]{1,0:T(8,128)(2,1)} %bitcast.6, bf16[1568,512]{1,0:T(8,128)(2,1)} %fc_ref.1, bf16[512,512]{1,0:T(8,128)(2,1)} %class_ref.9, s32[1,512]{1,0:T(1,128)} %bitcast.21), custom_call_target="tpu_custom_call" | custom-call | tf_op jit(solution)/shard_map/embed/pallas_call | solution.py:155
  3.6 17.7 %all_to_all.34.got_ref = bf16[8,64,1024]{2,1,0:T(8,128)(2,1)S(1)} all-to-all(bf16[8,64,1024]{2,1,0:T(8,128)(2,1)S(1)} %bitcast.20), channel_id=1, replica_groups=mesh['za'=2,'zb'=2,'zl'=2,'ya'=2,'yb'=2,'core'=2,'x'=4,'yl'=2] {'x','yl'}, dimensions={0} | all-to-all | bytes 2097152 | tf_op jit(solution)/shard_map/all_to_all | solution.py:29
  21.3 0.2 units.1
  21.5 10.3 %all_to_all.35 = bf16[8,64,512]{2,1,0:T(8,128)(2,1)S(1)} all-to-all(bf16[8,64,512]{2,1,0:T(8,128)(2,1)S(1)} %get-tuple-element.21), channel_id=1, replica_groups=mesh['za'=2,'zb'=2,'zl'=2,'ya'=2,'yb'=2,'core'=2,'x'=4,'yl'=2] {'x','yl'}, dimensions={0} | all-to-all | bytes 1048576 | tf_op jit(solution)/shard_map/all_to_all | solution.py:29
  31.8 1.3 cosines.1
  33.1 10.5 %all_to_all.36.pulls_ref = bf16[8,72,512]{2,1,0:T(8,128)(2,1)S(1)} all-to-all(bf16[8,72,512]{2,1,0:T(8,128)(2,1)S(1)} %get-tuple-element.23), channel_id=1, replica_groups=mesh['za'=2,'zb'=2,'zl'=2,'ya'=2,'yb'=2,'core'=2,'x'=4,'yl'=2] {'x','yl'}, dimensions={0} | all-to-all | bytes 1179648 | tf_op jit(solution)/shard_map/all_to_all | solution.py:29
  43.6 0.6 raw_grads.1
  44.2 10.0 %all_to_all.37 = bf16[8,64,512]{2,1,0:T(8,128)(2,1)S(1)} all-to-all(bf16[8,64,512]{2,1,0:T(8,128)(2,1)S(1)} %get-tuple-element.26), channel_id=1, replica_groups=mesh['za'=2,'zb'=2,'zl'=2,'ya'=2,'yb'=2,'core'=2,'x'=4,'yl'=2] {'x','yl'}, dimensions={0} | all-to-all | bytes 1048576 | tf_op jit(solution)/shard_map/all_to_all | solution.py:29
  54.1 0.6 parts.5
  54.7 10.0 %collective-permute-start = (bf16[16,136,128]{2,1,0:T(8,128)(2,1)S(1)}, bf16[16,136,128]{2,1,0:T(8,128)(2,1)S(1)}, u32[]{:S(2)}, u32[]{:S(2)}) collective-permute-start(bf16[16,136,128]{2,1,0:T(8,128)(2,1)S(1)} %parts.5), channel_id=1, source_target_pairs={{0,8},{8,0},{1,9},{9,1},{2,10},{10,2},{3,11},{11,3},{4,12},{12,4},... | collective-permute-start | bytes 1671176 | tf_op jit(solution)/shard_map/ppermute | solution.py:487
  64.7 0.6 parts.4
  65.3 1.0 collective-permute-done
  66.3 0.1 add_convert_fusion.1
  66.4 11.1 %collective-permute-start.1 = (bf16[16,136,128]{2,1,0:T(8,128)(2,1)S(1)}, bf16[16,136,128]{2,1,0:T(8,128)(2,1)S(1)}, u32[]{:S(2)}, u32[]{:S(2)}) collective-permute-start(bf16[16,136,128]{2,1,0:T(8,128)(2,1)S(1)} %add_convert_fusion.1), channel_id=1, source_target_pairs={{0,64},{8,456},{64,0},{72,136},{128,192},{136,72},{192,128},{200,2... | collective-permute-start | bytes 1671176 | tf_op jit(solution)/shard_map/ppermute | solution.py:490
  77.5 0.6 parts.7
  78.0 1.9 %collective-permute-start.2 = (bf16[16,136,128]{2,1,0:T(8,128)(2,1)S(1)}, bf16[16,136,128]{2,1,0:T(8,128)(2,1)S(1)}, u32[]{:S(2)}, u32[]{:S(2)}) collective-permute-start(bf16[16,136,128]{2,1,0:T(8,128)(2,1)S(1)} %parts.7), channel_id=1, source_target_pairs={{0,8},{8,0},{1,9},{9,1},{2,10},{10,2},{3,11},{11,3},{4,12},{12,4},... | collective-permute-start | bytes 1671176 | tf_op jit(solution)/shard_map/ppermute | solution.py:492
  80.0 0.6 parts.6
  80.5 3.8 %collective-permute-done.1 = bf16[16,136,128]{2,1,0:T(8,128)(2,1)S(1)} collective-permute-done((bf16[16,136,128]{2,1,0:T(8,128)(2,1)S(1)}, bf16[16,136,128]{2,1,0:T(8,128)(2,1)S(1)}, u32[]{:S(2)}, u32[]{:S(2)}) %collective-permute-start.1) | collective-permute-done | bytes 557088 | tf_op jit(solution)/shard_map/ppermute | solution.py:490
  84.4 0.1 convert_add_fusion
  84.5 0.0 collective-permute-done.2
  84.5 0.1 add_convert_fusion
  84.6 30.2 %all_to_all.38.got_ref = bf16[16,136,128]{2,1,0:T(8,128)(2,1)S(1)} all-to-all(bf16[16,136,128]{2,1,0:T(8,128)(2,1)S(1)} %add_convert_fusion), channel_id=1, replica_groups=mesh['za'=2,'zb'=2,'zl'=2,'ya'=2,'yb'=2,'core'=2,'x'=4,'yl'=2] {'ya','za..., dimensions={0} | all-to-all | bytes 1114112 | tf_op jit(solution)/shard_map/all_to_all | solution.py:29
  114.8 0.1 totals.1
  114.9 26.6 %all_to_all.39.refs_0_ = bf16[16,136,128]{2,1,0:T(8,128)(2,1)S(1)} all-to-all(bf16[16,136,128]{2,1,0:T(8,128)(2,1)S(1)} %totals.1), channel_id=1, replica_groups=mesh['za'=2,'zb'=2,'zl'=2,'ya'=2,'yb'=2,'core'=2,'x'=4,'yl'=2] {'ya','za..., dimensions={0} | all-to-all | bytes 1114112 | tf_op jit(solution)/shard_map/all_to_all | solution.py:29
  141.5 2.2 %collective-permute-start.3 = (bf16[16,136,128]{2,1,0:T(8,128)(2,1)S(1)}, bf16[16,136,128]{2,1,0:T(8,128)(2,1)S(1)}, u32[]{:S(2)}, u32[]{:S(2)}) collective-permute-start(bf16[16,136,128]{2,1,0:T(8,128)(2,1)S(1)} %all_to_all.39.refs_0_), channel_id=1, source_target_pairs={{0,64},{8,456},{64,0},{72,136},{128,192},{136,72},{192,128},{200,2... | collective-permute-start | bytes 1671176 | tf_op jit(solution)/shard_map/ppermute | solution.py:498
  143.7 3.2 %collective-permute-start.5 = (bf16[16,136,128]{2,1,0:T(8,128)(2,1)S(1)}, bf16[16,136,128]{2,1,0:T(8,128)(2,1)S(1)}, u32[]{:S(2)}, u32[]{:S(2)}) collective-permute-start(bf16[16,136,128]{2,1,0:T(8,128)(2,1)S(1)} %all_to_all.39.refs_0_), channel_id=1, source_target_pairs={{0,8},{8,0},{1,9},{9,1},{2,10},{10,2},{3,11},{11,3},{4,12},{12,4},... | collective-permute-start | bytes 1671176 | tf_op jit(solution)/shard_map/ppermute | solution.py:499
  147.0 0.9 assemble.3
  147.8 5.1 %collective-permute-done.3.refs_0_ = bf16[16,136,128]{2,1,0:T(8,128)(2,1)S(1)} collective-permute-done((bf16[16,136,128]{2,1,0:T(8,128)(2,1)S(1)}, bf16[16,136,128]{2,1,0:T(8,128)(2,1)S(1)}, u32[]{:S(2)}, u32[]{:S(2)}) %collective-permute-start.3) | collective-permute-done | bytes 557088 | tf_op jit(solution)/shard_map/ppermute | solution.py:498
  153.0 3.5 %collective-permute-start.4 = (bf16[16,136,128]{2,1,0:T(8,128)(2,1)S(1)}, bf16[16,136,128]{2,1,0:T(8,128)(2,1)S(1)}, u32[]{:S(2)}, u32[]{:S(2)}) collective-permute-start(bf16[16,136,128]{2,1,0:T(8,128)(2,1)S(1)} %collective-permute-done.3.refs_0_), channel_id=1, source_target_pairs={{0,8},{8,0},{1,9},{9,1},{2,10},{10,2},{3,11},{11,3},{4,12},{12,4},... | collective-permute-start | bytes 1671176 | tf_op jit(solution)/shard_map/ppermute | solution.py:502
  156.5 1.1 assemble.4
  157.6 0.5 collective-permute-done.4.refs_0_
  158.0 0.9 assemble.5
  (7 shorter events, 0.0 us)
Async XLA Ops:
  21.3 10.5 %copy-start.2 = (s32[512]{0:T(512)S(1)}, s32[512]{0:T(512)}, u32[]{:S(2)}) copy-start(s32[512]{0:T(512)} %param.7) | copy-start | bytes 6148
  33.1 21.1 %copy-start.1 = (bf16[512,512]{1,0:T(8,128)(2,1)S(1)}, bf16[512,512]{1,0:T(8,128)(2,1)}, u32[]{:S(2)}) copy-start(bf16[512,512]{1,0:T(8,128)(2,1)} %class_ref.9) | copy-start | bytes 1572868
  43.6 10.5 %copy-start = (bf16[512,1568]{0,1:T(8,128)(2,1)S(1)}, bf16[512,1568]{0,1:T(8,128)(2,1)}, u32[]{:S(2)}) copy-start(bf16[512,1568]{0,1:T(8,128)(2,1)} %param.4) | copy-start | bytes 4816900
  54.7 11.6 %collective-permute-start = (bf16[16,136,128]{2,1,0:T(8,128)(2,1)S(1)}, bf16[16,136,128]{2,1,0:T(8,128)(2,1)S(1)}, u32[]{:S(2)}, u32[]{:S(2)}) collective-permute-start(bf16[16,136,128]{2,1,0:T(8,128)(2,1)S(1)} %parts.5), channel_id=1, source_target_pairs={{0,8},{8,0},{1,9},{9,1},{2,10},{10,2},{3,11},{11,3},{4,12},{12,4},... | collective-permute-start | bytes 1671176 | tf_op jit(solution)/shard_map/ppermute | solution.py:487
  66.4 18.0 %collective-permute-start.1 = (bf16[16,136,128]{2,1,0:T(8,128)(2,1)S(1)}, bf16[16,136,128]{2,1,0:T(8,128)(2,1)S(1)}, u32[]{:S(2)}, u32[]{:S(2)}) collective-permute-start(bf16[16,136,128]{2,1,0:T(8,128)(2,1)S(1)} %add_convert_fusion.1), channel_id=1, source_target_pairs={{0,64},{8,456},{64,0},{72,136},{128,192},{136,72},{192,128},{200,2... | collective-permute-start | bytes 1671176 | tf_op jit(solution)/shard_map/ppermute | solution.py:490
  78.0 6.4 %collective-permute-start.2 = (bf16[16,136,128]{2,1,0:T(8,128)(2,1)S(1)}, bf16[16,136,128]{2,1,0:T(8,128)(2,1)S(1)}, u32[]{:S(2)}, u32[]{:S(2)}) collective-permute-start(bf16[16,136,128]{2,1,0:T(8,128)(2,1)S(1)} %parts.7), channel_id=1, source_target_pairs={{0,8},{8,0},{1,9},{9,1},{2,10},{10,2},{3,11},{11,3},{4,12},{12,4},... | collective-permute-start | bytes 1671176 | tf_op jit(solution)/shard_map/ppermute | solution.py:492
  141.5 11.5 %collective-permute-start.3 = (bf16[16,136,128]{2,1,0:T(8,128)(2,1)S(1)}, bf16[16,136,128]{2,1,0:T(8,128)(2,1)S(1)}, u32[]{:S(2)}, u32[]{:S(2)}) collective-permute-start(bf16[16,136,128]{2,1,0:T(8,128)(2,1)S(1)} %all_to_all.39.refs_0_), channel_id=1, source_target_pairs={{0,64},{8,456},{64,0},{72,136},{128,192},{136,72},{192,128},{200,2... | collective-permute-start | bytes 1671176 | tf_op jit(solution)/shard_map/ppermute | solution.py:498
  143.7 12.7 %collective-permute-start.5 = (bf16[16,136,128]{2,1,0:T(8,128)(2,1)S(1)}, bf16[16,136,128]{2,1,0:T(8,128)(2,1)S(1)}, u32[]{:S(2)}, u32[]{:S(2)}) collective-permute-start(bf16[16,136,128]{2,1,0:T(8,128)(2,1)S(1)} %all_to_all.39.refs_0_), channel_id=1, source_target_pairs={{0,8},{8,0},{1,9},{9,1},{2,10},{10,2},{3,11},{11,3},{4,12},{12,4},... | collective-permute-start | bytes 1671176 | tf_op jit(solution)/shard_map/ppermute | solution.py:499
  153.0 5.0 %collective-permute-start.4 = (bf16[16,136,128]{2,1,0:T(8,128)(2,1)S(1)}, bf16[16,136,128]{2,1,0:T(8,128)(2,1)S(1)}, u32[]{:S(2)}, u32[]{:S(2)}) collective-permute-start(bf16[16,136,128]{2,1,0:T(8,128)(2,1)S(1)} %collective-permute-done.3.refs_0_), channel_id=1, source_target_pairs={{0,8},{8,0},{1,9},{9,1},{2,10},{10,2},{3,11},{11,3},{4,12},{12,4},... | collective-permute-start | bytes 1671176 | tf_op jit(solution)/shard_map/ppermute | solution.py:502

commit v13 on v10

--- a/solution.py
+++ b/solution.py
@@ -315,10 +315,14 @@
     quarter = 2 * half + parity
     grads = grads_ref[...]
 
+    each = (inputs - main) // 2
     first = pl.multiple_of(quarter * (some * rows), LANES)
-    part = jnp.dot(
-        features_ref[pl.ds(first, some * rows), :], grads, preferred_element_type=jnp.float32
-    )
+    left = pl.multiple_of(main + half * each, each)
+    faces = [features_ref[pl.ds(first, some * rows), :], features_ref[pl.ds(left, each), :]]
+    both = jnp.dot(
+        jnp.concatenate(faces, axis=0), grads, preferred_element_type=jnp.float32
+    )
+    part, over = both[: some * rows], both[some * rows :].astype(out_ref.dtype)
     part = part.astype(out_ref.dtype).reshape(some, rows, width)
     for group in range(groups):
         out_ref[:, group * rows : (group + 1) * rows, :] = part[
@@ -341,12 +345,6 @@
             :, :, group * LANES : (group + 1) * LANES
         ]
 
-    each = (inputs - main) // 2
-    over = jnp.dot(
-        features_ref[pl.ds(pl.multiple_of(main + half * each, each), each), :],
-        grads,
-        preferred_element_type=jnp.float32,
-    ).astype(out_ref.dtype)
     strip = jnp.where(parity == 0, over[:8], over[8:])
     for group in range(groups):
         out_ref[group, base + groups * 8 :, :] = strip[:, group * LANES : (group + 1) * LANES]

time: 158 us -> 158 us (level)
  no operation moved by 1% of the time
where the time goes in v13:
time: 158 us
  blocking collectives  104 us (66%)
  starting transfers between devices  32.7 us (21%)
  Pallas kernels  10.1 us (6%)
  waiting for transfers between devices  9.54 us (6%)
    all_to_all x6, blocking collectives, exchange(): return lax.all_to_all(blocks, axes, 0, 0, tiled=True)  104 us
    ppermute x2, starting transfers between devices, shards(): theirs = lax.ppermute(theirs, 'core', swap)  11.9 us
    ppermute x1, starting transfers between devices, shards(): got = lax.ppermute(sent, neighbour, pairs)  11.1 us
    pallas_call x8, Pallas kernels, call(): pl.pallas_call(kernel, in_specs=specs, out_specs=[VMEM] * len(results), o...  4.39 us
    ppermute x1, waiting for transfers between devices, shards(): next_mine = lax.ppermute(mine, neighbour, pairs)  4.22 us
    ppermute x1, waiting for transfers between devices, shards(): got = lax.ppermute(sent, neighbour, pairs)  3.86 us
    ppermute x1, starting transfers between devices, shards(): next_mine = lax.ppermute(mine, neighbour, pairs)  3.53 us
    ppermute x1, starting transfers between devices, shards(): across_next = lax.ppermute(next_mine, 'core', swap)  3.36 us
  transfers between devices with their start and end apart: 6, of which 4 were waited for; matrix products, arithmetic and copies ran while one was open for 0% of the time, Pallas kernels for 2%

profile of v13, /device:TPU:1, one launch (start us, length us, event | category | flops | bytes accessed | tf_op | source)
XLA Modules:
  0.0 157.7 jit_solution(10724952741266006139)
XLA Ops:
  0.6 2.9 %embed.1 = (bf16[512,1024]{1,0:T(8,128)(2,1)S(1)}, bf16[512,512]{1,0:T(8,128)(2,1)S(1)}) custom-call(s32[1]{0:T(128)} %bitcast.place_ref, bf16[1568,512]{1,0:T(8,128)(2,1)} %bitcast.6, bf16[1568,512]{1,0:T(8,128)(2,1)} %fc_ref.1, bf16[512,512]{1,0:T(8,128)(2,1)} %class_ref.9, s32[1,512]{1,0:T(1,128)} %bitcast.21), custom_call_target="tpu_custom_call" | custom-call | tf_op jit(solution)/shard_map/embed/pallas_call | solution.py:155
  3.6 17.7 %all_to_all.34.got_ref = bf16[8,64,1024]{2,1,0:T(8,128)(2,1)S(1)} all-to-all(bf16[8,64,1024]{2,1,0:T(8,128)(2,1)S(1)} %bitcast.20), channel_id=1, replica_groups=mesh['zh'=4,'zl'=2,'yh'=4,'core'=2,'x'=4,'yl'=2] {'x','yl'}, dimensions={0} | all-to-all | bytes 2097152 | tf_op jit(solution)/shard_map/all_to_all | solution.py:29
  21.3 0.2 units.1
  21.5 10.3 %all_to_all.35 = bf16[8,64,512]{2,1,0:T(8,128)(2,1)S(1)} all-to-all(bf16[8,64,512]{2,1,0:T(8,128)(2,1)S(1)} %get-tuple-element.21), channel_id=1, replica_groups=mesh['zh'=4,'zl'=2,'yh'=4,'core'=2,'x'=4,'yl'=2] {'x','yl'}, dimensions={0} | all-to-all | bytes 1048576 | tf_op jit(solution)/shard_map/all_to_all | solution.py:29
  31.8 1.3 cosines.1
  33.1 10.5 %all_to_all.36.pulls_ref = bf16[8,72,512]{2,1,0:T(8,128)(2,1)S(1)} all-to-all(bf16[8,72,512]{2,1,0:T(8,128)(2,1)S(1)} %get-tuple-element.23), channel_id=1, replica_groups=mesh['zh'=4,'zl'=2,'yh'=4,'core'=2,'x'=4,'yl'=2] {'x','yl'}, dimensions={0} | all-to-all | bytes 1179648 | tf_op jit(solution)/shard_map/all_to_all | solution.py:29
  43.6 0.6 raw_grads.1
  44.2 10.0 %all_to_all.37 = bf16[8,64,512]{2,1,0:T(8,128)(2,1)S(1)} all-to-all(bf16[8,64,512]{2,1,0:T(8,128)(2,1)S(1)} %get-tuple-element.26), channel_id=1, replica_groups=mesh['zh'=4,'zl'=2,'yh'=4,'core'=2,'x'=4,'yl'=2] {'x','yl'}, dimensions={0} | all-to-all | bytes 1048576 | tf_op jit(solution)/shard_map/all_to_all | solution.py:29
  54.1 0.6 parts.5
  54.7 10.0 %collective-permute-start = (bf16[16,136,128]{2,1,0:T(8,128)(2,1)S(1)}, bf16[16,136,128]{2,1,0:T(8,128)(2,1)S(1)}, u32[]{:S(2)}, u32[]{:S(2)}) collective-permute-start(bf16[16,136,128]{2,1,0:T(8,128)(2,1)S(1)} %parts.5), channel_id=1, source_target_pairs={{0,8},{8,0},{1,9},{9,1},{2,10},{10,2},{3,11},{11,3},{4,12},{12,4},... | collective-permute-start | bytes 1671176 | tf_op jit(solution)/shard_map/ppermute | solution.py:485
  64.7 0.6 parts.4
  65.3 1.0 collective-permute-done
  66.3 0.1 add_convert_fusion.1
  66.4 11.1 %collective-permute-start.1 = (bf16[16,136,128]{2,1,0:T(8,128)(2,1)S(1)}, bf16[16,136,128]{2,1,0:T(8,128)(2,1)S(1)}, u32[]{:S(2)}, u32[]{:S(2)}) collective-permute-start(bf16[16,136,128]{2,1,0:T(8,128)(2,1)S(1)} %add_convert_fusion.1), channel_id=1, source_target_pairs={{0,64},{8,456},{64,0},{72,136},{128,192},{136,72},{192,128},{200,2... | collective-permute-start | bytes 1671176 | tf_op jit(solution)/shard_map/ppermute | solution.py:488
  77.5 0.6 parts.7
  78.0 1.9 %collective-permute-start.2 = (bf16[16,136,128]{2,1,0:T(8,128)(2,1)S(1)}, bf16[16,136,128]{2,1,0:T(8,128)(2,1)S(1)}, u32[]{:S(2)}, u32[]{:S(2)}) collective-permute-start(bf16[16,136,128]{2,1,0:T(8,128)(2,1)S(1)} %parts.7), channel_id=1, source_target_pairs={{0,8},{8,0},{1,9},{9,1},{2,10},{10,2},{3,11},{11,3},{4,12},{12,4},... | collective-permute-start | bytes 1671176 | tf_op jit(solution)/shard_map/ppermute | solution.py:490
  80.0 0.6 parts.6
  80.5 3.9 %collective-permute-done.1 = bf16[16,136,128]{2,1,0:T(8,128)(2,1)S(1)} collective-permute-done((bf16[16,136,128]{2,1,0:T(8,128)(2,1)S(1)}, bf16[16,136,128]{2,1,0:T(8,128)(2,1)S(1)}, u32[]{:S(2)}, u32[]{:S(2)}) %collective-permute-start.1) | collective-permute-done | bytes 557088 | tf_op jit(solution)/shard_map/ppermute | solution.py:488
  84.4 0.1 convert_add_fusion
  84.5 0.0 collective-permute-done.2
  84.5 0.1 add_convert_fusion
  84.6 28.8 %all_to_all.38.got_ref = bf16[16,136,128]{2,1,0:T(8,128)(2,1)S(1)} all-to-all(bf16[16,136,128]{2,1,0:T(8,128)(2,1)S(1)} %add_convert_fusion), channel_id=1, replica_groups=mesh['zh'=4,'zl'=2,'yh'=4,'core'=2,'x'=4,'yl'=2] {'zh','yh'}, dimensions={0} | all-to-all | bytes 1114112 | tf_op jit(solution)/shard_map/all_to_all | solution.py:29
  113.4 0.1 totals.1
  113.5 27.0 %all_to_all.39.refs_0_ = bf16[16,136,128]{2,1,0:T(8,128)(2,1)S(1)} all-to-all(bf16[16,136,128]{2,1,0:T(8,128)(2,1)S(1)} %totals.1), channel_id=1, replica_groups=mesh['zh'=4,'zl'=2,'yh'=4,'core'=2,'x'=4,'yl'=2] {'zh','yh'}, dimensions={0} | all-to-all | bytes 1114112 | tf_op jit(solution)/shard_map/all_to_all | solution.py:29
  140.5 3.5 %collective-permute-start.3 = (bf16[16,136,128]{2,1,0:T(8,128)(2,1)S(1)}, bf16[16,136,128]{2,1,0:T(8,128)(2,1)S(1)}, u32[]{:S(2)}, u32[]{:S(2)}) collective-permute-start(bf16[16,136,128]{2,1,0:T(8,128)(2,1)S(1)} %all_to_all.39.refs_0_), channel_id=1, source_target_pairs={{0,64},{8,456},{64,0},{72,136},{128,192},{136,72},{192,128},{200,2... | collective-permute-start | bytes 1671176 | tf_op jit(solution)/shard_map/ppermute | solution.py:496
  144.0 2.8 %collective-permute-start.5 = (bf16[16,136,128]{2,1,0:T(8,128)(2,1)S(1)}, bf16[16,136,128]{2,1,0:T(8,128)(2,1)S(1)}, u32[]{:S(2)}, u32[]{:S(2)}) collective-permute-start(bf16[16,136,128]{2,1,0:T(8,128)(2,1)S(1)} %all_to_all.39.refs_0_), channel_id=1, source_target_pairs={{0,8},{8,0},{1,9},{9,1},{2,10},{10,2},{3,11},{11,3},{4,12},{12,4},... | collective-permute-start | bytes 1671176 | tf_op jit(solution)/shard_map/ppermute | solution.py:497
  146.8 0.9 assemble.3
  147.7 4.2 %collective-permute-done.3.refs_0_ = bf16[16,136,128]{2,1,0:T(8,128)(2,1)S(1)} collective-permute-done((bf16[16,136,128]{2,1,0:T(8,128)(2,1)S(1)}, bf16[16,136,128]{2,1,0:T(8,128)(2,1)S(1)}, u32[]{:S(2)}, u32[]{:S(2)}) %collective-permute-start.3) | collective-permute-done | bytes 557088 | tf_op jit(solution)/shard_map/ppermute | solution.py:496
  151.9 3.4 %collective-permute-start.4 = (bf16[16,136,128]{2,1,0:T(8,128)(2,1)S(1)}, bf16[16,136,128]{2,1,0:T(8,128)(2,1)S(1)}, u32[]{:S(2)}, u32[]{:S(2)}) collective-permute-start(bf16[16,136,128]{2,1,0:T(8,128)(2,1)S(1)} %collective-permute-done.3.refs_0_), channel_id=1, source_target_pairs={{0,8},{8,0},{1,9},{9,1},{2,10},{10,2},{3,11},{11,3},{4,12},{12,4},... | collective-permute-start | bytes 1671176 | tf_op jit(solution)/shard_map/ppermute | solution.py:500
  155.3 1.1 assemble.4
  156.4 0.5 collective-permute-done.4.refs_0_
  156.9 0.9 assemble.5
  (7 shorter events, 0.0 us)
Async XLA Ops:
  21.3 10.5 %copy-start.2 = (s32[512]{0:T(512)S(1)}, s32[512]{0:T(512)}, u32[]{:S(2)}) copy-start(s32[512]{0:T(512)} %param.7) | copy-start | bytes 6148
  33.1 21.1 %copy-start.1 = (bf16[512,512]{1,0:T(8,128)(2,1)S(1)}, bf16[512,512]{1,0:T(8,128)(2,1)}, u32[]{:S(2)}) copy-start(bf16[512,512]{1,0:T(8,128)(2,1)} %class_ref.9) | copy-start | bytes 1572868
  43.6 10.5 %copy-start = (bf16[512,1568]{0,1:T(8,128)(2,1)S(1)}, bf16[512,1568]{0,1:T(8,128)(2,1)}, u32[]{:S(2)}) copy-start(bf16[512,1568]{0,1:T(8,128)(2,1)} %param.4) | copy-start | bytes 4816900
  54.7 11.6 %collective-permute-start = (bf16[16,136,128]{2,1,0:T(8,128)(2,1)S(1)}, bf16[16,136,128]{2,1,0:T(8,128)(2,1)S(1)}, u32[]{:S(2)}, u32[]{:S(2)}) collective-permute-start(bf16[16,136,128]{2,1,0:T(8,128)(2,1)S(1)} %parts.5), channel_id=1, source_target_pairs={{0,8},{8,0},{1,9},{9,1},{2,10},{10,2},{3,11},{11,3},{4,12},{12,4},... | collective-permute-start | bytes 1671176 | tf_op jit(solution)/shard_map/ppermute | solution.py:485
  66.4 18.0 %collective-permute-start.1 = (bf16[16,136,128]{2,1,0:T(8,128)(2,1)S(1)}, bf16[16,136,128]{2,1,0:T(8,128)(2,1)S(1)}, u32[]{:S(2)}, u32[]{:S(2)}) collective-permute-start(bf16[16,136,128]{2,1,0:T(8,128)(2,1)S(1)} %add_convert_fusion.1), channel_id=1, source_target_pairs={{0,64},{8,456},{64,0},{72,136},{128,192},{136,72},{192,128},{200,2... | collective-permute-start | bytes 1671176 | tf_op jit(solution)/shard_map/ppermute | solution.py:488
  78.0 6.4 %collective-permute-start.2 = (bf16[16,136,128]{2,1,0:T(8,128)(2,1)S(1)}, bf16[16,136,128]{2,1,0:T(8,128)(2,1)S(1)}, u32[]{:S(2)}, u32[]{:S(2)}) collective-permute-start(bf16[16,136,128]{2,1,0:T(8,128)(2,1)S(1)} %parts.7), channel_id=1, source_target_pairs={{0,8},{8,0},{1,9},{9,1},{2,10},{10,2},{3,11},{11,3},{4,12},{12,4},... | collective-permute-start | bytes 1671176 | tf_op jit(solution)/shard_map/ppermute | solution.py:490
  140.5 11.5 %collective-permute-start.3 = (bf16[16,136,128]{2,1,0:T(8,128)(2,1)S(1)}, bf16[16,136,128]{2,1,0:T(8,128)(2,1)S(1)}, u32[]{:S(2)}, u32[]{:S(2)}) collective-permute-start(bf16[16,136,128]{2,1,0:T(8,128)(2,1)S(1)} %all_to_all.39.refs_0_), channel_id=1, source_target_pairs={{0,64},{8,456},{64,0},{72,136},{128,192},{136,72},{192,128},{200,2... | collective-permute-start | bytes 1671176 | tf_op jit(solution)/shard_map/ppermute | solution.py:496
  144.0 11.3 %collective-permute-start.5 = (bf16[16,136,128]{2,1,0:T(8,128)(2,1)S(1)}, bf16[16,136,128]{2,1,0:T(8,128)(2,1)S(1)}, u32[]{:S(2)}, u32[]{:S(2)}) collective-permute-start(bf16[16,136,128]{2,1,0:T(8,128)(2,1)S(1)} %all_to_all.39.refs_0_), channel_id=1, source_target_pairs={{0,8},{8,0},{1,9},{9,1},{2,10},{10,2},{3,11},{11,3},{4,12},{12,4},... | collective-permute-start | bytes 1671176 | tf_op jit(solution)/shard_map/ppermute | solution.py:497
  151.9 4.9 %collective-permute-start.4 = (bf16[16,136,128]{2,1,0:T(8,128)(2,1)S(1)}, bf16[16,136,128]{2,1,0:T(8,128)(2,1)S(1)}, u32[]{:S(2)}, u32[]{:S(2)}) collective-permute-start(bf16[16,136,128]{2,1,0:T(8,128)(2,1)S(1)} %collective-permute-done.3.refs_0_), channel_id=1, source_target_pairs={{0,8},{8,0},{1,9},{9,1},{2,10},{10,2},{3,11},{11,3},{4,12},{12,4},... | collective-permute-start | bytes 1671176 | tf_op jit(solution)/shard_map/ppermute | solution.py:500
